TPU v7x, 768 devices: a whole 4x8x12 slice. The times are simulated.
768 devices in a mesh: chan: 48 (over y_lo, z), space: 16 (over x, y_hi, core).
Axes of the slice: x: 4, y: 8 (y_hi: 2, y_lo: 4; y = y_hi * 4 + y_lo), z: 12, core: 2. Of those that a mesh axis runs over, the one named last changes fastest.
Arguments:
- floor_tokens: int32 [128, 128], P('space'), may hold values from 0 to 255
- token_table: bfloat16 [256, 1536], P(None, 'chan'), may hold values from -6 to 6
- depth_kernel: bfloat16 [7, 7, 1536], P(None, None, 'chan'), may hold values from -2 to 2
- norm_gain: float32 [1536], replicated, may hold values from 0.5 to 1.5
- layer_scale: float32 [1536], replicated, may hold values from 0.5 to 2
- w_in: bfloat16 [1536, 6144], P(None, 'chan'), may hold values from -0.375 to 0.375
- w_out: bfloat16 [6144, 1536], P('chan'), may hold values from -0.1875 to 0.1875
- grad_out: bfloat16 [128, 128, 1536], P('space', None, 'chan'), may hold values from -6 to 6
Outputs:
- block_out: bfloat16 [128, 128, 1536], P('space', None, 'chan')
- grad_embedded: bfloat16 [128, 128, 1536], P('space', None, 'chan')
Inputs may be any that keep to these rules, and one draw needn't show every extreme that they name: `floor_tokens`: token ids of the floor cells.
All inputs are finite; a program needn't handle non-finite values.
Results may differ from a plain program's by a relative error of at most 0.0067.
Values may be sent and summed in bfloat16 or wider, within the bound.
No kernel may reach another device: no remote copies, remote signals or barrier semaphores. Data moves between devices by JAX's collectives and lax.ppermute only.
A program may use at most 128 MiB of HBM per device.

v0:
```python
import jax
import jax.numpy as jnp
from jax import lax
from jax.sharding import PartitionSpec as P


def padded_2(block, sides, width):
    for axis, dim in sides:
        count = lax.axis_size(axis)
        forward = [(i, i + 1) for i in range(count - 1)]
        backward = [(target, source) for source, target in forward]
        low = lax.ppermute(
            lax.slice_in_dim(block, block.shape[dim] - width, None, axis=dim), axis, forward
        )
        high = lax.ppermute(lax.slice_in_dim(block, 0, width, axis=dim), axis, backward)
        block = jnp.concatenate([low, block, high], axis=dim)
    return block


def forward_conv(padded, depth_kernel, rows, cols):
    total = jnp.zeros((rows, cols, padded.shape[2]), jnp.float32)
    for row_off in range(7):
        for col_off in range(7):
            window = padded[row_off : row_off + rows, col_off : col_off + cols].astype(jnp.float32)
            total = total + window * depth_kernel[row_off, col_off].astype(jnp.float32)
    return total


def backward_conv(padded, depth_kernel, rows, cols):
    total = jnp.zeros((rows, cols, padded.shape[2]), jnp.float32)
    for row_off in range(7):
        for col_off in range(7):
            start_row = 6 - row_off
            start_col = 6 - col_off
            window = padded[start_row : start_row + rows, start_col : start_col + cols].astype(
                jnp.float32
            )
            total = total + window * depth_kernel[row_off, col_off].astype(jnp.float32)
    return total


def gelu_tanh(value):
    return jax.nn.gelu(value, approximate=True)


def pad_columns(field):
    return jnp.pad(field, ((0, 0), (3, 3), (0, 0)))


def on_device(
    floor_tokens, token_table, depth_kernel, norm_gain, layer_scale, w_in, w_out, grad_out
):
    rows, cols = floor_tokens.shape
    local_chan = depth_kernel.shape[2]
    width = norm_gain.shape[0]
    offset = lax.axis_index("chan") * local_chan
    x_local = jnp.take(token_table, floor_tokens, axis=0)
    framed = padded_2(x_local, (("space", 0),), 3)
    conv_local = forward_conv(pad_columns(framed), depth_kernel, rows, cols).astype(jnp.bfloat16)
    conv_full, grad_full = (
        lax.all_gather(conv_local, "chan", axis=2, tiled=True),
        lax.all_gather(grad_out, "chan", axis=2, tiled=True),
    )
    flat = conv_full.reshape(rows * cols, width).astype(jnp.float32)
    row_mean = jnp.mean(flat, axis=-1, keepdims=True)
    centered = flat - row_mean
    inv_std = lax.rsqrt(jnp.mean(centered * centered, axis=-1, keepdims=True) + 1e-06)
    normed = centered * inv_std
    scaled = (normed * norm_gain).astype(jnp.bfloat16)
    pre = jnp.dot(scaled, w_in, preferred_element_type=jnp.float32)
    act = gelu_tanh(pre).astype(jnp.bfloat16)
    grad_flat = grad_full.reshape(rows * cols, width)
    grad_mix = (layer_scale * grad_flat.astype(jnp.float32)).astype(jnp.bfloat16)
    grad_act = jnp.dot(grad_mix, w_out.T, preferred_element_type=jnp.float32)
    grad_pre = jax.vjp(gelu_tanh, pre)[1](grad_act)[0].astype(jnp.bfloat16)
    grad_norm = jnp.dot(grad_pre, w_in.T, preferred_element_type=jnp.float32)
    scaled_grad = grad_norm * norm_gain
    conv_part = inv_std * (
        scaled_grad
        - jnp.mean(scaled_grad, axis=-1, keepdims=True)
        - normed * jnp.mean(scaled_grad * normed, axis=-1, keepdims=True)
    )
    mix_part = jnp.dot(act, w_out, preferred_element_type=jnp.float32)
    mix_share, conv_share = (
        lax.psum_scatter(mix_part, "chan", scatter_dimension=1, tiled=True),
        lax.psum_scatter(conv_part, "chan", scatter_dimension=1, tiled=True),
    )
    scale_local = lax.dynamic_slice_in_dim(layer_scale, offset, local_chan, 0)
    base = x_local.reshape(rows * cols, local_chan).astype(jnp.float32)
    block_out = (
        (base + scale_local * mix_share).astype(jnp.bfloat16).reshape(rows, cols, local_chan)
    )
    grad_conv = conv_share.astype(jnp.bfloat16).reshape(rows, cols, local_chan)
    grad_framed = padded_2(grad_conv, (("space", 0),), 3)
    through = backward_conv(pad_columns(grad_framed), depth_kernel, rows, cols)
    grad_embedded = (grad_out.astype(jnp.float32) + through).astype(jnp.bfloat16)
    return (block_out, grad_embedded)


def solution(mesh):
    placed = (
        P("space", None),
        P(None, "chan"),
        P(None, None, "chan"),
        P(),
        P(),
        P(None, "chan"),
        P("chan", None),
        P("space", None, "chan"),
    )
    return jax.shard_map(
        on_device,
        mesh=mesh,
        in_specs=placed,
        out_specs=(P("space", None, "chan"), P("space", None, "chan")),
        check_vma=False,
    )
```

profile of v0, /device:TPU:6, one launch (start us, length us, event | category | flops | bytes accessed | tf_op | source)
XLA Modules:
  0.0 1010.5 jit_solution(359807614613027143)
XLA Ops:
  7.2 0.0 copy-start
  7.2 0.0 all-gather.5.cloned.1.call-start
  7.2 1.5 copy.37
  8.8 0.0 all-gather.5.cloned.1.call-update
  8.8 0.0 all-gather.3.cloned.1.call-start
  8.8 0.8 copy.33
  9.7 0.7 bitcast_clamp_fusion
  10.4 3.2 gather_fusion
  13.6 0.1 copy.35
  13.7 0.7 compare_and_fusion
  14.4 7.4 collective-permute-start.1
  21.9 1.9 collective-permute-start
  23.8 1.0 bitcast_convert_fusion.48
  24.8 1.0 bitcast_convert_fusion.47
  25.8 0.9 bitcast_convert_fusion.46
  26.7 0.0 collective-permute-done.1
  26.7 5.1 collective-permute-done
  31.8 0.1 select_maximum_fusion.2
  32.0 1.8 add_convert_fusion.2
  33.8 0.0 all-gather.3.cloned.1.call-update
  33.8 0.0 reduce-scatter.7.cloned.1.call-start
  33.9 214.1 %all-gather.5.cloned.1.call-done = bf16[8,128,1536]{1,0,2:T(8,128)(2,1)} async-done(((bf16[8,128,32]{1,0,2:T(8,128)(2,1)}), bf16[8,128,1536]{1,0,2:T(8,128)(2,1)}) %all-gather.5.cloned.1.call-update) | async-done | bytes 3145744 | tf_op jit(solution)/shard_map/all_gather | solution.py:62
  248.0 5.0 copy.38
  253.0 220.6 %all-gather.3.cloned.1.call-done = bf16[8,128,1536]{1,2,0:T(8,128)(2,1)} async-done(((bf16[8,128,32]{1,2,0:T(8,128)(2,1)}), bf16[8,128,1536]{1,2,0:T(8,128)(2,1)}) %all-gather.3.cloned.1.call-update) | async-done | bytes 3145744 | tf_op jit(solution)/shard_map/all_gather | solution.py:61
  473.6 2.3 convert_reduce_fusion
  475.9 0.0 copy-start.3
  476.0 2.7 multiply_reduce_fusion.1
  478.7 5.4 copy.36
  484.1 0.0 copy-start.1
  484.1 0.0 copy-done.3
  484.1 0.0 copy-start.5
  484.1 3.7 multiply_convert_fusion
  487.8 0.0 copy-done.1
  487.8 1.0 fusion.57
  488.8 0.0 copy-done
  488.8 0.0 copy-done.5
  488.8 9.8 multiply_reduce_fusion.2
  498.6 7.2 subtract_multiply_fusion
  505.8 6.6 copy.46
  512.4 0.0 reduce-scatter.7.cloned.1.call-update
  512.4 0.0 copy-start.4
  512.4 0.0 reduce-scatter.5.cloned.1.call-start
  512.5 3.7 fusion.21
  516.2 0.0 copy-start.2
  516.2 0.0 reduce-scatter.5.cloned.1.call-update
  516.2 0.1 copy.34
  516.3 0.1 dynamic_slice.3
  516.4 0.0 copy-done.4
  516.4 239.3 %reduce-scatter.7.cloned.1.call-done = f32[32,1024]{1,0:T(8,128)} async-done(((f32[1536,1024]{1,0:T(8,128)}), f32[32,1024]{1,0:T(8,128)}) %reduce-scatter.7.cloned.1.call-update) | async-done | bytes 131088
  755.7 1.1 copy.47
  756.8 0.1 copy.39
  756.9 1.9 collective-permute-start.2
  758.8 0.1 copy.40
  758.9 8.4 collective-permute-start.3
  767.4 232.8 %reduce-scatter.5.cloned.1.call-done = f32[1024,32]{0,1:T(8,128)} async-done(((f32[1024,1536]{0,1:T(8,128)}), f32[1024,32]{0,1:T(8,128)}) %reduce-scatter.5.cloned.1.call-update) | async-done | bytes 131088 | tf_op jit(solution)/shard_map/reduce_scatter | solution.py:85
  1000.2 1.6 copy_bitcast_fusion
  1001.8 0.1 copy.41
  1001.9 0.0 collective-permute-done.2
  1002.0 0.0 collective-permute-done.3
  1002.0 0.1 select_maximum_fusion
  1002.1 0.0 copy-done.2
  1002.1 1.9 add_convert_fusion
  (7 shorter events, 0.1 us)
Async XLA Ops:
  7.2 481.6 %copy-start = (bf16[128,1536]{1,0:T(8,128)(2,1)S(1)}, bf16[128,1536]{1,0:T(8,128)(2,1)}, u32[]{:S(2)}) copy-start(bf16[128,1536]{1,0:T(8,128)(2,1)} %param.14) | copy-start | bytes 1179652
  7.2 240.8 %all-gather.5.cloned.1.call-start = ((), (), s32[]{:S(2)}) async-start(), calls=%async_computation.4 | async-start | bytes 3211264 | tf_op jit(solution)/shard_map/all_gather | solution.py:62
  8.8 464.8 %all-gather.3.cloned.1.call-start = ((), (), s32[]{:S(2)}) async-start(), calls=%async_computation.2 | async-start | bytes 3211264 | tf_op jit(solution)/shard_map/all_gather | solution.py:61
  14.4 12.3 %collective-permute-start.1 = (bf16[3,128,32]{1,2,0:T(8,128)(2,1)S(1)}, bf16[3,128,32]{1,2,0:T(8,128)(2,1)S(1)}, u32[]{:S(2)}, u32[]{:S(2)}) collective-permute-start(bf16[3,128,32]{1,2,0:T(8,128)(2,1)S(1)} %get-tuple-element.13), channel_id=1, source_target_pairs={{1,0},{2,1},{3,2},{4,3},{5,4},{6,5},{7,6},{8,7},{9,8},{10,9},{11,1... | collective-permute-start | bytes 73736 | tf_op jit(solution)/shard_map/ppermute | solution.py:15
  21.9 10.0 collective-permute-start
  33.8 721.9 %reduce-scatter.7.cloned.1.call-start = ((), (), s32[]{:S(2)}) async-start(), calls=%async_computation.5 | async-start | bytes 6422528
  475.9 8.1 copy-start.3
  484.1 3.7 copy-start.1
  484.1 4.7 copy-start.5
  512.4 4.0 copy-start.4
  512.4 487.8 %reduce-scatter.5.cloned.1.call-start = ((), (), s32[]{:S(2)}) async-start(), calls=%async_computation.3 | async-start | bytes 6422528 | tf_op jit(solution)/shard_map/reduce_scatter | solution.py:85
  516.2 486.0 %copy-start.2 = (bf16[8,128,32]{1,2,0:T(8,128)(2,1)S(1)}, bf16[8,128,32]{1,2,0:T(8,128)(2,1)}, u32[]{:S(2)}) copy-start(bf16[8,128,32]{1,2,0:T(8,128)(2,1)} %param.15) | copy-start | bytes 196612
  756.9 245.1 %collective-permute-start.2 = (bf16[3,128,32]{1,2,0:T(8,128)(2,1)S(1)}, bf16[3,128,32]{1,2,0:T(8,128)(2,1)S(1)}, u32[]{:S(2)}, u32[]{:S(2)}) collective-permute-start(bf16[3,128,32]{1,2,0:T(8,128)(2,1)S(1)} %copy.39), channel_id=1, source_target_pairs={{0,1},{1,2},{2,3},{3,4},{4,5},{5,6},{6,7},{7,8},{8,9},{9,10},{10,1... | collective-permute-start | bytes 73736 | tf_op jit(solution)/shard_map/ppermute | solution.py:12
  758.9 243.1 %collective-permute-start.3 = (bf16[3,128,32]{1,2,0:T(8,128)(2,1)S(1)}, bf16[3,128,32]{1,2,0:T(8,128)(2,1)S(1)}, u32[]{:S(2)}, u32[]{:S(2)}) collective-permute-start(bf16[3,128,32]{1,2,0:T(8,128)(2,1)S(1)} %copy.40), channel_id=1, source_target_pairs={{1,0},{2,1},{3,2},{4,3},{5,4},{6,5},{7,6},{8,7},{9,8},{10,9},{11,1... | collective-permute-start | bytes 73736 | tf_op jit(solution)/shard_map/ppermute | solution.py:15
Sparse Core Ops, SparseCore 0:
  11.0 236.9 all-gather.4
  251.0 222.6 all-gather.2
  512.5 243.1 reduce-scatter.6
  758.7 241.4 reduce-scatter.4
where the time goes:
time: 1010 us
  waiting for transfers between devices  912 us (90%)
  other arithmetic  25.8 us (3%)
  local copies, waits for them, and re-layouts  24.3 us (2%)
  starting transfers between devices  19.9 us (2%)
  matrix products  14.5 us (1%)
  between operations  14 us (1%)
    unnamed x5, waiting for transfers between devices  239 us
    reduce_scatter x1, waiting for transfers between devices, on_device(): lax.psum_scatter(mix_part, 'chan', scatter_dimension=1, tiled=True)  233 us
    all_gather x1, waiting for transfers between devices, on_device(): lax.all_gather(conv_local, 'chan', axis=2, tiled=True)  221 us
    all_gather x1, waiting for transfers between devices, on_device(): lax.all_gather(grad_out, 'chan', axis=2, tiled=True)  214 us
  transfers between devices with their start and end apart: 8, of which 5 were waited for; matrix products, arithmetic and copies ran while one was open for 2% of the time, Pallas kernels for 0%

commit v1 on v0

v1 whole, which is shorter than its diff:
```python
import jax
import jax.numpy as jnp
from jax import lax
from jax.sharding import Mesh, PartitionSpec as P

AXES = ("y", "z", "x", "h", "c")
CHAN = ("y", "z")
SPACE = ("x", "h", "c")


def halo(block, width):
    count = lax.axis_size(SPACE)
    forward = [(i, i + 1) for i in range(count - 1)]
    backward = [(j, i) for i, j in forward]
    low = lax.ppermute(block[block.shape[0] - width :], SPACE, forward)
    high = lax.ppermute(block[:width], SPACE, backward)
    return jnp.concatenate([low, block, high], axis=0)


def conv49(framed, kernel, rows, flip):
    cols = framed.shape[2]
    padded = jnp.pad(framed, ((0, 0), (0, 0), (3, 3)))
    total = jnp.zeros((rows, framed.shape[1], cols), jnp.float32)
    for a in range(7):
        for b in range(7):
            i, j = (6 - a, 6 - b) if flip else (a, b)
            window = padded[i : i + rows, :, j : j + cols].astype(jnp.float32)
            total = total + window * kernel[a, b].astype(jnp.float32)[None, :, None]
    return total


def gelu_tanh(value):
    return jax.nn.gelu(value, approximate=True)


def spread(strip):
    ny, nz = lax.axis_size("y"), lax.axis_size("z")
    rows, chans, cols = strip.shape
    part = rows // ny
    blocks = strip.reshape(ny, 1, part, chans, cols)
    blocks = jnp.broadcast_to(blocks, (ny, nz, part, chans, cols)).reshape(ny * nz, part, chans, cols)
    got = lax.all_to_all(blocks, CHAN, 0, 0, tiled=True)
    return got.transpose(0, 2, 1, 3).reshape(ny * nz * chans, part * cols)


def collect(total, part):
    ny, nz = lax.axis_size("y"), lax.axis_size("z")
    chans, cols = total.shape[0] // (ny * nz), total.shape[1] // part
    blocks = total.astype(jnp.bfloat16).reshape(ny * nz, chans, part, cols).transpose(0, 2, 1, 3)
    got = lax.all_to_all(blocks, CHAN, 0, 0, tiled=True)
    got = got.reshape(ny, nz, part, chans, cols).astype(jnp.float32)
    return jnp.sum(got, axis=1).reshape(ny * part, chans, cols)


def on_device(
    floor_tokens, token_table, depth_kernel, norm_gain, layer_scale, w_in, w_out, grad_out
):
    rows, cols = floor_tokens.shape
    chans = depth_kernel.shape[2]
    part = rows // lax.axis_size("y")
    offset = lax.axis_index(CHAN) * chans
    grad_local = grad_out.transpose(0, 2, 1)
    grad = spread(grad_local).astype(jnp.float32)
    x_local = jnp.take(token_table, floor_tokens, axis=0).transpose(0, 2, 1)
    conv_local = conv49(halo(x_local, 3), depth_kernel, rows, False).astype(jnp.bfloat16)
    w_in = lax.all_gather(w_in, "y", axis=1, tiled=True)
    w_out = lax.all_gather(w_out, "y", axis=0, tiled=True)
    conv = spread(conv_local).astype(jnp.float32)

    gain = norm_gain[:, None]
    mean = jnp.mean(conv, axis=0, keepdims=True)
    centered = conv - mean
    inv_std = lax.rsqrt(jnp.mean(centered * centered, axis=0, keepdims=True) + 1e-06)
    normed = centered * inv_std
    scaled = (normed * gain).astype(jnp.bfloat16)
    pre = lax.dot_general(w_in, scaled, (((0,), (0,)), ((), ())), preferred_element_type=jnp.float32)
    grad_mix = (layer_scale[:, None] * grad).astype(jnp.bfloat16)
    grad_act = jnp.dot(w_out, grad_mix, preferred_element_type=jnp.float32)
    act, vjp = jax.vjp(gelu_tanh, pre)
    mix = lax.dot_general(
        w_out, act.astype(jnp.bfloat16), (((0,), (0,)), ((), ())), preferred_element_type=jnp.float32
    )
    mix = collect(mix, part)
    grad_pre = vjp(grad_act)[0].astype(jnp.bfloat16)
    scaled_grad = jnp.dot(w_in, grad_pre, preferred_element_type=jnp.float32) * gain
    conv_part = inv_std * (
        scaled_grad
        - jnp.mean(scaled_grad, axis=0, keepdims=True)
        - normed * jnp.mean(scaled_grad * normed, axis=0, keepdims=True)
    )
    grad_conv = collect(conv_part, part).astype(jnp.bfloat16)

    scale_local = lax.dynamic_slice_in_dim(layer_scale, offset, chans, 0)[None, :, None]
    block_out = (x_local.astype(jnp.float32) + scale_local * mix).astype(jnp.bfloat16)
    through = conv49(halo(grad_conv, 3), depth_kernel, rows, True)
    grad_embedded = (grad_local.astype(jnp.float32) + through).astype(jnp.bfloat16)
    return block_out.transpose(0, 2, 1), grad_embedded.transpose(0, 2, 1)


def solution(mesh):
    chan, space = mesh.shape["chan"], mesh.shape["space"]
    grid = Mesh(mesh.devices.reshape(4, chan // 4, space // 4, 2, 2), AXES)
    placed = (
        P(SPACE, None),
        P(None, CHAN),
        P(None, None, CHAN),
        P(),
        P(),
        P(None, CHAN),
        P(CHAN, None),
        P(SPACE, None, CHAN),
    )
    return jax.shard_map(
        on_device,
        mesh=grid,
        in_specs=placed,
        out_specs=(P(SPACE, None, CHAN), P(SPACE, None, CHAN)),
        check_vma=False,
    )
```

time: 1010 us -> 255 us (0.25)
  the two profiles are of different devices: /device:TPU:6 before, /device:TPU:56 now
where the time goes in v1:
time: 255 us; the launch traced here: 254 us
  waiting for transfers between devices  147 us (58%)
  starting transfers between devices  56 us (22%)
  local copies, waits for them, and re-layouts  15.8 us (6%)
  between operations  14.4 us (6%)
  other arithmetic  12.7 us (5%)
  matrix products  8.22 us (3%)
    all_to_all x2, waiting for transfers between devices, collect(): got = lax.all_to_all(blocks, CHAN, 0, 0, tiled=True)  53.9 us
    all_gather x1, waiting for transfers between devices, on_device(): w_out = lax.all_gather(w_out, 'y', axis=0, tiled=True)  48 us
    all_to_all x2, waiting for transfers between devices, spread(): got = lax.all_to_all(blocks, CHAN, 0, 0, tiled=True)  30.5 us
    all_to_all x2, starting transfers between devices, spread(): got = lax.all_to_all(blocks, CHAN, 0, 0, tiled=True)  25.3 us
    all_to_all x2, starting transfers between devices, collect(): got = lax.all_to_all(blocks, CHAN, 0, 0, tiled=True)  20.3 us
    ppermute x2, waiting for transfers between devices, halo(): low = lax.ppermute(block[block.shape[0] - width:], SPACE, forward)  13 us
    ppermute x2, starting transfers between devices, halo(): high = lax.ppermute(block[:width], SPACE, backward)  6.08 us
  transfers between devices with their start and end apart: 10, of which 6 were waited for; matrix products, arithmetic and copies ran while one was open for 13% of the time, Pallas kernels for 0%

profile of v1, /device:TPU:56, one launch (start us, length us, event | category | flops | bytes accessed | tf_op | source)
XLA Modules:
  0.0 253.8 jit_solution(12506097691615239617)
XLA Ops:
  7.2 0.0 all-gather.3.cloned.1.call-start
  7.2 0.7 all-gather.3.cloned.1.call-update
  7.9 0.0 copy-start.2
  7.9 0.7 bitcast_clamp_fusion
  8.6 0.7 compare_and_fusion
  9.3 0.8 copy.23
  10.1 3.2 %gather_fusion = bf16[1024,32]{1,0:T(8,128)(2,1)S(1)} fusion(bf16[256,32]{1,0:T(8,128)(2,1)S(1)} %copy.23, s32[1024]{0:T(1024)S(1)} %bitcast_clamp_fusion), kind=kCustom, calls=%fused_computation | custom fusion | bytes 135168 | tf_op jit(solution)/shard_map/jit(_take)/gather | solution.py:64
  13.3 0.1 copy.24
  13.5 4.2 %collective-permute-start.1 = (bf16[3,32,128]{2,1,0:T(8,128)(2,1)S(1)}, bf16[3,32,128]{2,1,0:T(8,128)(2,1)S(1)}, u32[]{:S(2)}, u32[]{:S(2)}) collective-permute-start(bf16[3,32,128]{2,1,0:T(8,128)(2,1)S(1)} %get-tuple-element.5), channel_id=1, source_target_pairs={{1,0},{2,1},{3,2},{4,3},{5,4},{6,5},{7,6},{8,7},{9,8},{10,9},{11,1... | collective-permute-start | bytes 73736 | tf_op jit(solution)/shard_map/ppermute | solution.py:16
  17.7 1.9 collective-permute-start
  19.6 0.0 copy-done.2
  19.7 0.0 collective-permute-done.1
  19.7 7.0 %collective-permute-done = bf16[3,32,128]{2,1,0:T(8,128)(2,1)S(1)} collective-permute-done((bf16[3,32,128]{2,1,0:T(8,128)(2,1)S(1)}, bf16[3,32,128]{2,1,0:T(8,128)(2,1)S(1)}, u32[]{:S(2)}, u32[]{:S(2)}) %collective-permute-start) | collective-permute-done | bytes 24608 | tf_op jit(solution)/shard_map/ppermute | solution.py:15
  26.7 0.1 select_maximum_fusion.2
  26.9 1.2 fusion.64
  28.0 0.0 copy-start.1
  28.0 1.1 broadcast_in_dim.24
  29.1 18.9 %all-to-all-start = ((bf16[48,2,32,128]{3,2,1,0:T(8,128)(2,1)}), bf16[48,2,32,128]{3,2,1,0:T(8,128)(2,1)S(1)}, u32[]{:S(2)}, u32[]{:S(2)}) async-start(bf16[48,2,32,128]{3,2,1,0:T(8,128)(2,1)} %bitcast.53), calls=%async_computation | async-start | bytes 1572864 | tf_op jit(solution)/shard_map/all_to_all | solution.py:42
  48.0 0.0 all-gather.5.cloned.1.call-start
  48.1 0.7 all-gather.5.cloned.1.call-update
  48.8 0.0 copy-done.1
  48.8 0.1 copy.29
  48.8 30.5 %all-to-all-done = bf16[48,2,32,128]{3,2,1,0:T(8,128)(2,1)S(1)} async-done(((bf16[48,2,32,128]{3,2,1,0:T(8,128)(2,1)}), bf16[48,2,32,128]{3,2,1,0:T(8,128)(2,1)S(1)}, u32[]{:S(2)}, u32[]{:S(2)}) %all-to-all-start) | async-done | bytes 786464 | tf_op jit(solution)/shard_map/all_to_all | solution.py:42
  79.3 1.6 broadcast_in_dim.26
  80.9 6.4 %all-to-all-start.2 = ((bf16[48,2,32,128]{3,1,2,0:T(2,128)(2,1)}), bf16[48,2,32,128]{3,1,2,0:T(2,128)(2,1)}, u32[]{:S(2)}, u32[]{:S(2)}) async-start(bf16[48,2,32,128]{3,1,2,0:T(2,128)(2,1)} %bitcast.65), calls=%async_computation.2 | async-start | bytes 1572864 | tf_op jit(solution)/shard_map/all_to_all | solution.py:42
  87.4 0.2 convert_bitcast_fusion
  87.6 1.4 copy.25
  89.0 1.3 copy.45
  90.2 1.9 copy.26
  92.1 0.0 copy-start.3
  92.1 0.2 fusion.6
  92.3 0.2 multiply_reduce_fusion
  92.6 0.0 all-gather.3.cloned.1.call-done
  92.6 0.2 copy-done.3
  92.8 2.0 convolution_bitcast_fusion.1
  94.8 0.0 copy-start
  94.8 48.0 %all-gather.5.cloned.1.call-done = bf16[512,1536]{1,0:T(8,128)(2,1)} async-done(((bf16[128,1536]{1,0:T(8,128)(2,1)}), bf16[512,1536]{1,0:T(8,128)(2,1)}) %all-gather.5.cloned.1.call-update) | async-done | bytes 1572880 | tf_op jit(solution)/shard_map/all_gather | solution.py:67
  142.8 2.0 fusion
  144.8 0.3 copy.27
  145.1 0.2 reshape.429
  145.3 1.1 copy.46
  146.4 0.0 all-to-all-done.2
  146.4 13.9 %all-to-all-start.1 = ((bf16[48,2,32,128]{3,2,1,0:T(8,128)(2,1)}), bf16[48,2,32,128]{3,2,1,0:T(8,128)(2,1)}, u32[]{:S(2)}, u32[]{:S(2)}) async-start(bf16[48,2,32,128]{3,2,1,0:T(8,128)(2,1)} %bitcast.235), calls=%async_computation.1 | async-start | bytes 1572864 | tf_op jit(solution)/shard_map/all_to_all | solution.py:50
  160.3 0.0 copy-start.4
  160.3 2.9 %convert_element_type.1185 = f32[48,2,32,128]{3,1,2,0:T(2,128)} convert(bf16[48,2,32,128]{3,1,2,0:T(2,128)(2,1)} %all-to-all-done.2) | non-fusion elementwise | flops 393216 | bytes 2359296 | tf_op jit(solution)/shard_map/convert_element_type | solution.py:63
  163.2 0.0 copy-done.4
  163.2 4.2 %fusion.5 = (f32[256]{0:T(256)S(1)}, f32[256,1536]{1,0:T(8,128)S(1)}) fusion(f32[1536,256]{0,1:T(8,128)S(1)} %copy.26, f32[256]{0:T(256)S(1)} %rsqrt_bitcast_fusion, f32[256]{0:T(256)S(1)} %get-tuple-element.55, f32[1536]{0:T(1024)S(1)} %copy-done.3, bf16[1536,512]{1,0:T(8,128)(2,1)} %all-gather.3.cloned.1.call-done, f32[512,256]{0,1:T(8,128)} %copy-done, ...), kind=kOutput, calls=%fused_computation.13 | convolution fusion | flops 810680064 | bytes 8403968 | tf_op jit(solution)/shard_map/dot_general | solution.py:85
  167.4 0.2 reduce_sum.57
  167.6 1.4 fusion.4
  168.9 1.4 copy.30
  170.3 1.1 reshape.432
  171.4 22.1 %all-to-all-done.1 = bf16[48,2,32,128]{3,2,1,0:T(8,128)(2,1)} async-done(((bf16[48,2,32,128]{3,2,1,0:T(8,128)(2,1)}), bf16[48,2,32,128]{3,2,1,0:T(8,128)(2,1)}, u32[]{:S(2)}, u32[]{:S(2)}) %all-to-all-start.1) | async-done | bytes 786464 | tf_op jit(solution)/shard_map/all_to_all | solution.py:50
  193.5 6.4 %all-to-all-start.3 = ((bf16[48,2,32,128]{3,1,2,0:T(2,128)(2,1)}), bf16[48,2,32,128]{3,1,2,0:T(2,128)(2,1)S(1)}, u32[]{:S(2)}, u32[]{:S(2)}) async-start(bf16[48,2,32,128]{3,1,2,0:T(2,128)(2,1)} %bitcast.69), calls=%async_computation.3 | async-start | bytes 1572864 | tf_op jit(solution)/shard_map/all_to_all | solution.py:50
  199.9 0.1 dynamic_slice.3
  200.0 1.3 convert_reduce_fusion
  201.3 31.8 %all-to-all-done.3 = bf16[48,2,32,128]{3,1,2,0:T(2,128)(2,1)S(1)} async-done(((bf16[48,2,32,128]{3,1,2,0:T(2,128)(2,1)}), bf16[48,2,32,128]{3,1,2,0:T(2,128)(2,1)S(1)}, u32[]{:S(2)}, u32[]{:S(2)}) %all-to-all-start.3) | async-done | bytes 786464 | tf_op jit(solution)/shard_map/all_to_all | solution.py:50
  233.1 0.8 reduce.4
  233.9 1.9 collective-permute-start.3
  235.8 2.4 collective-permute-start.2
  238.3 0.7 fusion.63
  239.0 0.0 collective-permute-done.3
  239.0 5.9 %collective-permute-done.2 = bf16[3,32,128]{2,1,0:T(8,128)(2,1)S(1)} collective-permute-done((bf16[3,32,128]{2,1,0:T(8,128)(2,1)S(1)}, bf16[3,32,128]{2,1,0:T(8,128)(2,1)S(1)}, u32[]{:S(2)}, u32[]{:S(2)}) %collective-permute-start.2) | collective-permute-done | bytes 24608 | tf_op jit(solution)/shard_map/ppermute | solution.py:15
  244.9 0.1 select_maximum_fusion
  245.0 1.9 fusion.73
  (11 shorter events, 0.1 us)
Async XLA Ops:
  7.2 85.4 %all-gather.3.cloned.1.call-start = ((), (), s32[]{:S(2)}) async-start(), calls=%async_computation.4 | async-start | bytes 1966080 | tf_op jit(solution)/shard_map/all_gather | solution.py:66
  7.9 11.7 %copy-start.2 = (bf16[7,7,32]{2,1,0:T(8,128)(2,1)S(1)}, bf16[7,7,32]{2,1,0:T(8,128)(2,1)}, u32[]{:S(2)}) copy-start(bf16[7,7,32]{2,1,0:T(8,128)(2,1)} %param.10) | copy-start | bytes 9412
  13.5 6.2 %collective-permute-start.1 = (bf16[3,32,128]{2,1,0:T(8,128)(2,1)S(1)}, bf16[3,32,128]{2,1,0:T(8,128)(2,1)S(1)}, u32[]{:S(2)}, u32[]{:S(2)}) collective-permute-start(bf16[3,32,128]{2,1,0:T(8,128)(2,1)S(1)} %get-tuple-element.5), channel_id=1, source_target_pairs={{1,0},{2,1},{3,2},{4,3},{5,4},{6,5},{7,6},{8,7},{9,8},{10,9},{11,1... | collective-permute-start | bytes 73736 | tf_op jit(solution)/shard_map/ppermute | solution.py:16
  17.7 9.1 %collective-permute-start = (bf16[3,32,128]{2,1,0:T(8,128)(2,1)S(1)}, bf16[3,32,128]{2,1,0:T(8,128)(2,1)S(1)}, u32[]{:S(2)}, u32[]{:S(2)}) collective-permute-start(bf16[3,32,128]{2,1,0:T(8,128)(2,1)S(1)} %get-tuple-element.4), channel_id=1, source_target_pairs={{0,1},{1,2},{2,3},{3,4},{4,5},{5,6},{6,7},{7,8},{8,9},{9,10},{10,1... | collective-permute-start | bytes 73736 | tf_op jit(solution)/shard_map/ppermute | solution.py:15
  28.0 20.7 %copy-start.1 = (bf16[8,128,32]{1,2,0:T(8,128)(2,1)S(1)}, bf16[8,128,32]{1,2,0:T(8,128)(2,1)}, u32[]{:S(2)}) copy-start(bf16[8,128,32]{1,2,0:T(8,128)(2,1)} %param.15) | copy-start | bytes 196612
  29.1 50.2 %all-to-all-start = ((bf16[48,2,32,128]{3,2,1,0:T(8,128)(2,1)}), bf16[48,2,32,128]{3,2,1,0:T(8,128)(2,1)S(1)}, u32[]{:S(2)}, u32[]{:S(2)}) async-start(bf16[48,2,32,128]{3,2,1,0:T(8,128)(2,1)} %bitcast.53), calls=%async_computation | async-start | bytes 1572864 | tf_op jit(solution)/shard_map/all_to_all | solution.py:42
  48.0 94.8 %all-gather.5.cloned.1.call-start = ((), (), s32[]{:S(2)}) async-start(), calls=%async_computation.5 | async-start | bytes 1966080 | tf_op jit(solution)/shard_map/all_gather | solution.py:67
  80.9 65.4 %all-to-all-start.2 = ((bf16[48,2,32,128]{3,1,2,0:T(2,128)(2,1)}), bf16[48,2,32,128]{3,1,2,0:T(2,128)(2,1)}, u32[]{:S(2)}, u32[]{:S(2)}) async-start(bf16[48,2,32,128]{3,1,2,0:T(2,128)(2,1)} %bitcast.65), calls=%async_computation.2 | async-start | bytes 1572864 | tf_op jit(solution)/shard_map/all_to_all | solution.py:42
  92.1 0.7 copy-start.3
  94.8 48.0 %copy-start = (f32[512,256]{0,1:T(8,128)}, f32[512,256]{0,1:T(8,128)S(1)}, u32[]{:S(2)}) copy-start(f32[512,256]{0,1:T(8,128)S(1)} %convolution_bitcast_fusion.1) | copy-start | bytes 1572868
  146.4 47.1 %all-to-all-start.1 = ((bf16[48,2,32,128]{3,2,1,0:T(8,128)(2,1)}), bf16[48,2,32,128]{3,2,1,0:T(8,128)(2,1)}, u32[]{:S(2)}, u32[]{:S(2)}) async-start(bf16[48,2,32,128]{3,2,1,0:T(8,128)(2,1)} %bitcast.235), calls=%async_computation.1 | async-start | bytes 1572864 | tf_op jit(solution)/shard_map/all_to_all | solution.py:50
  160.3 2.9 %copy-start.4 = (f32[1536]{0:T(1024)S(1)}, f32[1536]{0:T(1024)}, u32[]{:S(2)}) copy-start(f32[1536]{0:T(1024)} %param.12) | copy-start | bytes 18436
  193.5 39.6 %all-to-all-start.3 = ((bf16[48,2,32,128]{3,1,2,0:T(2,128)(2,1)}), bf16[48,2,32,128]{3,1,2,0:T(2,128)(2,1)S(1)}, u32[]{:S(2)}, u32[]{:S(2)}) async-start(bf16[48,2,32,128]{3,1,2,0:T(2,128)(2,1)} %bitcast.69), calls=%async_computation.3 | async-start | bytes 1572864 | tf_op jit(solution)/shard_map/all_to_all | solution.py:50
  233.9 5.1 %collective-permute-start.3 = (bf16[3,32,128]{2,1,0:T(8,128)(2,1)S(1)}, bf16[3,32,128]{2,1,0:T(8,128)(2,1)S(1)}, u32[]{:S(2)}, u32[]{:S(2)}) collective-permute-start(bf16[3,32,128]{2,1,0:T(8,128)(2,1)S(1)} %get-tuple-element.3), channel_id=1, source_target_pairs={{1,0},{2,1},{3,2},{4,3},{5,4},{6,5},{7,6},{8,7},{9,8},{10,9},{11,1... | collective-permute-start | bytes 73736 | tf_op jit(solution)/shard_map/ppermute | solution.py:16
  235.8 9.1 %collective-permute-start.2 = (bf16[3,32,128]{2,1,0:T(8,128)(2,1)S(1)}, bf16[3,32,128]{2,1,0:T(8,128)(2,1)S(1)}, u32[]{:S(2)}, u32[]{:S(2)}) collective-permute-start(bf16[3,32,128]{2,1,0:T(8,128)(2,1)S(1)} %get-tuple-element.2), channel_id=1, source_target_pairs={{0,1},{1,2},{2,3},{3,4},{4,5},{5,6},{6,7},{7,8},{8,9},{9,10},{10,1... | collective-permute-start | bytes 73736 | tf_op jit(solution)/shard_map/ppermute | solution.py:15
Sparse Core Ops, SparseCore 0:
  10.4 70.8 all-gather.2
  83.7 59.0 all-gather.4

commit v2 on v1

v2 whole, which is shorter than its diff:
```python
import functools
import math

import jax
import jax.numpy as jnp
from jax import lax
from jax.experimental import pallas as pl
from jax.experimental.pallas import tpu as pltpu
from jax.sharding import Mesh, PartitionSpec as P

AXES = ("y", "z", "x", "h", "c")
CHAN = ("y", "z")
SPACE = ("x", "h", "c")
BF16, F32 = jnp.bfloat16, jnp.float32
VMEM = pl.BlockSpec(memory_space=pltpu.VMEM)
ANY = pl.BlockSpec(memory_space=pl.ANY)
ROOT = math.sqrt(2.0 / math.pi)


def edges(low_side, high_side):
    count = lax.axis_size(SPACE)
    forward = [(i, i + 1) for i in range(count - 1)]
    backward = [(j, i) for i, j in forward]
    return lax.ppermute(high_side, SPACE, forward), lax.ppermute(low_side, SPACE, backward)


def conv_rows(framed, taps_ref, flip, emit):
    rows = len(framed) - 6
    chans, cols = framed[0].shape
    lane = lax.broadcasted_iota(jnp.int32, (chans, cols), 1)
    totals = [jnp.zeros((chans, cols), F32) for _ in range(rows)]
    for b in range(7):
        step = (6 - b if flip else b) - 3
        taps = [
            jnp.broadcast_to(taps_ref[:, a * 7 + b : a * 7 + b + 1].astype(F32), (chans, cols))
            for a in range(7)
        ]
        inside = (lane + step >= 0) & (lane + step < cols)
        for i, tile in enumerate(framed):
            if step:
                tile = jnp.where(inside, pltpu.roll(tile, (-step) % cols, 1), 0.0)
            for a in range(7):
                r = i - (6 - a if flip else a)
                if 0 <= r < rows:
                    totals[r] = totals[r] + tile * taps[a]
    for r in range(rows):
        emit(r, totals[r])


def first_kernel(copies, tok_ref, low_ref, high_ref, table_ref, taps_ref, scale_ref, grad_ref, x_ref, send_ref):
    rows, cols = tok_ref.shape
    chans, vocab = table_ref.shape
    ident = lax.broadcasted_iota(jnp.int32, (vocab, cols), 0) + 1
    lines = [low_ref[i : i + 1] for i in range(3)]
    lines += [tok_ref[i : i + 1] + 1 for i in range(rows)]
    lines += [high_ref[i : i + 1] for i in range(3)]
    framed = []
    for line in lines:
        hot = (ident == line).astype(F32).astype(BF16)
        framed.append(jnp.dot(table_ref[...], hot, preferred_element_type=F32))
    for r in range(rows):
        x_ref[r] = framed[r + 3].astype(BF16)

    def targets(r):
        return [(r // 2) * 2 * copies + 2 * k + r % 2 for k in range(copies)]

    scale = jnp.broadcast_to(scale_ref[...], (chans, cols))
    for r in range(rows):
        mixed = (grad_ref[r].astype(F32) * scale).astype(BF16)
        for d in targets(r):
            send_ref[d, 1] = mixed

    def emit(r, total):
        total = total.astype(BF16)
        for d in targets(r):
            send_ref[d, 0] = total

    conv_rows(framed, taps_ref, False, emit)


def middle_kernel(
    own_ref, oth_ref, gain_ref, w0_ref, w1_ref, w2_ref, w3_ref,
    keep_ref, sib_ref,
    win, wout, scaled, gmix, normed, grads, act, gpre, sem,
):
    blocks, _, chans, cols = own_ref.shape
    width = blocks * chans
    hid = w0_ref.shape[1]
    pieces = [(ref.at[0], ref.at[1]) for ref in (w0_ref, w1_ref, w2_ref, w3_ref)]
    copies = []
    for i, (a, b) in enumerate(pieces):
        spot = pl.ds(i * hid, hid)
        copies.append(pltpu.make_async_copy(a, win.at[spot], sem.at[2 * i]))
        copies.append(pltpu.make_async_copy(b, wout.at[spot], sem.at[2 * i + 1]))
    for copy in copies:
        copy.start()

    def cell(s, t):
        return jnp.concatenate([own_ref[s, t], oth_ref[s, t]], axis=1)

    zero = jnp.zeros((chans, 2 * cols), F32)
    total = lax.fori_loop(0, blocks, lambda s, acc: acc + cell(s, 0).astype(F32), zero, unroll=8)
    mean = jnp.sum(total, axis=0, keepdims=True) * (1.0 / width)

    def square(s, acc):
        diff = cell(s, 0).astype(F32) - mean
        return acc + diff * diff

    total = lax.fori_loop(0, blocks, square, zero, unroll=8)
    inv_std = lax.rsqrt(jnp.sum(total, axis=0, keepdims=True) * (1.0 / width) + 1e-06)

    def norm(s, carry):
        spot = pl.ds(pl.multiple_of(s * chans, chans), chans)
        value = (cell(s, 0).astype(F32) - mean) * inv_std
        gain = gain_ref[spot, :]
        normed[spot, :] = value
        scaled[spot, :] = (value * jnp.concatenate([gain, gain], axis=1)).astype(BF16)
        gmix[spot, :] = cell(s, 1)
        return carry

    lax.fori_loop(0, blocks, norm, 0, unroll=4)
    for copy in copies:
        copy.wait()

    for i in range(len(pieces)):
        spot = pl.ds(i * hid, hid)
        pre = jnp.dot(win[spot, :], scaled[...], preferred_element_type=F32)
        gact = jnp.dot(wout[spot, :], gmix[...], preferred_element_type=F32)
        cube = pre * pre
        tanh = jnp.tanh(ROOT * (pre + 0.044715 * (cube * pre)))
        half = 0.5 * (1.0 + tanh)
        act[spot, :] = (pre * half).astype(BF16)
        slope = half + (0.5 * pre) * (1.0 - tanh * tanh) * (ROOT * (1.0 + 0.134145 * cube))
        gpre[spot, :] = (gact * slope).astype(BF16)

    group = 256
    per = group // chans
    sums = [jnp.zeros((1, 2 * cols), F32), jnp.zeros((1, 2 * cols), F32)]
    turned = (((0,), (0,)), ((), ()))
    for j in range(width // group):
        spot = pl.ds(j * group, group)
        gain = gain_ref[spot, :]
        part = lax.dot_general(win[:, spot], gpre[...], turned, preferred_element_type=F32)
        part = part * jnp.concatenate([gain, gain], axis=1)
        grads[spot, :] = part
        sums[0] = sums[0] + jnp.sum(part, axis=0, keepdims=True)
        sums[1] = sums[1] + jnp.sum(part * normed[spot, :], axis=0, keepdims=True)
        mix = lax.dot_general(wout[:, spot], act[...], turned, preferred_element_type=F32)
        for q in range(per):
            piece = mix[q * chans : (q + 1) * chans]
            keep_ref[j * per + q, 0] = piece[:, :cols]
            sib_ref[j * per + q, 0] = piece[:, cols:].astype(BF16)
    first, second = sums[0] * (1.0 / width), sums[1] * (1.0 / width)

    def finish(s, carry):
        spot = pl.ds(pl.multiple_of(s * chans, chans), chans)
        piece = inv_std * (grads[spot, :] - first - normed[spot, :] * second)
        keep_ref[s, 1] = piece[:, :cols]
        sib_ref[s, 1] = piece[:, cols:].astype(BF16)
        return carry

    lax.fori_loop(0, blocks, finish, 0, unroll=4)


def sum_kernel(copies, got_ref, x_ref, scale_ref, out_ref, gconv_ref, low_ref, high_ref):
    rows, chans, cols = x_ref.shape
    scale = jnp.broadcast_to(scale_ref[...], (chans, cols))
    for r in range(rows):
        base = (r // 2) * 2 * copies + r % 2
        mix = got_ref[base, 0].astype(F32)
        conv = got_ref[base, 1].astype(F32)
        for k in range(1, copies):
            mix = mix + got_ref[base + 2 * k, 0].astype(F32)
            conv = conv + got_ref[base + 2 * k, 1].astype(F32)
        out_ref[r] = (x_ref[r].astype(F32) + scale * mix).astype(BF16)
        conv = conv.astype(BF16)
        gconv_ref[r] = conv
        if r < 3:
            low_ref[r] = conv
        if r >= rows - 3:
            high_ref[r - rows + 3] = conv


def last_kernel(gconv_ref, low_ref, high_ref, taps_ref, grad_ref, out_ref):
    rows = gconv_ref.shape[0]
    framed = [low_ref[i].astype(F32) for i in range(3)]
    framed += [gconv_ref[i].astype(F32) for i in range(rows)]
    framed += [high_ref[i].astype(F32) for i in range(3)]

    def emit(r, total):
        out_ref[r] = (grad_ref[r].astype(F32) + total).astype(BF16)

    conv_rows(framed, taps_ref, True, emit)


def call(body, outs, args, specs=None, scratch=(), flops=1 << 20, limit=32 << 20):
    outs = [jax.ShapeDtypeStruct(s, d) for s, d in outs]
    return pl.pallas_call(
        body,
        out_shape=outs,
        in_specs=specs or [VMEM] * len(args),
        out_specs=[VMEM] * len(outs),
        scratch_shapes=list(scratch),
        compiler_params=pltpu.CompilerParams(vmem_limit_bytes=limit),
        cost_estimate=pl.CostEstimate(flops=flops, bytes_accessed=4 << 20, transcendentals=0),
    )(*args)


def pair_weights(w_in, w_out):
    both = jnp.stack([w_in.T, w_out])
    nz, nh, ny = lax.axis_size("z"), lax.axis_size("h"), lax.axis_size("y")
    pairs = []
    for z in range(nz):
        for c in range(2):
            other = (z, c) if z % 2 == c else (z ^ 1, 1 - c)
            pairs.append((other[0] * 2 + other[1], z * 2 + c))
    return lax.ppermute(both, ("z", "c"), pairs)


def ring_weights(both):
    nh, ny = lax.axis_size("h"), lax.axis_size("y")
    ring = [y * nh + h for h in range(nh) for y in range(ny)]
    count = len(ring)

    def from_steps(steps):
        pairs = [
            (ring[(i + steps[c]) % count] * 2 + c, ring[i] * 2 + c) for i in range(count) for c in range(2)
        ]
        return lax.ppermute(both, ("y", "h", "c"), pairs)

    return both, from_steps((2, -2)), from_steps((1, 1)), from_steps((-1, -1))


def on_device(
    floor_tokens, token_table, depth_kernel, norm_gain, layer_scale, w_in, w_out, grad_out
):
    rows, cols = floor_tokens.shape
    chans = depth_kernel.shape[2]
    width = norm_gain.shape[0]
    blocks = width // chans
    copies = lax.axis_size("z") // 2
    hid = w_out.shape[0] * lax.axis_size("y")
    swap = [(0, 1), (1, 0)]

    both = pair_weights(w_in, w_out)
    low, high = edges(floor_tokens[:3] + 1, floor_tokens[rows - 3 :] + 1)
    taps = depth_kernel.reshape(49, chans).T
    scale = lax.dynamic_slice_in_dim(layer_scale, lax.axis_index(CHAN) * chans, chans, 0)[:, None]
    gain = jnp.broadcast_to(norm_gain[:, None], (width, cols))
    grad_local = grad_out.transpose(0, 2, 1)

    tile = (rows, chans, cols)
    packed = (blocks, 2, chans, cols)
    x_local, send = call(
        functools.partial(first_kernel, copies),
        [(tile, BF16), (packed, BF16)],
        (floor_tokens, low, high, token_table.T, taps, scale, grad_local),
    )
    send, both = lax.optimization_barrier((send, both))
    weights = ring_weights(both)
    own = lax.all_to_all(send, CHAN, 0, 0, tiled=True)
    oth = lax.ppermute(own, "c", swap)
    keep, sib = call(
        middle_kernel,
        [(packed, F32), (packed, BF16)],
        (own, oth, gain, *weights),
        [VMEM] * 3 + [ANY] * 4,
        [
            pltpu.VMEM((hid, width), BF16),
            pltpu.VMEM((hid, width), BF16),
            pltpu.VMEM((width, 2 * cols), BF16),
            pltpu.VMEM((width, 2 * cols), BF16),
            pltpu.VMEM((width, 2 * cols), F32),
            pltpu.VMEM((width, 2 * cols), F32),
            pltpu.VMEM((hid, 2 * cols), BF16),
            pltpu.VMEM((hid, 2 * cols), BF16),
            pltpu.SemaphoreType.DMA((8,)),
        ],
        flops=8 * hid * width * 2 * cols,
        limit=40 << 20,
    )
    part = (keep + lax.ppermute(sib, "c", swap).astype(F32)).astype(BF16)
    got = lax.all_to_all(part, CHAN, 0, 0, tiled=True)
    edge = (3, chans, cols)
    block_out, gconv, low_side, high_side = call(
        functools.partial(sum_kernel, copies),
        [(tile, BF16), (tile, BF16), (edge, BF16), (edge, BF16)],
        (got, x_local, scale),
    )
    low, high = edges(low_side, high_side)
    (grad_embedded,) = call(last_kernel, [(tile, BF16)], (gconv, low, high, taps, grad_local))
    return block_out.transpose(0, 2, 1), grad_embedded.transpose(0, 2, 1)


def solution(mesh):
    chan, space = mesh.shape["chan"], mesh.shape["space"]
    grid = Mesh(mesh.devices.reshape(4, chan // 4, space // 4, 2, 2), AXES)
    placed = (
        P(SPACE, None),
        P(None, CHAN),
        P(None, None, CHAN),
        P(),
        P(),
        P(None, CHAN),
        P(CHAN, None),
        P(SPACE, None, CHAN),
    )
    return jax.shard_map(
        on_device,
        mesh=grid,
        in_specs=placed,
        out_specs=(P(SPACE, None, CHAN), P(SPACE, None, CHAN)),
        check_vma=False,
    )
```

time: 255 us -> 163 us (0.64)
  the two profiles are of different devices: /device:TPU:56 before, /device:TPU:57 now
where the time goes in v2:
time: 163 us; the launch traced here: 162 us
  starting transfers between devices  62.1 us (38%)
  waiting for transfers between devices  48.4 us (30%)
  blocking collectives  39.8 us (24%)
  Pallas kernels  7.98 us (5%)
  local copies, waits for them, and re-layouts  1.77 us (1%)
    all_to_all x1, blocking collectives, on_device(): got = lax.all_to_all(part, CHAN, 0, 0, tiled=True)  39.8 us
    all_to_all x1, waiting for transfers between devices, on_device(): own = lax.all_to_all(send, CHAN, 0, 0, tiled=True)  20.5 us
    ppermute x2, starting transfers between devices, edges(): lax.ppermute(high_side, SPACE, forward)  18.6 us
    all_to_all x1, starting transfers between devices, on_device(): own = lax.all_to_all(send, CHAN, 0, 0, tiled=True)  17.4 us
    ppermute x3, waiting for transfers between devices, from_steps(): return lax.ppermute(both, ('y', 'h', 'c'), pairs)  17.2 us
    ppermute x1, starting transfers between devices, on_device(): oth = lax.ppermute(own, 'c', swap)  8.61 us
    ppermute x2, waiting for transfers between devices, edges(): lax.ppermute(low_side, SPACE, backward)  8.02 us
    pallas_call x4, Pallas kernels, call(): pl.pallas_call(body, out_shape=outs, in_specs=specs or [VMEM] * len(args)...  7.98 us
  transfers between devices with their start and end apart: 11, of which 6 were waited for; matrix products, arithmetic and copies ran while one was open for 0% of the time, Pallas kernels for 1%

profile of v2, /device:TPU:57, one launch (start us, length us, event | category | flops | bytes accessed | tf_op | source)
XLA Modules:
  0.0 162.2 jit_solution(13876507962318777972)
XLA Ops:
  0.6 0.0 copy-start
  0.6 0.0 copy-start.3
  0.7 0.0 copy-start.4
  0.7 0.0 copy-start.1
  0.7 0.0 copy-start.2
  0.7 1.2 copy.16
  1.9 0.0 copy-start.5
  1.9 1.1 pad_maximum_fusion
  3.0 4.6 %collective-permute-start.2 = (bf16[2,128,1536]{2,1,0:T(8,128)(2,1)S(1)}, bf16[2,128,1536]{2,1,0:T(8,128)(2,1)S(1)}, u32[]{:S(2)}, u32[]{:S(2)}) collective-permute-start(bf16[2,128,1536]{2,1,0:T(8,128)(2,1)S(1)} %pad_maximum_fusion), channel_id=1, source_target_pairs={{0,0},{16,1},{1,16},{17,17},{32,32},{48,33},{33,48},{49,49},{64,64... | collective-permute-start | bytes 2359304 | tf_op jit(solution)/shard_map/ppermute | solution.py:217
  7.6 0.0 copy-done.3
  7.6 1.9 %collective-permute-start.1 = (s32[3,128]{1,0:T(4,128)S(1)}, s32[3,128]{1,0:T(4,128)S(1)}, u32[]{:S(2)}, u32[]{:S(2)}) collective-permute-start(s32[3,128]{1,0:T(4,128)S(1)} %get-tuple-element.22), channel_id=1, source_target_pairs={{1,0},{2,1},{3,2},{4,3},{5,4},{6,5},{7,6},{8,7},{9,8},{10,9},{11,1... | collective-permute-start | bytes 4616 | tf_op jit(solution)/shard_map/ppermute | solution.py:24
  9.5 8.4 %collective-permute-start = (s32[3,128]{1,0:T(4,128)S(1)}, s32[3,128]{1,0:T(4,128)S(1)}, u32[]{:S(2)}, u32[]{:S(2)}) collective-permute-start(s32[3,128]{1,0:T(4,128)S(1)} %get-tuple-element.23), channel_id=1, source_target_pairs={{0,1},{1,2},{2,3},{3,4},{4,5},{5,6},{6,7},{7,8},{8,9},{9,10},{10,1... | collective-permute-start | bytes 4616 | tf_op jit(solution)/shard_map/ppermute | solution.py:24
  18.0 0.0 copy-done
  18.0 0.1 dynamic-slice_bitcast_fusion
  18.1 0.0 copy-done.4
  18.1 0.1 copy.14
  18.2 0.1 copy.15.scale_ref
  18.3 0.0 collective-permute-done.1.high_ref
  18.3 0.4 collective-permute-done.low_ref
  18.7 0.0 copy-done.1
  18.7 0.0 copy-done.2
  18.7 1.7 %shard_map.95 = (bf16[8,32,128]{2,1,0:T(8,128)(2,1)S(1)}, bf16[48,2,32,128]{3,2,1,0:T(8,128)(2,1)}) custom-call(s32[8,128]{1,0:T(8,128)S(1)} %copy-done.3, s32[3,128]{1,0:T(4,128)S(1)} %collective-permute-done.low_ref, s32[3,128]{1,0:T(4,128)S(1)} %collective-permute-done.1.high_ref, bf16[32,256]{1,0:T(8,128)(2,1)S(1)} %bitcast.15, ...), custom_call_target="tpu_custom_call" | custom-call | flops 1048576 | bytes 4194304 | tf_op jit(solution)/shard_map/pallas_call | solution.py:198
  20.4 0.0 collective-permute-done.2.w0_ref
  20.4 17.4 %all-to-all-start = ((bf16[48,2,32,128]{3,2,1,0:T(8,128)(2,1)}), bf16[48,2,32,128]{3,2,1,0:T(8,128)(2,1)S(1)}, u32[]{:S(2)}, u32[]{:S(2)}) async-start(bf16[48,2,32,128]{3,2,1,0:T(8,128)(2,1)} %get-tuple-element.13), calls=%async_computation | async-start | bytes 1572864 | tf_op jit(solution)/shard_map/all_to_all | solution.py:261
  37.8 1.9 %collective-permute-start.6 = (bf16[2,128,1536]{2,1,0:T(8,128)(2,1)S(1)}, bf16[2,128,1536]{2,1,0:T(8,128)(2,1)S(1)}, u32[]{:S(2)}, u32[]{:S(2)}) collective-permute-start(bf16[2,128,1536]{2,1,0:T(8,128)(2,1)S(1)} %collective-permute-done.2.w0_ref), channel_id=1, source_target_pairs={{578,0},{579,1},{0,192},{1,193},{192,384},{193,385},{384,576},{385... | collective-permute-start | bytes 2359304 | tf_op jit(solution)/shard_map/ppermute | solution.py:229
  39.7 3.4 %collective-permute-start.5 = (bf16[2,128,1536]{2,1,0:T(8,128)(2,1)S(1)}, bf16[2,128,1536]{2,1,0:T(8,128)(2,1)S(1)}, u32[]{:S(2)}, u32[]{:S(2)}) collective-permute-start(bf16[2,128,1536]{2,1,0:T(8,128)(2,1)S(1)} %collective-permute-done.2.w0_ref), channel_id=1, source_target_pairs={{192,0},{193,1},{384,192},{385,193},{576,384},{577,385},{2,576},{3... | collective-permute-start | bytes 2359304 | tf_op jit(solution)/shard_map/ppermute | solution.py:229
  43.1 1.9 %collective-permute-start.4 = (bf16[2,128,1536]{2,1,0:T(8,128)(2,1)S(1)}, bf16[2,128,1536]{2,1,0:T(8,128)(2,1)}, u32[]{:S(2)}, u32[]{:S(2)}) collective-permute-start(bf16[2,128,1536]{2,1,0:T(8,128)(2,1)S(1)} %collective-permute-done.2.w0_ref), channel_id=1, source_target_pairs={{384,0},{387,1},{576,192},{579,193},{2,384},{1,385},{194,576},{193... | collective-permute-start | bytes 2359304 | tf_op jit(solution)/shard_map/ppermute | solution.py:229
  45.0 20.5 %all-to-all-done.own_ref = bf16[48,2,32,128]{3,2,1,0:T(8,128)(2,1)S(1)} async-done(((bf16[48,2,32,128]{3,2,1,0:T(8,128)(2,1)}), bf16[48,2,32,128]{3,2,1,0:T(8,128)(2,1)S(1)}, u32[]{:S(2)}, u32[]{:S(2)}) %all-to-all-start) | async-done | bytes 786464 | tf_op jit(solution)/shard_map/all_to_all | solution.py:261
  65.6 8.6 %collective-permute-start.3 = (bf16[48,2,32,128]{3,2,1,0:T(8,128)(2,1)S(1)}, bf16[48,2,32,128]{3,2,1,0:T(8,128)(2,1)S(1)}, u32[]{:S(2)}, u32[]{:S(2)}) collective-permute-start(bf16[48,2,32,128]{3,2,1,0:T(8,128)(2,1)S(1)} %all-to-all-done.own_ref), channel_id=1, source_target_pairs={{0,1},{1,0},{2,3},{3,2},{4,5},{5,4},{6,7},{7,6},{8,9},{9,8},{10,11... | collective-permute-start | bytes 2359304 | tf_op jit(solution)/shard_map/ppermute | solution.py:262
  74.2 0.0 collective-permute-done.6.w3_ref
  74.2 2.7 %collective-permute-done.5.w2_ref = bf16[2,128,1536]{2,1,0:T(8,128)(2,1)S(1)} collective-permute-done((bf16[2,128,1536]{2,1,0:T(8,128)(2,1)S(1)}, bf16[2,128,1536]{2,1,0:T(8,128)(2,1)S(1)}, u32[]{:S(2)}, u32[]{:S(2)}) %collective-permute-start.5) | collective-permute-done | bytes 786464 | tf_op jit(solution)/shard_map/ppermute | solution.py:229
  76.8 14.5 %collective-permute-done.4.w1_ref = bf16[2,128,1536]{2,1,0:T(8,128)(2,1)} collective-permute-done((bf16[2,128,1536]{2,1,0:T(8,128)(2,1)S(1)}, bf16[2,128,1536]{2,1,0:T(8,128)(2,1)}, u32[]{:S(2)}, u32[]{:S(2)}) %collective-permute-start.4) | collective-permute-done | bytes 786464 | tf_op jit(solution)/shard_map/ppermute | solution.py:229
  91.3 0.0 collective-permute-done.3.oth_ref
  91.4 0.0 copy-done.5
  91.4 0.3 broadcast_in_dim.10.gain_ref
  91.6 4.2 %shard_map.96 = (f32[48,2,32,128]{3,2,1,0:T(8,128)S(1)}, bf16[48,2,32,128]{3,2,1,0:T(8,128)(2,1)S(1)}) custom-call(bf16[48,2,32,128]{3,2,1,0:T(8,128)(2,1)S(1)} %all-to-all-done.own_ref, bf16[48,2,32,128]{3,2,1,0:T(8,128)(2,1)S(1)} %collective-permute-done.3.oth_ref, f32[1536,128]{1,0:T(8,128)S(1)} %broadcast_in_dim.10.gain_ref, ...), custom_call_target="tpu_custom_call" | custom-call | flops 1610612736 | bytes 4194304 | tf_op jit(solution)/shard_map/pallas_call | solution.py:198
  95.8 1.9 %collective-permute-start.7 = (bf16[48,2,32,128]{3,2,1,0:T(8,128)(2,1)S(1)}, bf16[48,2,32,128]{3,2,1,0:T(8,128)(2,1)S(1)}, u32[]{:S(2)}, u32[]{:S(2)}) collective-permute-start(bf16[48,2,32,128]{3,2,1,0:T(8,128)(2,1)S(1)} %get-tuple-element.16), channel_id=1, source_target_pairs={{0,1},{1,0},{2,3},{3,2},{4,5},{5,4},{6,7},{7,6},{8,9},{9,8},{10,11... | collective-permute-start | bytes 2359304 | tf_op jit(solution)/shard_map/ppermute | solution.py:282
  97.8 2.3 %collective-permute-done.7 = bf16[48,2,32,128]{3,2,1,0:T(8,128)(2,1)S(1)} collective-permute-done((bf16[48,2,32,128]{3,2,1,0:T(8,128)(2,1)S(1)}, bf16[48,2,32,128]{3,2,1,0:T(8,128)(2,1)S(1)}, u32[]{:S(2)}, u32[]{:S(2)}) %collective-permute-start.7) | collective-permute-done | bytes 786464 | tf_op jit(solution)/shard_map/ppermute | solution.py:282
  100.0 0.3 add_convert_fusion
  100.3 39.8 %all_to_all.10.got_ref = bf16[48,2,32,128]{3,2,1,0:T(8,128)(2,1)S(1)} all-to-all(bf16[48,2,32,128]{3,2,1,0:T(8,128)(2,1)S(1)} %add_convert_fusion), channel_id=1, replica_groups=mesh['y'=4,'z'=12,'x'=4,'h'=2,'c'=2] {'y','z'}, dimensions={0} | all-to-all | bytes 1572864 | tf_op jit(solution)/shard_map/all_to_all | solution.py:283
  140.1 0.7 shard_map.97
  140.8 10.1 %collective-permute-start.8 = (bf16[3,32,128]{2,1,0:T(8,128)(2,1)S(1)}, bf16[3,32,128]{2,1,0:T(8,128)(2,1)S(1)}, u32[]{:S(2)}, u32[]{:S(2)}) collective-permute-start(bf16[3,32,128]{2,1,0:T(8,128)(2,1)S(1)} %get-tuple-element.20), channel_id=1, source_target_pairs={{0,1},{1,2},{2,3},{3,4},{4,5},{5,6},{6,7},{7,8},{8,9},{9,10},{10,1... | collective-permute-start | bytes 73736 | tf_op jit(solution)/shard_map/ppermute | solution.py:24
  151.0 1.9 %collective-permute-start.9 = (bf16[3,32,128]{2,1,0:T(8,128)(2,1)S(1)}, bf16[3,32,128]{2,1,0:T(8,128)(2,1)S(1)}, u32[]{:S(2)}, u32[]{:S(2)}) collective-permute-start(bf16[3,32,128]{2,1,0:T(8,128)(2,1)S(1)} %get-tuple-element.21), channel_id=1, source_target_pairs={{1,0},{2,1},{3,2},{4,3},{5,4},{6,5},{7,6},{8,7},{9,8},{10,9},{11,1... | collective-permute-start | bytes 73736 | tf_op jit(solution)/shard_map/ppermute | solution.py:24
  152.9 0.0 collective-permute-done.8.low_ref
  152.9 8.0 %collective-permute-done.9.high_ref = bf16[3,32,128]{2,1,0:T(8,128)(2,1)S(1)} collective-permute-done((bf16[3,32,128]{2,1,0:T(8,128)(2,1)S(1)}, bf16[3,32,128]{2,1,0:T(8,128)(2,1)S(1)}, u32[]{:S(2)}, u32[]{:S(2)}) %collective-permute-start.9) | collective-permute-done | bytes 24608 | tf_op jit(solution)/shard_map/ppermute | solution.py:24
  160.9 1.3 shard_map.98
  (2 shorter events, 0.0 us)
Async XLA Ops:
  0.6 17.4 %copy-start = (f32[1536]{0:T(1024)S(1)}, f32[1536]{0:T(1024)}, u32[]{:S(2)}) copy-start(f32[1536]{0:T(1024)} %param.12) | copy-start | bytes 18436
  0.6 6.9 %copy-start.3 = (s32[8,128]{1,0:T(8,128)S(1)}, s32[8,128]{1,0:T(8,128)}, u32[]{:S(2)}) copy-start(s32[8,128]{1,0:T(8,128)} %tok_ref.1) | copy-start | bytes 12292
  0.7 17.4 %copy-start.4 = (bf16[7,7,32]{2,1,0:T(8,128)(2,1)S(1)}, bf16[7,7,32]{2,1,0:T(8,128)(2,1)}, u32[]{:S(2)}) copy-start(bf16[7,7,32]{2,1,0:T(8,128)(2,1)} %param.10) | copy-start | bytes 9412
  0.7 18.0 %copy-start.1 = (bf16[8,128,32]{1,2,0:T(8,128)(2,1)S(1)}, bf16[8,128,32]{1,2,0:T(8,128)(2,1)}, u32[]{:S(2)}) copy-start(bf16[8,128,32]{1,2,0:T(8,128)(2,1)} %param.15) | copy-start | bytes 196612
  0.7 18.0 %copy-start.2 = (bf16[256,32]{0,1:T(8,128)(2,1)S(1)}, bf16[256,32]{0,1:T(8,128)(2,1)}, u32[]{:S(2)}) copy-start(bf16[256,32]{0,1:T(8,128)(2,1)} %param.9) | copy-start | bytes 49156
  1.9 89.5 %copy-start.5 = (f32[1536]{0:T(1024)S(1)}, f32[1536]{0:T(1024)}, u32[]{:S(2)}) copy-start(f32[1536]{0:T(1024)} %param.11) | copy-start | bytes 18436
  3.0 17.4 %collective-permute-start.2 = (bf16[2,128,1536]{2,1,0:T(8,128)(2,1)S(1)}, bf16[2,128,1536]{2,1,0:T(8,128)(2,1)S(1)}, u32[]{:S(2)}, u32[]{:S(2)}) collective-permute-start(bf16[2,128,1536]{2,1,0:T(8,128)(2,1)S(1)} %pad_maximum_fusion), channel_id=1, source_target_pairs={{0,0},{16,1},{1,16},{17,17},{32,32},{48,33},{33,48},{49,49},{64,64... | collective-permute-start | bytes 2359304 | tf_op jit(solution)/shard_map/ppermute | solution.py:217
  7.6 10.7 %collective-permute-start.1 = (s32[3,128]{1,0:T(4,128)S(1)}, s32[3,128]{1,0:T(4,128)S(1)}, u32[]{:S(2)}, u32[]{:S(2)}) collective-permute-start(s32[3,128]{1,0:T(4,128)S(1)} %get-tuple-element.22), channel_id=1, source_target_pairs={{1,0},{2,1},{3,2},{4,3},{5,4},{6,5},{7,6},{8,7},{9,8},{10,9},{11,1... | collective-permute-start | bytes 4616 | tf_op jit(solution)/shard_map/ppermute | solution.py:24
  9.5 9.2 %collective-permute-start = (s32[3,128]{1,0:T(4,128)S(1)}, s32[3,128]{1,0:T(4,128)S(1)}, u32[]{:S(2)}, u32[]{:S(2)}) collective-permute-start(s32[3,128]{1,0:T(4,128)S(1)} %get-tuple-element.23), channel_id=1, source_target_pairs={{0,1},{1,2},{2,3},{3,4},{4,5},{5,6},{6,7},{7,8},{8,9},{9,10},{10,1... | collective-permute-start | bytes 4616 | tf_op jit(solution)/shard_map/ppermute | solution.py:24
  20.4 45.2 %all-to-all-start = ((bf16[48,2,32,128]{3,2,1,0:T(8,128)(2,1)}), bf16[48,2,32,128]{3,2,1,0:T(8,128)(2,1)S(1)}, u32[]{:S(2)}, u32[]{:S(2)}) async-start(bf16[48,2,32,128]{3,2,1,0:T(8,128)(2,1)} %get-tuple-element.13), calls=%async_computation | async-start | bytes 1572864 | tf_op jit(solution)/shard_map/all_to_all | solution.py:261
  37.8 36.4 %collective-permute-start.6 = (bf16[2,128,1536]{2,1,0:T(8,128)(2,1)S(1)}, bf16[2,128,1536]{2,1,0:T(8,128)(2,1)S(1)}, u32[]{:S(2)}, u32[]{:S(2)}) collective-permute-start(bf16[2,128,1536]{2,1,0:T(8,128)(2,1)S(1)} %collective-permute-done.2.w0_ref), channel_id=1, source_target_pairs={{578,0},{579,1},{0,192},{1,193},{192,384},{193,385},{384,576},{385... | collective-permute-start | bytes 2359304 | tf_op jit(solution)/shard_map/ppermute | solution.py:229
  39.7 37.1 %collective-permute-start.5 = (bf16[2,128,1536]{2,1,0:T(8,128)(2,1)S(1)}, bf16[2,128,1536]{2,1,0:T(8,128)(2,1)S(1)}, u32[]{:S(2)}, u32[]{:S(2)}) collective-permute-start(bf16[2,128,1536]{2,1,0:T(8,128)(2,1)S(1)} %collective-permute-done.2.w0_ref), channel_id=1, source_target_pairs={{192,0},{193,1},{384,192},{385,193},{576,384},{577,385},{2,576},{3... | collective-permute-start | bytes 2359304 | tf_op jit(solution)/shard_map/ppermute | solution.py:229
  43.1 48.2 %collective-permute-start.4 = (bf16[2,128,1536]{2,1,0:T(8,128)(2,1)S(1)}, bf16[2,128,1536]{2,1,0:T(8,128)(2,1)}, u32[]{:S(2)}, u32[]{:S(2)}) collective-permute-start(bf16[2,128,1536]{2,1,0:T(8,128)(2,1)S(1)} %collective-permute-done.2.w0_ref), channel_id=1, source_target_pairs={{384,0},{387,1},{576,192},{579,193},{2,384},{1,385},{194,576},{193... | collective-permute-start | bytes 2359304 | tf_op jit(solution)/shard_map/ppermute | solution.py:229
  65.6 25.8 %collective-permute-start.3 = (bf16[48,2,32,128]{3,2,1,0:T(8,128)(2,1)S(1)}, bf16[48,2,32,128]{3,2,1,0:T(8,128)(2,1)S(1)}, u32[]{:S(2)}, u32[]{:S(2)}) collective-permute-start(bf16[48,2,32,128]{3,2,1,0:T(8,128)(2,1)S(1)} %all-to-all-done.own_ref), channel_id=1, source_target_pairs={{0,1},{1,0},{2,3},{3,2},{4,5},{5,4},{6,7},{7,6},{8,9},{9,8},{10,11... | collective-permute-start | bytes 2359304 | tf_op jit(solution)/shard_map/ppermute | solution.py:262
  95.8 4.2 %collective-permute-start.7 = (bf16[48,2,32,128]{3,2,1,0:T(8,128)(2,1)S(1)}, bf16[48,2,32,128]{3,2,1,0:T(8,128)(2,1)S(1)}, u32[]{:S(2)}, u32[]{:S(2)}) collective-permute-start(bf16[48,2,32,128]{3,2,1,0:T(8,128)(2,1)S(1)} %get-tuple-element.16), channel_id=1, source_target_pairs={{0,1},{1,0},{2,3},{3,2},{4,5},{5,4},{6,7},{7,6},{8,9},{9,8},{10,11... | collective-permute-start | bytes 2359304 | tf_op jit(solution)/shard_map/ppermute | solution.py:282
  140.8 12.1 %collective-permute-start.8 = (bf16[3,32,128]{2,1,0:T(8,128)(2,1)S(1)}, bf16[3,32,128]{2,1,0:T(8,128)(2,1)S(1)}, u32[]{:S(2)}, u32[]{:S(2)}) collective-permute-start(bf16[3,32,128]{2,1,0:T(8,128)(2,1)S(1)} %get-tuple-element.20), channel_id=1, source_target_pairs={{0,1},{1,2},{2,3},{3,4},{4,5},{5,6},{6,7},{7,8},{8,9},{9,10},{10,1... | collective-permute-start | bytes 73736 | tf_op jit(solution)/shard_map/ppermute | solution.py:24
  151.0 10.0 %collective-permute-start.9 = (bf16[3,32,128]{2,1,0:T(8,128)(2,1)S(1)}, bf16[3,32,128]{2,1,0:T(8,128)(2,1)S(1)}, u32[]{:S(2)}, u32[]{:S(2)}) collective-permute-start(bf16[3,32,128]{2,1,0:T(8,128)(2,1)S(1)} %get-tuple-element.21), channel_id=1, source_target_pairs={{1,0},{2,1},{3,2},{4,3},{5,4},{6,5},{7,6},{8,7},{9,8},{10,9},{11,1... | collective-permute-start | bytes 73736 | tf_op jit(solution)/shard_map/ppermute | solution.py:24

commit v3 on v2

--- a/solution.py
+++ b/solution.py
@@ -1,4 +1,5 @@
 import functools
+import itertools
 import math
 
 import jax
@@ -79,18 +80,18 @@
 
 
 def middle_kernel(
-    own_ref, oth_ref, gain_ref, w0_ref, w1_ref, w2_ref, w3_ref,
+    own_ref, oth_ref, gain_ref, i0_ref, i1_ref, i2_ref, i3_ref, o0_ref, o1_ref, o2_ref, o3_ref,
     keep_ref, sib_ref,
     win, wout, scaled, gmix, normed, grads, act, gpre, sem,
 ):
     blocks, _, chans, cols = own_ref.shape
     width = blocks * chans
-    hid = w0_ref.shape[1]
-    pieces = [(ref.at[0], ref.at[1]) for ref in (w0_ref, w1_ref, w2_ref, w3_ref)]
+    hid = o0_ref.shape[0]
+    pieces = [(i0_ref, o0_ref), (i1_ref, o1_ref), (i2_ref, o2_ref), (i3_ref, o3_ref)]
     copies = []
     for i, (a, b) in enumerate(pieces):
         spot = pl.ds(i * hid, hid)
-        copies.append(pltpu.make_async_copy(a, win.at[spot], sem.at[2 * i]))
+        copies.append(pltpu.make_async_copy(a, win.at[:, spot], sem.at[2 * i]))
         copies.append(pltpu.make_async_copy(b, wout.at[spot], sem.at[2 * i + 1]))
     for copy in copies:
         copy.start()
@@ -122,9 +123,10 @@
     for copy in copies:
         copy.wait()
 
+    turned = (((0,), (0,)), ((), ()))
     for i in range(len(pieces)):
         spot = pl.ds(i * hid, hid)
-        pre = jnp.dot(win[spot, :], scaled[...], preferred_element_type=F32)
+        pre = lax.dot_general(win[:, spot], scaled[...], turned, preferred_element_type=F32)
         gact = jnp.dot(wout[spot, :], gmix[...], preferred_element_type=F32)
         cube = pre * pre
         tanh = jnp.tanh(ROOT * (pre + 0.044715 * (cube * pre)))
@@ -136,11 +138,10 @@
     group = 256
     per = group // chans
     sums = [jnp.zeros((1, 2 * cols), F32), jnp.zeros((1, 2 * cols), F32)]
-    turned = (((0,), (0,)), ((), ()))
     for j in range(width // group):
         spot = pl.ds(j * group, group)
         gain = gain_ref[spot, :]
-        part = lax.dot_general(win[:, spot], gpre[...], turned, preferred_element_type=F32)
+        part = jnp.dot(win[spot, :], gpre[...], preferred_element_type=F32)
         part = part * jnp.concatenate([gain, gain], axis=1)
         grads[spot, :] = part
         sums[0] = sums[0] + jnp.sum(part, axis=0, keepdims=True)
@@ -206,29 +207,28 @@
     )(*args)
 
 
-def pair_weights(w_in, w_out):
-    both = jnp.stack([w_in.T, w_out])
-    nz, nh, ny = lax.axis_size("z"), lax.axis_size("h"), lax.axis_size("y")
+def shifted(shard):
+    ny, nz, nx, nh, nc = (lax.axis_size(a) for a in AXES)
+    count = ny * nh
+
+    def place(y, z, x, h, c):
+        return (((y * nz + z) * nx + x) * nh + h) * nc + c
+
     pairs = []
-    for z in range(nz):
-        for c in range(2):
-            other = (z, c) if z % 2 == c else (z ^ 1, 1 - c)
-            pairs.append((other[0] * 2 + other[1], z * 2 + c))
-    return lax.ppermute(both, ("z", "c"), pairs)
-
-
-def ring_weights(both):
-    nh, ny = lax.axis_size("h"), lax.axis_size("y")
-    ring = [y * nh + h for h in range(nh) for y in range(ny)]
-    count = len(ring)
-
-    def from_steps(steps):
-        pairs = [
-            (ring[(i + steps[c]) % count] * 2 + c, ring[i] * 2 + c) for i in range(count) for c in range(2)
-        ]
-        return lax.ppermute(both, ("y", "h", "c"), pairs)
-
-    return both, from_steps((2, -2)), from_steps((1, 1)), from_steps((-1, -1))
+    for y, z, x, h, c in itertools.product(*[range(n) for n in (ny, nz, nx, nh, nc)]):
+        turn = x % ny
+        if 2 * turn == ny and c:
+            turn = -turn
+        spot = (h * ny + y + turn) % count
+        other = (z, c) if z % 2 == c else (z ^ 1, 1 - c)
+        pairs.append((place(spot % ny, other[0], x, spot // ny, other[1]), place(y, z, x, h, c)))
+    return lax.ppermute(shard, AXES, pairs)
+
+
+def gathered(shard):
+    nx = lax.axis_size("x")
+    others = [lax.ppermute(shard, "x", [((i + k) % nx, i) for i in range(nx)]) for k in (2, 1, 3)]
+    return [shard, *others]
 
 
 def on_device(
@@ -242,7 +242,7 @@
     hid = w_out.shape[0] * lax.axis_size("y")
     swap = [(0, 1), (1, 0)]
 
-    both = pair_weights(w_in, w_out)
+    w_in = shifted(w_in)
     low, high = edges(floor_tokens[:3] + 1, floor_tokens[rows - 3 :] + 1)
     taps = depth_kernel.reshape(49, chans).T
     scale = lax.dynamic_slice_in_dim(layer_scale, lax.axis_index(CHAN) * chans, chans, 0)[:, None]
@@ -256,17 +256,21 @@
         [(tile, BF16), (packed, BF16)],
         (floor_tokens, low, high, token_table.T, taps, scale, grad_local),
     )
-    send, both = lax.optimization_barrier((send, both))
-    weights = ring_weights(both)
+    send, w_in = lax.optimization_barrier((send, w_in))
+    w_out = shifted(w_out)
+    weights = gathered(w_in)
+    w_out, weights[1] = lax.optimization_barrier((w_out, weights[1]))
+    weights = weights + gathered(w_out)
     own = lax.all_to_all(send, CHAN, 0, 0, tiled=True)
+    own, *weights = lax.optimization_barrier((own, *weights))
     oth = lax.ppermute(own, "c", swap)
     keep, sib = call(
         middle_kernel,
         [(packed, F32), (packed, BF16)],
         (own, oth, gain, *weights),
-        [VMEM] * 3 + [ANY] * 4,
+        [VMEM] * 3 + [ANY] * 8,
         [
-            pltpu.VMEM((hid, width), BF16),
+            pltpu.VMEM((width, hid), BF16),
             pltpu.VMEM((hid, width), BF16),
             pltpu.VMEM((width, 2 * cols), BF16),
             pltpu.VMEM((width, 2 * cols), BF16),

time: 163 us -> 208 us (1.28)
  starting transfers between devices: 62.1 us -> 129 us
  waiting for transfers between devices: 48.4 us -> 19.3 us
  local copies, waits for them, and re-layouts: 1.77 us -> 7.01 us
    ppermute x4 -> x8, starting transfers between devices: 11.8 us -> 77.1 us  [the longest x6 66.6 us: gathered(): lax.ppermute(shard, 'x', [((i + k) % nx, i) for i in range(nx)])]
    all_to_all x1, waiting for transfers between devices: 20.5 us -> 0.01 us  [on_device(): own = lax.all_to_all(send, CHAN, 0, 0, tiled=True)]
    ppermute x4 -> x8, waiting for transfers between devices: 17.2 us -> 7.45 us  [the longest x6 7.45 us: gathered(): lax.ppermute(shard, 'x', [((i + k) % nx, i) for i in range(nx)])]
    unnamed x13 -> x22, local copies, waits for them, and re-layouts: 1.24 us -> 5.77 us
  transfers between devices with their start and end apart: 11 -> 15, of which waited for: 6 -> 6; matrix products, arithmetic and copies ran while one was open for 0% -> 1% of each run, Pallas kernels for 1% -> 1%
where the time goes in v3:
time: 208 us; the launch traced here: 207 us
  starting transfers between devices  129 us (62%)
  blocking collectives  41.5 us (20%)
  waiting for transfers between devices  19.3 us (9%)
  Pallas kernels  7.97 us (4%)
  local copies, waits for them, and re-layouts  7.01 us (3%)
    ppermute x6, starting transfers between devices, gathered(): lax.ppermute(shard, 'x', [((i + k) % nx, i) for i in range(nx)])  66.6 us
    all_to_all x1, blocking collectives, on_device(): got = lax.all_to_all(part, CHAN, 0, 0, tiled=True)  41.5 us
    ppermute x2, starting transfers between devices, edges(): lax.ppermute(high_side, SPACE, forward)  18.9 us
    all_to_all x1, starting transfers between devices, on_device(): own = lax.all_to_all(send, CHAN, 0, 0, tiled=True)  17.4 us
    ppermute x2, starting transfers between devices, shifted(): return lax.ppermute(shard, AXES, pairs)  10.5 us
    ppermute x1, starting transfers between devices, on_device(): oth = lax.ppermute(own, 'c', swap)  10.1 us
    ppermute x2, waiting for transfers between devices, edges(): lax.ppermute(low_side, SPACE, backward)  8.02 us
    pallas_call x4, Pallas kernels, call(): pl.pallas_call(body, out_shape=outs, in_specs=specs or [VMEM] * len(args)...  7.97 us
  transfers between devices with their start and end apart: 15, of which 6 were waited for; matrix products, arithmetic and copies ran while one was open for 1% of the time, Pallas kernels for 1%

profile of v3, /device:TPU:57, one launch (start us, length us, event | category | flops | bytes accessed | tf_op | source)
XLA Modules:
  0.0 207.2 jit_solution(12141402376888145661)
XLA Ops:
  0.6 0.0 copy-start
  0.6 0.0 copy-start.9
  0.7 4.7 %collective-permute-start.2 = (bf16[1536,128]{1,0:T(8,128)(2,1)}, bf16[1536,128]{1,0:T(8,128)(2,1)S(1)}, u32[]{:S(2)}, u32[]{:S(2)}) collective-permute-start(bf16[1536,128]{1,0:T(8,128)(2,1)} %param.13), channel_id=1, source_target_pairs={{0,0},{16,1},{2,2},{18,3},{196,4},{212,5},{198,6},{214,7},{392,8},... | collective-permute-start | bytes 1179656 | tf_op jit(solution)/shard_map/ppermute | solution.py:225
  5.4 0.8 slice_add_fusion
  6.1 1.9 collective-permute-start.1
  8.0 8.4 %collective-permute-start = (s32[3,128]{1,0:T(4,128)S(1)}, s32[3,128]{1,0:T(4,128)S(1)}, u32[]{:S(2)}, u32[]{:S(2)}) collective-permute-start(s32[3,128]{1,0:T(4,128)S(1)} %get-tuple-element.45), channel_id=1, source_target_pairs={{0,1},{1,2},{2,3},{3,4},{4,5},{5,6},{6,7},{7,8},{8,9},{9,10},{10,1... | collective-permute-start | bytes 4616 | tf_op jit(solution)/shard_map/ppermute | solution.py:25
  16.5 0.0 copy-done
  16.5 0.1 dynamic-slice_bitcast_fusion
  16.6 0.7 reshape.8
  17.3 0.1 copy.13
  17.4 0.1 copy.14.scale_ref
  17.5 0.0 collective-permute-done.1.high_ref
  17.5 0.0 collective-permute-done.low_ref
  17.5 0.0 copy-start.1
  17.5 0.8 copy-done.1
  18.4 0.0 copy-start.3
  18.4 0.7 copy-done.3
  19.1 0.0 copy-start.4
  19.1 0.7 copy-done.4
  19.8 0.0 copy-start.10
  19.8 1.7 shard_map.95
  21.5 0.0 collective-permute-done.2.i0_ref
  21.5 17.4 %all-to-all-start = ((bf16[48,2,32,128]{3,2,1,0:T(8,128)(2,1)}), bf16[48,2,32,128]{3,2,1,0:T(8,128)(2,1)S(1)}, u32[]{:S(2)}, u32[]{:S(2)}) async-start(bf16[48,2,32,128]{3,2,1,0:T(8,128)(2,1)} %get-tuple-element.24), calls=%async_computation | async-start | bytes 1572864 | tf_op jit(solution)/shard_map/all_to_all | solution.py:264
  38.9 0.0 copy-done.10
  38.9 5.8 %collective-permute-start.3 = (bf16[128,1536]{1,0:T(8,128)(2,1)S(1)}, bf16[128,1536]{1,0:T(8,128)(2,1)S(1)}, u32[]{:S(2)}, u32[]{:S(2)}) collective-permute-start(bf16[128,1536]{1,0:T(8,128)(2,1)S(1)} %copy-done.10), channel_id=1, source_target_pairs={{0,0},{16,1},{2,2},{18,3},{196,4},{212,5},{198,6},{214,7},{392,8},... | collective-permute-start | bytes 1179656 | tf_op jit(solution)/shard_map/ppermute | solution.py:225
  44.7 23.0 %collective-permute-start.4 = (bf16[1536,128]{1,0:T(8,128)(2,1)S(1)}, bf16[1536,128]{1,0:T(8,128)(2,1)S(1)}, u32[]{:S(2)}, u32[]{:S(2)}) collective-permute-start(bf16[1536,128]{1,0:T(8,128)(2,1)S(1)} %collective-permute-done.2.i0_ref), channel_id=1, source_target_pairs={{8,0},{12,4},{0,8},{4,12},{9,1},{13,5},{1,9},{5,13},{10,2},{14,6},... | collective-permute-start | bytes 1179656 | tf_op jit(solution)/shard_map/ppermute | solution.py:230
  67.7 3.1 %collective-permute-start.6 = (bf16[1536,128]{1,0:T(8,128)(2,1)S(1)}, bf16[1536,128]{1,0:T(8,128)(2,1)S(1)}, u32[]{:S(2)}, u32[]{:S(2)}) collective-permute-start(bf16[1536,128]{1,0:T(8,128)(2,1)S(1)} %collective-permute-done.2.i0_ref), channel_id=1, source_target_pairs={{12,0},{0,4},{4,8},{8,12},{13,1},{1,5},{5,9},{9,13},{14,2},{2,6},{... | collective-permute-start | bytes 1179656 | tf_op jit(solution)/shard_map/ppermute | solution.py:230
  70.8 3.4 %collective-permute-start.5 = (bf16[1536,128]{1,0:T(8,128)(2,1)S(1)}, bf16[1536,128]{1,0:T(8,128)(2,1)S(1)}, u32[]{:S(2)}, u32[]{:S(2)}) collective-permute-start(bf16[1536,128]{1,0:T(8,128)(2,1)S(1)} %collective-permute-done.2.i0_ref), channel_id=1, source_target_pairs={{4,0},{8,4},{12,8},{0,12},{5,1},{9,5},{13,9},{1,13},{6,2},{10,6},{... | collective-permute-start | bytes 1179656 | tf_op jit(solution)/shard_map/ppermute | solution.py:230
  74.2 0.0 collective-permute-done.3.o0_ref
  74.2 0.0 collective-permute-done.4.i1_ref
  74.2 5.9 %collective-permute-start.9 = (bf16[128,1536]{1,0:T(8,128)(2,1)S(1)}, bf16[128,1536]{1,0:T(8,128)(2,1)S(1)}, u32[]{:S(2)}, u32[]{:S(2)}) collective-permute-start(bf16[128,1536]{1,0:T(8,128)(2,1)S(1)} %collective-permute-done.3.o0_ref), channel_id=1, source_target_pairs={{12,0},{0,4},{4,8},{8,12},{13,1},{1,5},{5,9},{9,13},{14,2},{2,6},{... | collective-permute-start | bytes 1179656 | tf_op jit(solution)/shard_map/ppermute | solution.py:230
  80.1 28.2 %collective-permute-start.8 = (bf16[128,1536]{1,0:T(8,128)(2,1)S(1)}, bf16[128,1536]{1,0:T(8,128)(2,1)S(1)}, u32[]{:S(2)}, u32[]{:S(2)}) collective-permute-start(bf16[128,1536]{1,0:T(8,128)(2,1)S(1)} %collective-permute-done.3.o0_ref), channel_id=1, source_target_pairs={{4,0},{8,4},{12,8},{0,12},{5,1},{9,5},{13,9},{1,13},{6,2},{10,6},{... | collective-permute-start | bytes 1179656 | tf_op jit(solution)/shard_map/ppermute | solution.py:230
  108.3 3.1 %collective-permute-start.7 = (bf16[128,1536]{1,0:T(8,128)(2,1)S(1)}, bf16[128,1536]{1,0:T(8,128)(2,1)S(1)}, u32[]{:S(2)}, u32[]{:S(2)}) collective-permute-start(bf16[128,1536]{1,0:T(8,128)(2,1)S(1)} %collective-permute-done.3.o0_ref), channel_id=1, source_target_pairs={{8,0},{12,4},{0,8},{4,12},{9,1},{13,5},{1,9},{5,13},{10,2},{14,6},... | collective-permute-start | bytes 1179656 | tf_op jit(solution)/shard_map/ppermute | solution.py:230
  111.4 0.0 collective-permute-done.6.i3_ref
  111.4 0.0 collective-permute-done.5.i2_ref
  111.4 0.1 collective-permute-done.9.o3_ref
  111.5 5.7 %collective-permute-done.8.o2_ref = bf16[128,1536]{1,0:T(8,128)(2,1)S(1)} collective-permute-done((bf16[128,1536]{1,0:T(8,128)(2,1)S(1)}, bf16[128,1536]{1,0:T(8,128)(2,1)S(1)}, u32[]{:S(2)}, u32[]{:S(2)}) %collective-permute-start.8) | collective-permute-done | bytes 393248 | tf_op jit(solution)/shard_map/ppermute | solution.py:230
  117.2 0.0 copy-start.5
  117.2 0.8 copy-done.5
  118.0 1.6 collective-permute-done.7.o1_ref
  119.6 0.0 copy-start.7
  119.6 0.8 copy-done.7
  120.4 0.0 all-to-all-done.own_ref
  120.4 10.1 %collective-permute-start.10 = (bf16[48,2,32,128]{3,2,1,0:T(8,128)(2,1)S(1)}, bf16[48,2,32,128]{3,2,1,0:T(8,128)(2,1)S(1)}, u32[]{:S(2)}, u32[]{:S(2)}) collective-permute-start(bf16[48,2,32,128]{3,2,1,0:T(8,128)(2,1)S(1)} %all-to-all-done.own_ref), channel_id=1, source_target_pairs={{0,1},{1,0},{2,3},{3,2},{4,5},{5,4},{6,7},{7,6},{8,9},{9,8},{10,11... | collective-permute-start | bytes 2359304 | tf_op jit(solution)/shard_map/ppermute | solution.py:266
  130.4 1.9 collective-permute-done.10.oth_ref
  132.3 0.0 copy-done.9
  132.3 0.3 broadcast_in_dim.10.gain_ref
  132.6 0.0 copy-start.6
  132.6 1.0 copy-done.6
  133.6 0.0 copy-start.8
  133.6 1.0 copy-done.8
  134.6 4.2 %shard_map.96 = (f32[48,2,32,128]{3,2,1,0:T(8,128)S(1)}, bf16[48,2,32,128]{3,2,1,0:T(8,128)(2,1)S(1)}) custom-call(bf16[48,2,32,128]{3,2,1,0:T(8,128)(2,1)S(1)} %all-to-all-done.own_ref, bf16[48,2,32,128]{3,2,1,0:T(8,128)(2,1)S(1)} %collective-permute-done.10.oth_ref, f32[1536,128]{1,0:T(8,128)S(1)} %broadcast_in_dim.10.gain_ref, ...), custom_call_target="tpu_custom_call" | custom-call | flops 1610612736 | bytes 4194304 | tf_op jit(solution)/shard_map/pallas_call | solution.py:199
  138.8 2.3 %collective-permute-start.11 = (bf16[48,2,32,128]{3,2,1,0:T(8,128)(2,1)S(1)}, bf16[48,2,32,128]{3,2,1,0:T(8,128)(2,1)S(1)}, u32[]{:S(2)}, u32[]{:S(2)}) collective-permute-start(bf16[48,2,32,128]{3,2,1,0:T(8,128)(2,1)S(1)} %get-tuple-element.38), channel_id=1, source_target_pairs={{0,1},{1,0},{2,3},{3,2},{4,5},{5,4},{6,7},{7,6},{8,9},{9,8},{10,11... | collective-permute-start | bytes 2359304 | tf_op jit(solution)/shard_map/ppermute | solution.py:286
  141.1 1.9 collective-permute-done.11
  143.0 0.3 add_convert_fusion
  143.2 0.0 copy-start.2
  143.2 41.5 %all_to_all.10.got_ref = bf16[48,2,32,128]{3,2,1,0:T(8,128)(2,1)S(1)} all-to-all(bf16[48,2,32,128]{3,2,1,0:T(8,128)(2,1)S(1)} %add_convert_fusion), channel_id=1, replica_groups=mesh['y'=4,'z'=12,'x'=4,'h'=2,'c'=2] {'y','z'}, dimensions={0} | all-to-all | bytes 1572864 | tf_op jit(solution)/shard_map/all_to_all | solution.py:287
  184.8 0.7 shard_map.97
  185.5 10.4 %collective-permute-start.12 = (bf16[3,32,128]{2,1,0:T(8,128)(2,1)S(1)}, bf16[3,32,128]{2,1,0:T(8,128)(2,1)S(1)}, u32[]{:S(2)}, u32[]{:S(2)}) collective-permute-start(bf16[3,32,128]{2,1,0:T(8,128)(2,1)S(1)} %get-tuple-element.42), channel_id=1, source_target_pairs={{0,1},{1,2},{2,3},{3,4},{4,5},{5,6},{6,7},{7,8},{8,9},{9,10},{10,1... | collective-permute-start | bytes 73736 | tf_op jit(solution)/shard_map/ppermute | solution.py:25
  195.9 1.9 collective-permute-start.13
  197.9 0.0 collective-permute-done.12.low_ref
  197.9 8.0 %collective-permute-done.13.high_ref = bf16[3,32,128]{2,1,0:T(8,128)(2,1)S(1)} collective-permute-done((bf16[3,32,128]{2,1,0:T(8,128)(2,1)S(1)}, bf16[3,32,128]{2,1,0:T(8,128)(2,1)S(1)}, u32[]{:S(2)}, u32[]{:S(2)}) %collective-permute-start.13) | collective-permute-done | bytes 24608 | tf_op jit(solution)/shard_map/ppermute | solution.py:25
  205.9 0.0 copy-done.2
  205.9 1.3 shard_map.98
Async XLA Ops:
  0.6 15.9 %copy-start = (f32[1536]{0:T(1024)S(1)}, f32[1536]{0:T(1024)}, u32[]{:S(2)}) copy-start(f32[1536]{0:T(1024)} %param.12) | copy-start | bytes 18436
  0.6 131.7 %copy-start.9 = (f32[1536]{0:T(1024)S(1)}, f32[1536]{0:T(1024)}, u32[]{:S(2)}) copy-start(f32[1536]{0:T(1024)} %param.11) | copy-start | bytes 18436
  0.7 20.9 %collective-permute-start.2 = (bf16[1536,128]{1,0:T(8,128)(2,1)}, bf16[1536,128]{1,0:T(8,128)(2,1)S(1)}, u32[]{:S(2)}, u32[]{:S(2)}) collective-permute-start(bf16[1536,128]{1,0:T(8,128)(2,1)} %param.13), channel_id=1, source_target_pairs={{0,0},{16,1},{2,2},{18,3},{196,4},{212,5},{198,6},{214,7},{392,8},... | collective-permute-start | bytes 1179656 | tf_op jit(solution)/shard_map/ppermute | solution.py:225
  6.1 11.4 %collective-permute-start.1 = (s32[3,128]{1,0:T(4,128)S(1)}, s32[3,128]{1,0:T(4,128)S(1)}, u32[]{:S(2)}, u32[]{:S(2)}) collective-permute-start(s32[3,128]{1,0:T(4,128)S(1)} %get-tuple-element.44), channel_id=1, source_target_pairs={{1,0},{2,1},{3,2},{4,3},{5,4},{6,5},{7,6},{8,7},{9,8},{10,9},{11,1... | collective-permute-start | bytes 4616 | tf_op jit(solution)/shard_map/ppermute | solution.py:25
  8.0 9.5 %collective-permute-start = (s32[3,128]{1,0:T(4,128)S(1)}, s32[3,128]{1,0:T(4,128)S(1)}, u32[]{:S(2)}, u32[]{:S(2)}) collective-permute-start(s32[3,128]{1,0:T(4,128)S(1)} %get-tuple-element.45), channel_id=1, source_target_pairs={{0,1},{1,2},{2,3},{3,4},{4,5},{5,6},{6,7},{7,8},{8,9},{9,10},{10,1... | collective-permute-start | bytes 4616 | tf_op jit(solution)/shard_map/ppermute | solution.py:25
  17.5 0.8 copy-start.1
  18.4 0.7 copy-start.3
  19.1 0.7 copy-start.4
  19.8 19.2 %copy-start.10 = (bf16[128,1536]{1,0:T(8,128)(2,1)S(1)}, bf16[128,1536]{1,0:T(8,128)(2,1)}, u32[]{:S(2)}) copy-start(bf16[128,1536]{1,0:T(8,128)(2,1)} %param.14) | copy-start | bytes 1179652
  21.5 98.9 %all-to-all-start = ((bf16[48,2,32,128]{3,2,1,0:T(8,128)(2,1)}), bf16[48,2,32,128]{3,2,1,0:T(8,128)(2,1)S(1)}, u32[]{:S(2)}, u32[]{:S(2)}) async-start(bf16[48,2,32,128]{3,2,1,0:T(8,128)(2,1)} %get-tuple-element.24), calls=%async_computation | async-start | bytes 1572864 | tf_op jit(solution)/shard_map/all_to_all | solution.py:264
  38.9 35.3 %collective-permute-start.3 = (bf16[128,1536]{1,0:T(8,128)(2,1)S(1)}, bf16[128,1536]{1,0:T(8,128)(2,1)S(1)}, u32[]{:S(2)}, u32[]{:S(2)}) collective-permute-start(bf16[128,1536]{1,0:T(8,128)(2,1)S(1)} %copy-done.10), channel_id=1, source_target_pairs={{0,0},{16,1},{2,2},{18,3},{196,4},{212,5},{198,6},{214,7},{392,8},... | collective-permute-start | bytes 1179656 | tf_op jit(solution)/shard_map/ppermute | solution.py:225
  44.7 29.5 %collective-permute-start.4 = (bf16[1536,128]{1,0:T(8,128)(2,1)S(1)}, bf16[1536,128]{1,0:T(8,128)(2,1)S(1)}, u32[]{:S(2)}, u32[]{:S(2)}) collective-permute-start(bf16[1536,128]{1,0:T(8,128)(2,1)S(1)} %collective-permute-done.2.i0_ref), channel_id=1, source_target_pairs={{8,0},{12,4},{0,8},{4,12},{9,1},{13,5},{1,9},{5,13},{10,2},{14,6},... | collective-permute-start | bytes 1179656 | tf_op jit(solution)/shard_map/ppermute | solution.py:230
  67.7 43.7 %collective-permute-start.6 = (bf16[1536,128]{1,0:T(8,128)(2,1)S(1)}, bf16[1536,128]{1,0:T(8,128)(2,1)S(1)}, u32[]{:S(2)}, u32[]{:S(2)}) collective-permute-start(bf16[1536,128]{1,0:T(8,128)(2,1)S(1)} %collective-permute-done.2.i0_ref), channel_id=1, source_target_pairs={{12,0},{0,4},{4,8},{8,12},{13,1},{1,5},{5,9},{9,13},{14,2},{2,6},{... | collective-permute-start | bytes 1179656 | tf_op jit(solution)/shard_map/ppermute | solution.py:230
  70.8 40.7 %collective-permute-start.5 = (bf16[1536,128]{1,0:T(8,128)(2,1)S(1)}, bf16[1536,128]{1,0:T(8,128)(2,1)S(1)}, u32[]{:S(2)}, u32[]{:S(2)}) collective-permute-start(bf16[1536,128]{1,0:T(8,128)(2,1)S(1)} %collective-permute-done.2.i0_ref), channel_id=1, source_target_pairs={{4,0},{8,4},{12,8},{0,12},{5,1},{9,5},{13,9},{1,13},{6,2},{10,6},{... | collective-permute-start | bytes 1179656 | tf_op jit(solution)/shard_map/ppermute | solution.py:230
  74.2 37.3 %collective-permute-start.9 = (bf16[128,1536]{1,0:T(8,128)(2,1)S(1)}, bf16[128,1536]{1,0:T(8,128)(2,1)S(1)}, u32[]{:S(2)}, u32[]{:S(2)}) collective-permute-start(bf16[128,1536]{1,0:T(8,128)(2,1)S(1)} %collective-permute-done.3.o0_ref), channel_id=1, source_target_pairs={{12,0},{0,4},{4,8},{8,12},{13,1},{1,5},{5,9},{9,13},{14,2},{2,6},{... | collective-permute-start | bytes 1179656 | tf_op jit(solution)/shard_map/ppermute | solution.py:230
  80.1 37.1 %collective-permute-start.8 = (bf16[128,1536]{1,0:T(8,128)(2,1)S(1)}, bf16[128,1536]{1,0:T(8,128)(2,1)S(1)}, u32[]{:S(2)}, u32[]{:S(2)}) collective-permute-start(bf16[128,1536]{1,0:T(8,128)(2,1)S(1)} %collective-permute-done.3.o0_ref), channel_id=1, source_target_pairs={{4,0},{8,4},{12,8},{0,12},{5,1},{9,5},{13,9},{1,13},{6,2},{10,6},{... | collective-permute-start | bytes 1179656 | tf_op jit(solution)/shard_map/ppermute | solution.py:230
  108.3 11.3 %collective-permute-start.7 = (bf16[128,1536]{1,0:T(8,128)(2,1)S(1)}, bf16[128,1536]{1,0:T(8,128)(2,1)S(1)}, u32[]{:S(2)}, u32[]{:S(2)}) collective-permute-start(bf16[128,1536]{1,0:T(8,128)(2,1)S(1)} %collective-permute-done.3.o0_ref), channel_id=1, source_target_pairs={{8,0},{12,4},{0,8},{4,12},{9,1},{13,5},{1,9},{5,13},{10,2},{14,6},... | collective-permute-start | bytes 1179656 | tf_op jit(solution)/shard_map/ppermute | solution.py:230
  117.2 0.8 copy-start.5
  119.6 0.8 copy-start.7
  120.4 11.9 %collective-permute-start.10 = (bf16[48,2,32,128]{3,2,1,0:T(8,128)(2,1)S(1)}, bf16[48,2,32,128]{3,2,1,0:T(8,128)(2,1)S(1)}, u32[]{:S(2)}, u32[]{:S(2)}) collective-permute-start(bf16[48,2,32,128]{3,2,1,0:T(8,128)(2,1)S(1)} %all-to-all-done.own_ref), channel_id=1, source_target_pairs={{0,1},{1,0},{2,3},{3,2},{4,5},{5,4},{6,7},{7,6},{8,9},{9,8},{10,11... | collective-permute-start | bytes 2359304 | tf_op jit(solution)/shard_map/ppermute | solution.py:266
  132.6 1.0 copy-start.6
  133.6 1.0 copy-start.8
  138.8 4.2 %collective-permute-start.11 = (bf16[48,2,32,128]{3,2,1,0:T(8,128)(2,1)S(1)}, bf16[48,2,32,128]{3,2,1,0:T(8,128)(2,1)S(1)}, u32[]{:S(2)}, u32[]{:S(2)}) collective-permute-start(bf16[48,2,32,128]{3,2,1,0:T(8,128)(2,1)S(1)} %get-tuple-element.38), channel_id=1, source_target_pairs={{0,1},{1,0},{2,3},{3,2},{4,5},{5,4},{6,7},{7,6},{8,9},{9,8},{10,11... | collective-permute-start | bytes 2359304 | tf_op jit(solution)/shard_map/ppermute | solution.py:286
  143.2 62.7 %copy-start.2 = (bf16[8,128,32]{1,2,0:T(8,128)(2,1)S(1)}, bf16[8,128,32]{1,2,0:T(8,128)(2,1)}, u32[]{:S(2)}) copy-start(bf16[8,128,32]{1,2,0:T(8,128)(2,1)} %param.15) | copy-start | bytes 196612
  185.5 12.3 %collective-permute-start.12 = (bf16[3,32,128]{2,1,0:T(8,128)(2,1)S(1)}, bf16[3,32,128]{2,1,0:T(8,128)(2,1)S(1)}, u32[]{:S(2)}, u32[]{:S(2)}) collective-permute-start(bf16[3,32,128]{2,1,0:T(8,128)(2,1)S(1)} %get-tuple-element.42), channel_id=1, source_target_pairs={{0,1},{1,2},{2,3},{3,4},{4,5},{5,6},{6,7},{7,8},{8,9},{9,10},{10,1... | collective-permute-start | bytes 73736 | tf_op jit(solution)/shard_map/ppermute | solution.py:25
  195.9 10.0 %collective-permute-start.13 = (bf16[3,32,128]{2,1,0:T(8,128)(2,1)S(1)}, bf16[3,32,128]{2,1,0:T(8,128)(2,1)S(1)}, u32[]{:S(2)}, u32[]{:S(2)}) collective-permute-start(bf16[3,32,128]{2,1,0:T(8,128)(2,1)S(1)} %get-tuple-element.43), channel_id=1, source_target_pairs={{1,0},{2,1},{3,2},{4,3},{5,4},{6,5},{7,6},{8,7},{9,8},{10,9},{11,1... | collective-permute-start | bytes 73736 | tf_op jit(solution)/shard_map/ppermute | solution.py:25

commit v4 on v3

--- a/solution.py
+++ b/solution.py
@@ -217,8 +217,8 @@
     pairs = []
     for y, z, x, h, c in itertools.product(*[range(n) for n in (ny, nz, nx, nh, nc)]):
         turn = x % ny
-        if 2 * turn == ny and c:
-            turn = -turn
+        if 2 * turn > ny or (2 * turn == ny and c):
+            turn -= ny
         spot = (h * ny + y + turn) % count
         other = (z, c) if z % 2 == c else (z ^ 1, 1 - c)
         pairs.append((place(spot % ny, other[0], x, spot // ny, other[1]), place(y, z, x, h, c)))

time: 208 us -> 174 us (0.84)
  starting transfers between devices: 129 us -> 84 us
  waiting for transfers between devices: 19.3 us -> 31 us
    ppermute x6, starting transfers between devices: 66.6 us -> 27.4 us  [gathered(): lax.ppermute(shard, 'x', [((i + k) % nx, i) for i in range(nx)])]
    ppermute x2, waiting for transfers between devices: 0.01 us -> 14.2 us  [shifted(): return lax.ppermute(shard, AXES, pairs)]
    ppermute x1, starting transfers between devices: 10.1 us -> 1.91 us  [on_device(): oth = lax.ppermute(own, 'c', swap)]
    ppermute x6, waiting for transfers between devices: 7.45 us -> 4.36 us  [gathered(): lax.ppermute(shard, 'x', [((i + k) % nx, i) for i in range(nx)])]
where the time goes in v4:
time: 174 us; the launch traced here: 173 us
  starting transfers between devices  84 us (48%)
  blocking collectives  40.9 us (24%)
  waiting for transfers between devices  31 us (18%)
  Pallas kernels  7.97 us (5%)
  local copies, waits for them, and re-layouts  7.02 us (4%)
    all_to_all x1, blocking collectives, on_device(): got = lax.all_to_all(part, CHAN, 0, 0, tiled=True)  40.9 us
    ppermute x6, starting transfers between devices, gathered(): lax.ppermute(shard, 'x', [((i + k) % nx, i) for i in range(nx)])  27.4 us
    ppermute x2, starting transfers between devices, edges(): lax.ppermute(high_side, SPACE, forward)  20.9 us
    all_to_all x1, starting transfers between devices, on_device(): own = lax.all_to_all(send, CHAN, 0, 0, tiled=True)  17.4 us
    ppermute x2, waiting for transfers between devices, shifted(): return lax.ppermute(shard, AXES, pairs)  14.2 us
    ppermute x2, starting transfers between devices, shifted(): return lax.ppermute(shard, AXES, pairs)  10.5 us
    ppermute x2, waiting for transfers between devices, edges(): lax.ppermute(low_side, SPACE, backward)  8.02 us
    pallas_call x4, Pallas kernels, call(): pl.pallas_call(body, out_shape=outs, in_specs=specs or [VMEM] * len(args)...  7.97 us
  transfers between devices with their start and end apart: 15, of which 6 were waited for; matrix products, arithmetic and copies ran while one was open for 1% of the time, Pallas kernels for 1%

profile of v4, /device:TPU:57, one launch (start us, length us, event | category | flops | bytes accessed | tf_op | source)
XLA Modules:
  0.0 172.8 jit_solution(17532597957553406788)
XLA Ops:
  0.6 0.0 copy-start
  0.6 0.0 copy-start.9
  0.7 4.7 %collective-permute-start.2 = (bf16[1536,128]{1,0:T(8,128)(2,1)}, bf16[1536,128]{1,0:T(8,128)(2,1)S(1)}, u32[]{:S(2)}, u32[]{:S(2)}) collective-permute-start(bf16[1536,128]{1,0:T(8,128)(2,1)} %param.13), channel_id=1, source_target_pairs={{0,0},{16,1},{2,2},{18,3},{196,4},{212,5},{198,6},{214,7},{392,8},... | collective-permute-start | bytes 1179656 | tf_op jit(solution)/shard_map/ppermute | solution.py:225
  5.4 0.8 slice_add_fusion
  6.1 1.9 %collective-permute-start.1 = (s32[3,128]{1,0:T(4,128)S(1)}, s32[3,128]{1,0:T(4,128)S(1)}, u32[]{:S(2)}, u32[]{:S(2)}) collective-permute-start(s32[3,128]{1,0:T(4,128)S(1)} %get-tuple-element.44), channel_id=1, source_target_pairs={{1,0},{2,1},{3,2},{4,3},{5,4},{6,5},{7,6},{8,7},{9,8},{10,9},{11,1... | collective-permute-start | bytes 4616 | tf_op jit(solution)/shard_map/ppermute | solution.py:25
  8.0 8.4 %collective-permute-start = (s32[3,128]{1,0:T(4,128)S(1)}, s32[3,128]{1,0:T(4,128)S(1)}, u32[]{:S(2)}, u32[]{:S(2)}) collective-permute-start(s32[3,128]{1,0:T(4,128)S(1)} %get-tuple-element.45), channel_id=1, source_target_pairs={{0,1},{1,2},{2,3},{3,4},{4,5},{5,6},{6,7},{7,8},{8,9},{9,10},{10,1... | collective-permute-start | bytes 4616 | tf_op jit(solution)/shard_map/ppermute | solution.py:25
  16.5 0.0 copy-done
  16.5 0.1 dynamic-slice_bitcast_fusion
  16.6 0.7 reshape.8
  17.3 0.1 copy.13
  17.4 0.1 copy.14.scale_ref
  17.5 0.0 collective-permute-done.1.high_ref
  17.5 0.0 collective-permute-done.low_ref
  17.5 0.0 copy-start.1
  17.5 0.8 copy-done.1
  18.4 0.0 copy-start.3
  18.4 0.7 copy-done.3
  19.1 0.0 copy-start.4
  19.1 0.7 copy-done.4
  19.8 0.0 copy-start.10
  19.8 1.7 %shard_map.95 = (bf16[8,32,128]{2,1,0:T(8,128)(2,1)S(1)}, bf16[48,2,32,128]{3,2,1,0:T(8,128)(2,1)}) custom-call(s32[8,128]{1,0:T(8,128)S(1)} %copy-done.4, s32[3,128]{1,0:T(4,128)S(1)} %collective-permute-done.low_ref, s32[3,128]{1,0:T(4,128)S(1)} %collective-permute-done.1.high_ref, bf16[32,256]{1,0:T(8,128)(2,1)S(1)} %bitcast.11, ...), custom_call_target="tpu_custom_call" | custom-call | flops 1048576 | bytes 4194304 | tf_op jit(solution)/shard_map/pallas_call | solution.py:199
  21.5 0.0 collective-permute-done.2.i0_ref
  21.5 17.4 %all-to-all-start = ((bf16[48,2,32,128]{3,2,1,0:T(8,128)(2,1)}), bf16[48,2,32,128]{3,2,1,0:T(8,128)(2,1)S(1)}, u32[]{:S(2)}, u32[]{:S(2)}) async-start(bf16[48,2,32,128]{3,2,1,0:T(8,128)(2,1)} %get-tuple-element.24), calls=%async_computation | async-start | bytes 1572864 | tf_op jit(solution)/shard_map/all_to_all | solution.py:264
  38.9 0.0 copy-done.10
  38.9 5.8 %collective-permute-start.3 = (bf16[128,1536]{1,0:T(8,128)(2,1)S(1)}, bf16[128,1536]{1,0:T(8,128)(2,1)S(1)}, u32[]{:S(2)}, u32[]{:S(2)}) collective-permute-start(bf16[128,1536]{1,0:T(8,128)(2,1)S(1)} %copy-done.10), channel_id=1, source_target_pairs={{0,0},{16,1},{2,2},{18,3},{196,4},{212,5},{198,6},{214,7},{392,8},... | collective-permute-start | bytes 1179656 | tf_op jit(solution)/shard_map/ppermute | solution.py:225
  44.7 5.4 %collective-permute-start.4 = (bf16[1536,128]{1,0:T(8,128)(2,1)S(1)}, bf16[1536,128]{1,0:T(8,128)(2,1)S(1)}, u32[]{:S(2)}, u32[]{:S(2)}) collective-permute-start(bf16[1536,128]{1,0:T(8,128)(2,1)S(1)} %collective-permute-done.2.i0_ref), channel_id=1, source_target_pairs={{8,0},{12,4},{0,8},{4,12},{9,1},{13,5},{1,9},{5,13},{10,2},{14,6},... | collective-permute-start | bytes 1179656 | tf_op jit(solution)/shard_map/ppermute | solution.py:230
  50.1 3.9 %collective-permute-start.6 = (bf16[1536,128]{1,0:T(8,128)(2,1)S(1)}, bf16[1536,128]{1,0:T(8,128)(2,1)S(1)}, u32[]{:S(2)}, u32[]{:S(2)}) collective-permute-start(bf16[1536,128]{1,0:T(8,128)(2,1)S(1)} %collective-permute-done.2.i0_ref), channel_id=1, source_target_pairs={{12,0},{0,4},{4,8},{8,12},{13,1},{1,5},{5,9},{9,13},{14,2},{2,6},{... | collective-permute-start | bytes 1179656 | tf_op jit(solution)/shard_map/ppermute | solution.py:230
  54.1 2.6 %collective-permute-start.5 = (bf16[1536,128]{1,0:T(8,128)(2,1)S(1)}, bf16[1536,128]{1,0:T(8,128)(2,1)S(1)}, u32[]{:S(2)}, u32[]{:S(2)}) collective-permute-start(bf16[1536,128]{1,0:T(8,128)(2,1)S(1)} %collective-permute-done.2.i0_ref), channel_id=1, source_target_pairs={{4,0},{8,4},{12,8},{0,12},{5,1},{9,5},{13,9},{1,13},{6,2},{10,6},{... | collective-permute-start | bytes 1179656 | tf_op jit(solution)/shard_map/ppermute | solution.py:230
  56.6 14.2 %collective-permute-done.3.o0_ref = bf16[128,1536]{1,0:T(8,128)(2,1)S(1)} collective-permute-done((bf16[128,1536]{1,0:T(8,128)(2,1)S(1)}, bf16[128,1536]{1,0:T(8,128)(2,1)S(1)}, u32[]{:S(2)}, u32[]{:S(2)}) %collective-permute-start.3) | collective-permute-done | bytes 393248 | tf_op jit(solution)/shard_map/ppermute | solution.py:225
  70.9 0.0 collective-permute-done.4.i1_ref
  70.9 2.7 %collective-permute-start.9 = (bf16[128,1536]{1,0:T(8,128)(2,1)S(1)}, bf16[128,1536]{1,0:T(8,128)(2,1)S(1)}, u32[]{:S(2)}, u32[]{:S(2)}) collective-permute-start(bf16[128,1536]{1,0:T(8,128)(2,1)S(1)} %collective-permute-done.3.o0_ref), channel_id=1, source_target_pairs={{12,0},{0,4},{4,8},{8,12},{13,1},{1,5},{5,9},{9,13},{14,2},{2,6},{... | collective-permute-start | bytes 1179656 | tf_op jit(solution)/shard_map/ppermute | solution.py:230
  73.6 3.8 %collective-permute-start.8 = (bf16[128,1536]{1,0:T(8,128)(2,1)S(1)}, bf16[128,1536]{1,0:T(8,128)(2,1)S(1)}, u32[]{:S(2)}, u32[]{:S(2)}) collective-permute-start(bf16[128,1536]{1,0:T(8,128)(2,1)S(1)} %collective-permute-done.3.o0_ref), channel_id=1, source_target_pairs={{4,0},{8,4},{12,8},{0,12},{5,1},{9,5},{13,9},{1,13},{6,2},{10,6},{... | collective-permute-start | bytes 1179656 | tf_op jit(solution)/shard_map/ppermute | solution.py:230
  77.4 9.1 %collective-permute-start.7 = (bf16[128,1536]{1,0:T(8,128)(2,1)S(1)}, bf16[128,1536]{1,0:T(8,128)(2,1)S(1)}, u32[]{:S(2)}, u32[]{:S(2)}) collective-permute-start(bf16[128,1536]{1,0:T(8,128)(2,1)S(1)} %collective-permute-done.3.o0_ref), channel_id=1, source_target_pairs={{8,0},{12,4},{0,8},{4,12},{9,1},{13,5},{1,9},{5,13},{10,2},{14,6},... | collective-permute-start | bytes 1179656 | tf_op jit(solution)/shard_map/ppermute | solution.py:230
  86.5 0.0 collective-permute-done.6.i3_ref
  86.5 0.0 collective-permute-done.5.i2_ref
  86.5 0.0 collective-permute-done.9.o3_ref
  86.5 1.4 collective-permute-done.8.o2_ref
  87.9 0.0 copy-start.5
  87.9 0.8 copy-done.5
  88.7 2.9 %collective-permute-done.7.o1_ref = bf16[128,1536]{1,0:T(8,128)(2,1)S(1)} collective-permute-done((bf16[128,1536]{1,0:T(8,128)(2,1)S(1)}, bf16[128,1536]{1,0:T(8,128)(2,1)S(1)}, u32[]{:S(2)}, u32[]{:S(2)}) %collective-permute-start.7) | collective-permute-done | bytes 393248 | tf_op jit(solution)/shard_map/ppermute | solution.py:230
  91.6 0.0 copy-start.7
  91.6 0.8 copy-done.7
  92.4 0.0 all-to-all-done.own_ref
  92.4 1.9 %collective-permute-start.10 = (bf16[48,2,32,128]{3,2,1,0:T(8,128)(2,1)S(1)}, bf16[48,2,32,128]{3,2,1,0:T(8,128)(2,1)S(1)}, u32[]{:S(2)}, u32[]{:S(2)}) collective-permute-start(bf16[48,2,32,128]{3,2,1,0:T(8,128)(2,1)S(1)} %all-to-all-done.own_ref), channel_id=1, source_target_pairs={{0,1},{1,0},{2,3},{3,2},{4,5},{5,4},{6,7},{7,6},{8,9},{9,8},{10,11... | collective-permute-start | bytes 2359304 | tf_op jit(solution)/shard_map/ppermute | solution.py:266
  94.3 2.3 %collective-permute-done.10.oth_ref = bf16[48,2,32,128]{3,2,1,0:T(8,128)(2,1)S(1)} collective-permute-done((bf16[48,2,32,128]{3,2,1,0:T(8,128)(2,1)S(1)}, bf16[48,2,32,128]{3,2,1,0:T(8,128)(2,1)S(1)}, u32[]{:S(2)}, u32[]{:S(2)}) %collective-permute-start.10) | collective-permute-done | bytes 786464 | tf_op jit(solution)/shard_map/ppermute | solution.py:266
  96.5 0.0 copy-done.9
  96.5 0.3 broadcast_in_dim.10.gain_ref
  96.8 0.0 copy-start.6
  96.8 1.0 copy-done.6
  97.8 0.0 copy-start.8
  97.8 1.0 copy-done.8
  98.8 4.2 %shard_map.96 = (f32[48,2,32,128]{3,2,1,0:T(8,128)S(1)}, bf16[48,2,32,128]{3,2,1,0:T(8,128)(2,1)S(1)}) custom-call(bf16[48,2,32,128]{3,2,1,0:T(8,128)(2,1)S(1)} %all-to-all-done.own_ref, bf16[48,2,32,128]{3,2,1,0:T(8,128)(2,1)S(1)} %collective-permute-done.10.oth_ref, f32[1536,128]{1,0:T(8,128)S(1)} %broadcast_in_dim.10.gain_ref, ...), custom_call_target="tpu_custom_call" | custom-call | flops 1610612736 | bytes 4194304 | tf_op jit(solution)/shard_map/pallas_call | solution.py:199
  103.0 2.0 %collective-permute-start.11 = (bf16[48,2,32,128]{3,2,1,0:T(8,128)(2,1)S(1)}, bf16[48,2,32,128]{3,2,1,0:T(8,128)(2,1)S(1)}, u32[]{:S(2)}, u32[]{:S(2)}) collective-permute-start(bf16[48,2,32,128]{3,2,1,0:T(8,128)(2,1)S(1)} %get-tuple-element.38), channel_id=1, source_target_pairs={{0,1},{1,0},{2,3},{3,2},{4,5},{5,4},{6,7},{7,6},{8,9},{9,8},{10,11... | collective-permute-start | bytes 2359304 | tf_op jit(solution)/shard_map/ppermute | solution.py:286
  105.0 2.1 %collective-permute-done.11 = bf16[48,2,32,128]{3,2,1,0:T(8,128)(2,1)S(1)} collective-permute-done((bf16[48,2,32,128]{3,2,1,0:T(8,128)(2,1)S(1)}, bf16[48,2,32,128]{3,2,1,0:T(8,128)(2,1)S(1)}, u32[]{:S(2)}, u32[]{:S(2)}) %collective-permute-start.11) | collective-permute-done | bytes 786464 | tf_op jit(solution)/shard_map/ppermute | solution.py:286
  107.2 0.3 add_convert_fusion
  107.4 0.0 copy-start.2
  107.4 40.9 %all_to_all.10.got_ref = bf16[48,2,32,128]{3,2,1,0:T(8,128)(2,1)S(1)} all-to-all(bf16[48,2,32,128]{3,2,1,0:T(8,128)(2,1)S(1)} %add_convert_fusion), channel_id=1, replica_groups=mesh['y'=4,'z'=12,'x'=4,'h'=2,'c'=2] {'y','z'}, dimensions={0} | all-to-all | bytes 1572864 | tf_op jit(solution)/shard_map/all_to_all | solution.py:287
  148.3 0.7 shard_map.97
  149.1 12.5 %collective-permute-start.12 = (bf16[3,32,128]{2,1,0:T(8,128)(2,1)S(1)}, bf16[3,32,128]{2,1,0:T(8,128)(2,1)S(1)}, u32[]{:S(2)}, u32[]{:S(2)}) collective-permute-start(bf16[3,32,128]{2,1,0:T(8,128)(2,1)S(1)} %get-tuple-element.42), channel_id=1, source_target_pairs={{0,1},{1,2},{2,3},{3,4},{4,5},{5,6},{6,7},{7,8},{8,9},{9,10},{10,1... | collective-permute-start | bytes 73736 | tf_op jit(solution)/shard_map/ppermute | solution.py:25
  161.6 1.9 %collective-permute-start.13 = (bf16[3,32,128]{2,1,0:T(8,128)(2,1)S(1)}, bf16[3,32,128]{2,1,0:T(8,128)(2,1)S(1)}, u32[]{:S(2)}, u32[]{:S(2)}) collective-permute-start(bf16[3,32,128]{2,1,0:T(8,128)(2,1)S(1)} %get-tuple-element.43), channel_id=1, source_target_pairs={{1,0},{2,1},{3,2},{4,3},{5,4},{6,5},{7,6},{8,7},{9,8},{10,9},{11,1... | collective-permute-start | bytes 73736 | tf_op jit(solution)/shard_map/ppermute | solution.py:25
  163.5 0.0 collective-permute-done.12.low_ref
  163.5 8.0 %collective-permute-done.13.high_ref = bf16[3,32,128]{2,1,0:T(8,128)(2,1)S(1)} collective-permute-done((bf16[3,32,128]{2,1,0:T(8,128)(2,1)S(1)}, bf16[3,32,128]{2,1,0:T(8,128)(2,1)S(1)}, u32[]{:S(2)}, u32[]{:S(2)}) %collective-permute-start.13) | collective-permute-done | bytes 24608 | tf_op jit(solution)/shard_map/ppermute | solution.py:25
  171.5 0.0 copy-done.2
  171.5 1.3 shard_map.98
Async XLA Ops:
  0.6 15.9 %copy-start = (f32[1536]{0:T(1024)S(1)}, f32[1536]{0:T(1024)}, u32[]{:S(2)}) copy-start(f32[1536]{0:T(1024)} %param.12) | copy-start | bytes 18436
  0.6 95.9 %copy-start.9 = (f32[1536]{0:T(1024)S(1)}, f32[1536]{0:T(1024)}, u32[]{:S(2)}) copy-start(f32[1536]{0:T(1024)} %param.11) | copy-start | bytes 18436
  0.7 20.9 %collective-permute-start.2 = (bf16[1536,128]{1,0:T(8,128)(2,1)}, bf16[1536,128]{1,0:T(8,128)(2,1)S(1)}, u32[]{:S(2)}, u32[]{:S(2)}) collective-permute-start(bf16[1536,128]{1,0:T(8,128)(2,1)} %param.13), channel_id=1, source_target_pairs={{0,0},{16,1},{2,2},{18,3},{196,4},{212,5},{198,6},{214,7},{392,8},... | collective-permute-start | bytes 1179656 | tf_op jit(solution)/shard_map/ppermute | solution.py:225
  6.1 11.4 %collective-permute-start.1 = (s32[3,128]{1,0:T(4,128)S(1)}, s32[3,128]{1,0:T(4,128)S(1)}, u32[]{:S(2)}, u32[]{:S(2)}) collective-permute-start(s32[3,128]{1,0:T(4,128)S(1)} %get-tuple-element.44), channel_id=1, source_target_pairs={{1,0},{2,1},{3,2},{4,3},{5,4},{6,5},{7,6},{8,7},{9,8},{10,9},{11,1... | collective-permute-start | bytes 4616 | tf_op jit(solution)/shard_map/ppermute | solution.py:25
  8.0 9.5 %collective-permute-start = (s32[3,128]{1,0:T(4,128)S(1)}, s32[3,128]{1,0:T(4,128)S(1)}, u32[]{:S(2)}, u32[]{:S(2)}) collective-permute-start(s32[3,128]{1,0:T(4,128)S(1)} %get-tuple-element.45), channel_id=1, source_target_pairs={{0,1},{1,2},{2,3},{3,4},{4,5},{5,6},{6,7},{7,8},{8,9},{9,10},{10,1... | collective-permute-start | bytes 4616 | tf_op jit(solution)/shard_map/ppermute | solution.py:25
  17.5 0.8 copy-start.1
  18.4 0.7 copy-start.3
  19.1 0.7 copy-start.4
  19.8 19.2 %copy-start.10 = (bf16[128,1536]{1,0:T(8,128)(2,1)S(1)}, bf16[128,1536]{1,0:T(8,128)(2,1)}, u32[]{:S(2)}) copy-start(bf16[128,1536]{1,0:T(8,128)(2,1)} %param.14) | copy-start | bytes 1179652
  21.5 70.8 %all-to-all-start = ((bf16[48,2,32,128]{3,2,1,0:T(8,128)(2,1)}), bf16[48,2,32,128]{3,2,1,0:T(8,128)(2,1)S(1)}, u32[]{:S(2)}, u32[]{:S(2)}) async-start(bf16[48,2,32,128]{3,2,1,0:T(8,128)(2,1)} %get-tuple-element.24), calls=%async_computation | async-start | bytes 1572864 | tf_op jit(solution)/shard_map/all_to_all | solution.py:264
  38.9 31.9 %collective-permute-start.3 = (bf16[128,1536]{1,0:T(8,128)(2,1)S(1)}, bf16[128,1536]{1,0:T(8,128)(2,1)S(1)}, u32[]{:S(2)}, u32[]{:S(2)}) collective-permute-start(bf16[128,1536]{1,0:T(8,128)(2,1)S(1)} %copy-done.10), channel_id=1, source_target_pairs={{0,0},{16,1},{2,2},{18,3},{196,4},{212,5},{198,6},{214,7},{392,8},... | collective-permute-start | bytes 1179656 | tf_op jit(solution)/shard_map/ppermute | solution.py:225
  44.7 26.2 %collective-permute-start.4 = (bf16[1536,128]{1,0:T(8,128)(2,1)S(1)}, bf16[1536,128]{1,0:T(8,128)(2,1)S(1)}, u32[]{:S(2)}, u32[]{:S(2)}) collective-permute-start(bf16[1536,128]{1,0:T(8,128)(2,1)S(1)} %collective-permute-done.2.i0_ref), channel_id=1, source_target_pairs={{8,0},{12,4},{0,8},{4,12},{9,1},{13,5},{1,9},{5,13},{10,2},{14,6},... | collective-permute-start | bytes 1179656 | tf_op jit(solution)/shard_map/ppermute | solution.py:230
  50.1 36.3 %collective-permute-start.6 = (bf16[1536,128]{1,0:T(8,128)(2,1)S(1)}, bf16[1536,128]{1,0:T(8,128)(2,1)S(1)}, u32[]{:S(2)}, u32[]{:S(2)}) collective-permute-start(bf16[1536,128]{1,0:T(8,128)(2,1)S(1)} %collective-permute-done.2.i0_ref), channel_id=1, source_target_pairs={{12,0},{0,4},{4,8},{8,12},{13,1},{1,5},{5,9},{9,13},{14,2},{2,6},{... | collective-permute-start | bytes 1179656 | tf_op jit(solution)/shard_map/ppermute | solution.py:230
  54.1 32.4 %collective-permute-start.5 = (bf16[1536,128]{1,0:T(8,128)(2,1)S(1)}, bf16[1536,128]{1,0:T(8,128)(2,1)S(1)}, u32[]{:S(2)}, u32[]{:S(2)}) collective-permute-start(bf16[1536,128]{1,0:T(8,128)(2,1)S(1)} %collective-permute-done.2.i0_ref), channel_id=1, source_target_pairs={{4,0},{8,4},{12,8},{0,12},{5,1},{9,5},{13,9},{1,13},{6,2},{10,6},{... | collective-permute-start | bytes 1179656 | tf_op jit(solution)/shard_map/ppermute | solution.py:230
  70.9 15.6 %collective-permute-start.9 = (bf16[128,1536]{1,0:T(8,128)(2,1)S(1)}, bf16[128,1536]{1,0:T(8,128)(2,1)S(1)}, u32[]{:S(2)}, u32[]{:S(2)}) collective-permute-start(bf16[128,1536]{1,0:T(8,128)(2,1)S(1)} %collective-permute-done.3.o0_ref), channel_id=1, source_target_pairs={{12,0},{0,4},{4,8},{8,12},{13,1},{1,5},{5,9},{9,13},{14,2},{2,6},{... | collective-permute-start | bytes 1179656 | tf_op jit(solution)/shard_map/ppermute | solution.py:230
  73.6 14.3 %collective-permute-start.8 = (bf16[128,1536]{1,0:T(8,128)(2,1)S(1)}, bf16[128,1536]{1,0:T(8,128)(2,1)S(1)}, u32[]{:S(2)}, u32[]{:S(2)}) collective-permute-start(bf16[128,1536]{1,0:T(8,128)(2,1)S(1)} %collective-permute-done.3.o0_ref), channel_id=1, source_target_pairs={{4,0},{8,4},{12,8},{0,12},{5,1},{9,5},{13,9},{1,13},{6,2},{10,6},{... | collective-permute-start | bytes 1179656 | tf_op jit(solution)/shard_map/ppermute | solution.py:230
  77.4 14.2 %collective-permute-start.7 = (bf16[128,1536]{1,0:T(8,128)(2,1)S(1)}, bf16[128,1536]{1,0:T(8,128)(2,1)S(1)}, u32[]{:S(2)}, u32[]{:S(2)}) collective-permute-start(bf16[128,1536]{1,0:T(8,128)(2,1)S(1)} %collective-permute-done.3.o0_ref), channel_id=1, source_target_pairs={{8,0},{12,4},{0,8},{4,12},{9,1},{13,5},{1,9},{5,13},{10,2},{14,6},... | collective-permute-start | bytes 1179656 | tf_op jit(solution)/shard_map/ppermute | solution.py:230
  87.9 0.8 copy-start.5
  91.6 0.8 copy-start.7
  92.4 4.2 %collective-permute-start.10 = (bf16[48,2,32,128]{3,2,1,0:T(8,128)(2,1)S(1)}, bf16[48,2,32,128]{3,2,1,0:T(8,128)(2,1)S(1)}, u32[]{:S(2)}, u32[]{:S(2)}) collective-permute-start(bf16[48,2,32,128]{3,2,1,0:T(8,128)(2,1)S(1)} %all-to-all-done.own_ref), channel_id=1, source_target_pairs={{0,1},{1,0},{2,3},{3,2},{4,5},{5,4},{6,7},{7,6},{8,9},{9,8},{10,11... | collective-permute-start | bytes 2359304 | tf_op jit(solution)/shard_map/ppermute | solution.py:266
  96.8 1.0 copy-start.6
  97.8 1.0 copy-start.8
  103.0 4.2 %collective-permute-start.11 = (bf16[48,2,32,128]{3,2,1,0:T(8,128)(2,1)S(1)}, bf16[48,2,32,128]{3,2,1,0:T(8,128)(2,1)S(1)}, u32[]{:S(2)}, u32[]{:S(2)}) collective-permute-start(bf16[48,2,32,128]{3,2,1,0:T(8,128)(2,1)S(1)} %get-tuple-element.38), channel_id=1, source_target_pairs={{0,1},{1,0},{2,3},{3,2},{4,5},{5,4},{6,7},{7,6},{8,9},{9,8},{10,11... | collective-permute-start | bytes 2359304 | tf_op jit(solution)/shard_map/ppermute | solution.py:286
  107.4 64.1 %copy-start.2 = (bf16[8,128,32]{1,2,0:T(8,128)(2,1)S(1)}, bf16[8,128,32]{1,2,0:T(8,128)(2,1)}, u32[]{:S(2)}) copy-start(bf16[8,128,32]{1,2,0:T(8,128)(2,1)} %param.15) | copy-start | bytes 196612
  149.1 14.4 %collective-permute-start.12 = (bf16[3,32,128]{2,1,0:T(8,128)(2,1)S(1)}, bf16[3,32,128]{2,1,0:T(8,128)(2,1)S(1)}, u32[]{:S(2)}, u32[]{:S(2)}) collective-permute-start(bf16[3,32,128]{2,1,0:T(8,128)(2,1)S(1)} %get-tuple-element.42), channel_id=1, source_target_pairs={{0,1},{1,2},{2,3},{3,4},{4,5},{5,6},{6,7},{7,8},{8,9},{9,10},{10,1... | collective-permute-start | bytes 73736 | tf_op jit(solution)/shard_map/ppermute | solution.py:25
  161.6 10.0 %collective-permute-start.13 = (bf16[3,32,128]{2,1,0:T(8,128)(2,1)S(1)}, bf16[3,32,128]{2,1,0:T(8,128)(2,1)S(1)}, u32[]{:S(2)}, u32[]{:S(2)}) collective-permute-start(bf16[3,32,128]{2,1,0:T(8,128)(2,1)S(1)} %get-tuple-element.43), channel_id=1, source_target_pairs={{1,0},{2,1},{3,2},{4,3},{5,4},{6,5},{7,6},{8,7},{9,8},{10,9},{11,1... | collective-permute-start | bytes 73736 | tf_op jit(solution)/shard_map/ppermute | solution.py:25

commit v5 on v4

--- a/solution.py
+++ b/solution.py
@@ -80,18 +80,18 @@
 
 
 def middle_kernel(
-    own_ref, oth_ref, gain_ref, i0_ref, i1_ref, i2_ref, i3_ref, o0_ref, o1_ref, o2_ref, o3_ref,
+    own_ref, oth_ref, gain_ref, w0_ref, w1_ref, w2_ref, w3_ref,
     keep_ref, sib_ref,
     win, wout, scaled, gmix, normed, grads, act, gpre, sem,
 ):
     blocks, _, chans, cols = own_ref.shape
     width = blocks * chans
-    hid = o0_ref.shape[0]
-    pieces = [(i0_ref, o0_ref), (i1_ref, o1_ref), (i2_ref, o2_ref), (i3_ref, o3_ref)]
+    hid = w0_ref.shape[1]
+    pieces = [(ref.at[0], ref.at[1]) for ref in (w0_ref, w1_ref, w2_ref, w3_ref)]
     copies = []
     for i, (a, b) in enumerate(pieces):
         spot = pl.ds(i * hid, hid)
-        copies.append(pltpu.make_async_copy(a, win.at[:, spot], sem.at[2 * i]))
+        copies.append(pltpu.make_async_copy(a, win.at[spot], sem.at[2 * i]))
         copies.append(pltpu.make_async_copy(b, wout.at[spot], sem.at[2 * i + 1]))
     for copy in copies:
         copy.start()
@@ -123,10 +123,9 @@
     for copy in copies:
         copy.wait()
 
-    turned = (((0,), (0,)), ((), ()))
     for i in range(len(pieces)):
         spot = pl.ds(i * hid, hid)
-        pre = lax.dot_general(win[:, spot], scaled[...], turned, preferred_element_type=F32)
+        pre = jnp.dot(win[spot, :], scaled[...], preferred_element_type=F32)
         gact = jnp.dot(wout[spot, :], gmix[...], preferred_element_type=F32)
         cube = pre * pre
         tanh = jnp.tanh(ROOT * (pre + 0.044715 * (cube * pre)))
@@ -138,10 +137,11 @@
     group = 256
     per = group // chans
     sums = [jnp.zeros((1, 2 * cols), F32), jnp.zeros((1, 2 * cols), F32)]
+    turned = (((0,), (0,)), ((), ()))
     for j in range(width // group):
         spot = pl.ds(j * group, group)
         gain = gain_ref[spot, :]
-        part = jnp.dot(win[spot, :], gpre[...], preferred_element_type=F32)
+        part = lax.dot_general(win[:, spot], gpre[...], turned, preferred_element_type=F32)
         part = part * jnp.concatenate([gain, gain], axis=1)
         grads[spot, :] = part
         sums[0] = sums[0] + jnp.sum(part, axis=0, keepdims=True)
@@ -242,7 +242,7 @@
     hid = w_out.shape[0] * lax.axis_size("y")
     swap = [(0, 1), (1, 0)]
 
-    w_in = shifted(w_in)
+    both = shifted(jnp.stack([w_in.T, w_out]))
     low, high = edges(floor_tokens[:3] + 1, floor_tokens[rows - 3 :] + 1)
     taps = depth_kernel.reshape(49, chans).T
     scale = lax.dynamic_slice_in_dim(layer_scale, lax.axis_index(CHAN) * chans, chans, 0)[:, None]
@@ -256,21 +256,17 @@
         [(tile, BF16), (packed, BF16)],
         (floor_tokens, low, high, token_table.T, taps, scale, grad_local),
     )
-    send, w_in = lax.optimization_barrier((send, w_in))
-    w_out = shifted(w_out)
-    weights = gathered(w_in)
-    w_out, weights[1] = lax.optimization_barrier((w_out, weights[1]))
-    weights = weights + gathered(w_out)
+    send, both = lax.optimization_barrier((send, both))
+    weights = gathered(both)
     own = lax.all_to_all(send, CHAN, 0, 0, tiled=True)
-    own, *weights = lax.optimization_barrier((own, *weights))
     oth = lax.ppermute(own, "c", swap)
     keep, sib = call(
         middle_kernel,
         [(packed, F32), (packed, BF16)],
         (own, oth, gain, *weights),
-        [VMEM] * 3 + [ANY] * 8,
+        [VMEM] * 3 + [ANY] * 4,
         [
-            pltpu.VMEM((width, hid), BF16),
+            pltpu.VMEM((hid, width), BF16),
             pltpu.VMEM((hid, width), BF16),
             pltpu.VMEM((width, 2 * cols), BF16),
             pltpu.VMEM((width, 2 * cols), BF16),

time: 174 us -> 162 us (0.931)
  starting transfers between devices: 84 us -> 64.6 us
  waiting for transfers between devices: 31 us -> 44.5 us
  local copies, waits for them, and re-layouts: 7.02 us -> 1.77 us
    ppermute x6 -> x3, starting transfers between devices: 27.4 us -> 9.78 us  [gathered(): lax.ppermute(shard, 'x', [((i + k) % nx, i) for i in range(nx)])]
    all_to_all x1, waiting for transfers between devices: 0.01 us -> 15.5 us  [on_device(): own = lax.all_to_all(send, CHAN, 0, 0, tiled=True)]
    ppermute x2 -> x1, waiting for transfers between devices: 14.2 us -> 0.01 us  [shifted(): return lax.ppermute(shard, AXES, pairs)]
    ppermute x2, waiting for transfers between devices: 8.02 us -> 17.3 us  [edges(): lax.ppermute(low_side, SPACE, backward)]
    ppermute x2 -> x1, starting transfers between devices: 10.5 us -> 4.56 us  [shifted(): return lax.ppermute(shard, AXES, pairs)]
    ppermute x6 -> x3, waiting for transfers between devices: 4.36 us -> 9.88 us  [gathered(): lax.ppermute(shard, 'x', [((i + k) % nx, i) for i in range(nx)])]
    unnamed x22 -> x13, local copies, waits for them, and re-layouts: 5.77 us -> 1.24 us
    ppermute x1, starting transfers between devices: 2.04 us -> 5.95 us  [on_device(): part = (keep + lax.ppermute(sib, 'c', swap).astype(F32)).astype(BF16)]
  transfers between devices with their start and end apart: 15 -> 11, of which waited for: 6 -> 5; matrix products, arithmetic and copies ran while one was open for 1% -> 0% of each run, Pallas kernels for 1% -> 1%
where the time goes in v5:
time: 162 us; the launch traced here: 161 us
  starting transfers between devices  64.6 us (40%)
  waiting for transfers between devices  44.5 us (27%)
  blocking collectives  40.3 us (25%)
  Pallas kernels  7.98 us (5%)
  local copies, waits for them, and re-layouts  1.77 us (1%)
    all_to_all x1, blocking collectives, on_device(): got = lax.all_to_all(part, CHAN, 0, 0, tiled=True)  40.3 us
    ppermute x2, starting transfers between devices, edges(): lax.ppermute(high_side, SPACE, forward)  20.9 us
    all_to_all x1, starting transfers between devices, on_device(): own = lax.all_to_all(send, CHAN, 0, 0, tiled=True)  17.7 us
    ppermute x2, waiting for transfers between devices, edges(): lax.ppermute(low_side, SPACE, backward)  17.3 us
    all_to_all x1, waiting for transfers between devices, on_device(): own = lax.all_to_all(send, CHAN, 0, 0, tiled=True)  15.5 us
    ppermute x3, waiting for transfers between devices, gathered(): lax.ppermute(shard, 'x', [((i + k) % nx, i) for i in range(nx)])  9.88 us
    ppermute x3, starting transfers between devices, gathered(): lax.ppermute(shard, 'x', [((i + k) % nx, i) for i in range(nx)])  9.78 us
    pallas_call x4, Pallas kernels, call(): pl.pallas_call(body, out_shape=outs, in_specs=specs or [VMEM] * len(args)...  7.98 us
  transfers between devices with their start and end apart: 11, of which 5 were waited for; matrix products, arithmetic and copies ran while one was open for 0% of the time, Pallas kernels for 1%

profile of v5, /device:TPU:57, one launch (start us, length us, event | category | flops | bytes accessed | tf_op | source)
XLA Modules:
  0.0 161.3 jit_solution(17851175556741008572)
XLA Ops:
  0.6 0.0 copy-start
  0.6 0.0 copy-start.3
  0.7 0.0 copy-start.4
  0.7 0.0 copy-start.1
  0.7 0.0 copy-start.2
  0.7 1.2 copy.16
  1.9 0.0 copy-start.5
  1.9 1.1 pad_maximum_fusion
  3.0 4.6 %collective-permute-start.2 = (bf16[2,128,1536]{2,1,0:T(8,128)(2,1)S(1)}, bf16[2,128,1536]{2,1,0:T(8,128)(2,1)S(1)}, u32[]{:S(2)}, u32[]{:S(2)}) collective-permute-start(bf16[2,128,1536]{2,1,0:T(8,128)(2,1)S(1)} %pad_maximum_fusion), channel_id=1, source_target_pairs={{0,0},{16,1},{2,2},{18,3},{196,4},{212,5},{198,6},{214,7},{392,8},... | collective-permute-start | bytes 2359304 | tf_op jit(solution)/shard_map/ppermute | solution.py:225
  7.6 0.0 copy-done.3
  7.6 1.9 %collective-permute-start.1 = (s32[3,128]{1,0:T(4,128)S(1)}, s32[3,128]{1,0:T(4,128)S(1)}, u32[]{:S(2)}, u32[]{:S(2)}) collective-permute-start(s32[3,128]{1,0:T(4,128)S(1)} %get-tuple-element.22), channel_id=1, source_target_pairs={{1,0},{2,1},{3,2},{4,3},{5,4},{6,5},{7,6},{8,7},{9,8},{10,9},{11,1... | collective-permute-start | bytes 4616 | tf_op jit(solution)/shard_map/ppermute | solution.py:25
  9.5 8.4 %collective-permute-start = (s32[3,128]{1,0:T(4,128)S(1)}, s32[3,128]{1,0:T(4,128)S(1)}, u32[]{:S(2)}, u32[]{:S(2)}) collective-permute-start(s32[3,128]{1,0:T(4,128)S(1)} %get-tuple-element.23), channel_id=1, source_target_pairs={{0,1},{1,2},{2,3},{3,4},{4,5},{5,6},{6,7},{7,8},{8,9},{9,10},{10,1... | collective-permute-start | bytes 4616 | tf_op jit(solution)/shard_map/ppermute | solution.py:25
  18.0 0.0 copy-done
  18.0 0.1 dynamic-slice_bitcast_fusion
  18.1 0.0 copy-done.4
  18.1 0.1 copy.14
  18.2 0.1 copy.15.scale_ref
  18.3 9.2 %collective-permute-done.1.high_ref = s32[3,128]{1,0:T(4,128)S(1)} collective-permute-done((s32[3,128]{1,0:T(4,128)S(1)}, s32[3,128]{1,0:T(4,128)S(1)}, u32[]{:S(2)}, u32[]{:S(2)}) %collective-permute-start.1) | collective-permute-done | bytes 1568 | tf_op jit(solution)/shard_map/ppermute | solution.py:25
  27.5 0.0 collective-permute-done.low_ref
  27.5 0.0 copy-done.1
  27.5 0.0 copy-done.2
  27.5 1.7 %shard_map.95 = (bf16[8,32,128]{2,1,0:T(8,128)(2,1)S(1)}, bf16[48,2,32,128]{3,2,1,0:T(8,128)(2,1)}) custom-call(s32[8,128]{1,0:T(8,128)S(1)} %copy-done.3, s32[3,128]{1,0:T(4,128)S(1)} %collective-permute-done.low_ref, s32[3,128]{1,0:T(4,128)S(1)} %collective-permute-done.1.high_ref, bf16[32,256]{1,0:T(8,128)(2,1)S(1)} %bitcast.15, ...), custom_call_target="tpu_custom_call" | custom-call | flops 1048576 | bytes 4194304 | tf_op jit(solution)/shard_map/pallas_call | solution.py:199
  29.2 0.0 collective-permute-done.2.w0_ref
  29.2 17.7 %all-to-all-start = ((bf16[48,2,32,128]{3,2,1,0:T(8,128)(2,1)}), bf16[48,2,32,128]{3,2,1,0:T(8,128)(2,1)S(1)}, u32[]{:S(2)}, u32[]{:S(2)}) async-start(bf16[48,2,32,128]{3,2,1,0:T(8,128)(2,1)} %get-tuple-element.13), calls=%async_computation | async-start | bytes 1572864 | tf_op jit(solution)/shard_map/all_to_all | solution.py:261
  46.9 3.1 %collective-permute-start.6 = (bf16[2,128,1536]{2,1,0:T(8,128)(2,1)S(1)}, bf16[2,128,1536]{2,1,0:T(8,128)(2,1)S(1)}, u32[]{:S(2)}, u32[]{:S(2)}) collective-permute-start(bf16[2,128,1536]{2,1,0:T(8,128)(2,1)S(1)} %collective-permute-done.2.w0_ref), channel_id=1, source_target_pairs={{12,0},{0,4},{4,8},{8,12},{13,1},{1,5},{5,9},{9,13},{14,2},{2,6},{... | collective-permute-start | bytes 2359304 | tf_op jit(solution)/shard_map/ppermute | solution.py:230
  50.0 3.4 %collective-permute-start.5 = (bf16[2,128,1536]{2,1,0:T(8,128)(2,1)S(1)}, bf16[2,128,1536]{2,1,0:T(8,128)(2,1)S(1)}, u32[]{:S(2)}, u32[]{:S(2)}) collective-permute-start(bf16[2,128,1536]{2,1,0:T(8,128)(2,1)S(1)} %collective-permute-done.2.w0_ref), channel_id=1, source_target_pairs={{4,0},{8,4},{12,8},{0,12},{5,1},{9,5},{13,9},{1,13},{6,2},{10,6},{... | collective-permute-start | bytes 2359304 | tf_op jit(solution)/shard_map/ppermute | solution.py:230
  53.5 3.3 %collective-permute-start.4 = (bf16[2,128,1536]{2,1,0:T(8,128)(2,1)S(1)}, bf16[2,128,1536]{2,1,0:T(8,128)(2,1)}, u32[]{:S(2)}, u32[]{:S(2)}) collective-permute-start(bf16[2,128,1536]{2,1,0:T(8,128)(2,1)S(1)} %collective-permute-done.2.w0_ref), channel_id=1, source_target_pairs={{8,0},{12,4},{0,8},{4,12},{9,1},{13,5},{1,9},{5,13},{10,2},{14,6},... | collective-permute-start | bytes 2359304 | tf_op jit(solution)/shard_map/ppermute | solution.py:230
  56.7 15.5 %all-to-all-done.own_ref = bf16[48,2,32,128]{3,2,1,0:T(8,128)(2,1)S(1)} async-done(((bf16[48,2,32,128]{3,2,1,0:T(8,128)(2,1)}), bf16[48,2,32,128]{3,2,1,0:T(8,128)(2,1)S(1)}, u32[]{:S(2)}, u32[]{:S(2)}) %all-to-all-start) | async-done | bytes 786464 | tf_op jit(solution)/shard_map/all_to_all | solution.py:261
  72.2 1.9 %collective-permute-start.3 = (bf16[48,2,32,128]{3,2,1,0:T(8,128)(2,1)S(1)}, bf16[48,2,32,128]{3,2,1,0:T(8,128)(2,1)S(1)}, u32[]{:S(2)}, u32[]{:S(2)}) collective-permute-start(bf16[48,2,32,128]{3,2,1,0:T(8,128)(2,1)S(1)} %all-to-all-done.own_ref), channel_id=1, source_target_pairs={{0,1},{1,0},{2,3},{3,2},{4,5},{5,4},{6,7},{7,6},{8,9},{9,8},{10,11... | collective-permute-start | bytes 2359304 | tf_op jit(solution)/shard_map/ppermute | solution.py:262
  74.1 0.0 collective-permute-done.6.w3_ref
  74.2 0.0 collective-permute-done.5.w2_ref
  74.2 9.9 %collective-permute-done.4.w1_ref = bf16[2,128,1536]{2,1,0:T(8,128)(2,1)} collective-permute-done((bf16[2,128,1536]{2,1,0:T(8,128)(2,1)S(1)}, bf16[2,128,1536]{2,1,0:T(8,128)(2,1)}, u32[]{:S(2)}, u32[]{:S(2)}) %collective-permute-start.4) | collective-permute-done | bytes 786464 | tf_op jit(solution)/shard_map/ppermute | solution.py:230
  84.0 0.0 collective-permute-done.3.oth_ref
  84.0 0.0 copy-done.5
  84.0 0.3 broadcast_in_dim.10.gain_ref
  84.3 4.2 %shard_map.96 = (f32[48,2,32,128]{3,2,1,0:T(8,128)S(1)}, bf16[48,2,32,128]{3,2,1,0:T(8,128)(2,1)S(1)}) custom-call(bf16[48,2,32,128]{3,2,1,0:T(8,128)(2,1)S(1)} %all-to-all-done.own_ref, bf16[48,2,32,128]{3,2,1,0:T(8,128)(2,1)S(1)} %collective-permute-done.3.oth_ref, f32[1536,128]{1,0:T(8,128)S(1)} %broadcast_in_dim.10.gain_ref, ...), custom_call_target="tpu_custom_call" | custom-call | flops 1610612736 | bytes 4194304 | tf_op jit(solution)/shard_map/pallas_call | solution.py:199
  88.5 6.0 %collective-permute-start.7 = (bf16[48,2,32,128]{3,2,1,0:T(8,128)(2,1)S(1)}, bf16[48,2,32,128]{3,2,1,0:T(8,128)(2,1)S(1)}, u32[]{:S(2)}, u32[]{:S(2)}) collective-permute-start(bf16[48,2,32,128]{3,2,1,0:T(8,128)(2,1)S(1)} %get-tuple-element.16), channel_id=1, source_target_pairs={{0,1},{1,0},{2,3},{3,2},{4,5},{5,4},{6,7},{7,6},{8,9},{9,8},{10,11... | collective-permute-start | bytes 2359304 | tf_op jit(solution)/shard_map/ppermute | solution.py:282
  94.5 1.9 %collective-permute-done.7 = bf16[48,2,32,128]{3,2,1,0:T(8,128)(2,1)S(1)} collective-permute-done((bf16[48,2,32,128]{3,2,1,0:T(8,128)(2,1)S(1)}, bf16[48,2,32,128]{3,2,1,0:T(8,128)(2,1)S(1)}, u32[]{:S(2)}, u32[]{:S(2)}) %collective-permute-start.7) | collective-permute-done | bytes 786464 | tf_op jit(solution)/shard_map/ppermute | solution.py:282
  96.4 0.3 add_convert_fusion
  96.6 40.3 %all_to_all.10.got_ref = bf16[48,2,32,128]{3,2,1,0:T(8,128)(2,1)S(1)} all-to-all(bf16[48,2,32,128]{3,2,1,0:T(8,128)(2,1)S(1)} %add_convert_fusion), channel_id=1, replica_groups=mesh['y'=4,'z'=12,'x'=4,'h'=2,'c'=2] {'y','z'}, dimensions={0} | all-to-all | bytes 1572864 | tf_op jit(solution)/shard_map/all_to_all | solution.py:283
  136.9 0.7 shard_map.97
  137.7 12.4 %collective-permute-start.8 = (bf16[3,32,128]{2,1,0:T(8,128)(2,1)S(1)}, bf16[3,32,128]{2,1,0:T(8,128)(2,1)S(1)}, u32[]{:S(2)}, u32[]{:S(2)}) collective-permute-start(bf16[3,32,128]{2,1,0:T(8,128)(2,1)S(1)} %get-tuple-element.20), channel_id=1, source_target_pairs={{0,1},{1,2},{2,3},{3,4},{4,5},{5,6},{6,7},{7,8},{8,9},{9,10},{10,1... | collective-permute-start | bytes 73736 | tf_op jit(solution)/shard_map/ppermute | solution.py:25
  150.1 1.9 %collective-permute-start.9 = (bf16[3,32,128]{2,1,0:T(8,128)(2,1)S(1)}, bf16[3,32,128]{2,1,0:T(8,128)(2,1)S(1)}, u32[]{:S(2)}, u32[]{:S(2)}) collective-permute-start(bf16[3,32,128]{2,1,0:T(8,128)(2,1)S(1)} %get-tuple-element.21), channel_id=1, source_target_pairs={{1,0},{2,1},{3,2},{4,3},{5,4},{6,5},{7,6},{8,7},{9,8},{10,9},{11,1... | collective-permute-start | bytes 73736 | tf_op jit(solution)/shard_map/ppermute | solution.py:25
  152.0 0.0 collective-permute-done.8.low_ref
  152.0 8.0 %collective-permute-done.9.high_ref = bf16[3,32,128]{2,1,0:T(8,128)(2,1)S(1)} collective-permute-done((bf16[3,32,128]{2,1,0:T(8,128)(2,1)S(1)}, bf16[3,32,128]{2,1,0:T(8,128)(2,1)S(1)}, u32[]{:S(2)}, u32[]{:S(2)}) %collective-permute-start.9) | collective-permute-done | bytes 24608 | tf_op jit(solution)/shard_map/ppermute | solution.py:25
  160.0 1.3 shard_map.98
  (2 shorter events, 0.0 us)
Async XLA Ops:
  0.6 17.4 %copy-start = (f32[1536]{0:T(1024)S(1)}, f32[1536]{0:T(1024)}, u32[]{:S(2)}) copy-start(f32[1536]{0:T(1024)} %param.12) | copy-start | bytes 18436
  0.6 6.9 %copy-start.3 = (s32[8,128]{1,0:T(8,128)S(1)}, s32[8,128]{1,0:T(8,128)}, u32[]{:S(2)}) copy-start(s32[8,128]{1,0:T(8,128)} %tok_ref.1) | copy-start | bytes 12292
  0.7 17.4 %copy-start.4 = (bf16[7,7,32]{2,1,0:T(8,128)(2,1)S(1)}, bf16[7,7,32]{2,1,0:T(8,128)(2,1)}, u32[]{:S(2)}) copy-start(bf16[7,7,32]{2,1,0:T(8,128)(2,1)} %param.10) | copy-start | bytes 9412
  0.7 26.9 %copy-start.1 = (bf16[8,128,32]{1,2,0:T(8,128)(2,1)S(1)}, bf16[8,128,32]{1,2,0:T(8,128)(2,1)}, u32[]{:S(2)}) copy-start(bf16[8,128,32]{1,2,0:T(8,128)(2,1)} %param.15) | copy-start | bytes 196612
  0.7 26.8 %copy-start.2 = (bf16[256,32]{0,1:T(8,128)(2,1)S(1)}, bf16[256,32]{0,1:T(8,128)(2,1)}, u32[]{:S(2)}) copy-start(bf16[256,32]{0,1:T(8,128)(2,1)} %param.9) | copy-start | bytes 49156
  1.9 82.1 %copy-start.5 = (f32[1536]{0:T(1024)S(1)}, f32[1536]{0:T(1024)}, u32[]{:S(2)}) copy-start(f32[1536]{0:T(1024)} %param.11) | copy-start | bytes 18436
  3.0 26.2 %collective-permute-start.2 = (bf16[2,128,1536]{2,1,0:T(8,128)(2,1)S(1)}, bf16[2,128,1536]{2,1,0:T(8,128)(2,1)S(1)}, u32[]{:S(2)}, u32[]{:S(2)}) collective-permute-start(bf16[2,128,1536]{2,1,0:T(8,128)(2,1)S(1)} %pad_maximum_fusion), channel_id=1, source_target_pairs={{0,0},{16,1},{2,2},{18,3},{196,4},{212,5},{198,6},{214,7},{392,8},... | collective-permute-start | bytes 2359304 | tf_op jit(solution)/shard_map/ppermute | solution.py:225
  7.6 19.9 %collective-permute-start.1 = (s32[3,128]{1,0:T(4,128)S(1)}, s32[3,128]{1,0:T(4,128)S(1)}, u32[]{:S(2)}, u32[]{:S(2)}) collective-permute-start(s32[3,128]{1,0:T(4,128)S(1)} %get-tuple-element.22), channel_id=1, source_target_pairs={{1,0},{2,1},{3,2},{4,3},{5,4},{6,5},{7,6},{8,7},{9,8},{10,9},{11,1... | collective-permute-start | bytes 4616 | tf_op jit(solution)/shard_map/ppermute | solution.py:25
  9.5 18.0 %collective-permute-start = (s32[3,128]{1,0:T(4,128)S(1)}, s32[3,128]{1,0:T(4,128)S(1)}, u32[]{:S(2)}, u32[]{:S(2)}) collective-permute-start(s32[3,128]{1,0:T(4,128)S(1)} %get-tuple-element.23), channel_id=1, source_target_pairs={{0,1},{1,2},{2,3},{3,4},{4,5},{5,6},{6,7},{7,8},{8,9},{9,10},{10,1... | collective-permute-start | bytes 4616 | tf_op jit(solution)/shard_map/ppermute | solution.py:25
  29.2 43.0 %all-to-all-start = ((bf16[48,2,32,128]{3,2,1,0:T(8,128)(2,1)}), bf16[48,2,32,128]{3,2,1,0:T(8,128)(2,1)S(1)}, u32[]{:S(2)}, u32[]{:S(2)}) async-start(bf16[48,2,32,128]{3,2,1,0:T(8,128)(2,1)} %get-tuple-element.13), calls=%async_computation | async-start | bytes 1572864 | tf_op jit(solution)/shard_map/all_to_all | solution.py:261
  46.9 27.2 %collective-permute-start.6 = (bf16[2,128,1536]{2,1,0:T(8,128)(2,1)S(1)}, bf16[2,128,1536]{2,1,0:T(8,128)(2,1)S(1)}, u32[]{:S(2)}, u32[]{:S(2)}) collective-permute-start(bf16[2,128,1536]{2,1,0:T(8,128)(2,1)S(1)} %collective-permute-done.2.w0_ref), channel_id=1, source_target_pairs={{12,0},{0,4},{4,8},{8,12},{13,1},{1,5},{5,9},{9,13},{14,2},{2,6},{... | collective-permute-start | bytes 2359304 | tf_op jit(solution)/shard_map/ppermute | solution.py:230
  50.0 24.1 %collective-permute-start.5 = (bf16[2,128,1536]{2,1,0:T(8,128)(2,1)S(1)}, bf16[2,128,1536]{2,1,0:T(8,128)(2,1)S(1)}, u32[]{:S(2)}, u32[]{:S(2)}) collective-permute-start(bf16[2,128,1536]{2,1,0:T(8,128)(2,1)S(1)} %collective-permute-done.2.w0_ref), channel_id=1, source_target_pairs={{4,0},{8,4},{12,8},{0,12},{5,1},{9,5},{13,9},{1,13},{6,2},{10,6},{... | collective-permute-start | bytes 2359304 | tf_op jit(solution)/shard_map/ppermute | solution.py:230
  53.5 30.6 %collective-permute-start.4 = (bf16[2,128,1536]{2,1,0:T(8,128)(2,1)S(1)}, bf16[2,128,1536]{2,1,0:T(8,128)(2,1)}, u32[]{:S(2)}, u32[]{:S(2)}) collective-permute-start(bf16[2,128,1536]{2,1,0:T(8,128)(2,1)S(1)} %collective-permute-done.2.w0_ref), channel_id=1, source_target_pairs={{8,0},{12,4},{0,8},{4,12},{9,1},{13,5},{1,9},{5,13},{10,2},{14,6},... | collective-permute-start | bytes 2359304 | tf_op jit(solution)/shard_map/ppermute | solution.py:230
  72.2 11.8 %collective-permute-start.3 = (bf16[48,2,32,128]{3,2,1,0:T(8,128)(2,1)S(1)}, bf16[48,2,32,128]{3,2,1,0:T(8,128)(2,1)S(1)}, u32[]{:S(2)}, u32[]{:S(2)}) collective-permute-start(bf16[48,2,32,128]{3,2,1,0:T(8,128)(2,1)S(1)} %all-to-all-done.own_ref), channel_id=1, source_target_pairs={{0,1},{1,0},{2,3},{3,2},{4,5},{5,4},{6,7},{7,6},{8,9},{9,8},{10,11... | collective-permute-start | bytes 2359304 | tf_op jit(solution)/shard_map/ppermute | solution.py:262
  88.5 7.9 %collective-permute-start.7 = (bf16[48,2,32,128]{3,2,1,0:T(8,128)(2,1)S(1)}, bf16[48,2,32,128]{3,2,1,0:T(8,128)(2,1)S(1)}, u32[]{:S(2)}, u32[]{:S(2)}) collective-permute-start(bf16[48,2,32,128]{3,2,1,0:T(8,128)(2,1)S(1)} %get-tuple-element.16), channel_id=1, source_target_pairs={{0,1},{1,0},{2,3},{3,2},{4,5},{5,4},{6,7},{7,6},{8,9},{9,8},{10,11... | collective-permute-start | bytes 2359304 | tf_op jit(solution)/shard_map/ppermute | solution.py:282
  137.7 14.3 %collective-permute-start.8 = (bf16[3,32,128]{2,1,0:T(8,128)(2,1)S(1)}, bf16[3,32,128]{2,1,0:T(8,128)(2,1)S(1)}, u32[]{:S(2)}, u32[]{:S(2)}) collective-permute-start(bf16[3,32,128]{2,1,0:T(8,128)(2,1)S(1)} %get-tuple-element.20), channel_id=1, source_target_pairs={{0,1},{1,2},{2,3},{3,4},{4,5},{5,6},{6,7},{7,8},{8,9},{9,10},{10,1... | collective-permute-start | bytes 73736 | tf_op jit(solution)/shard_map/ppermute | solution.py:25
  150.1 10.0 %collective-permute-start.9 = (bf16[3,32,128]{2,1,0:T(8,128)(2,1)S(1)}, bf16[3,32,128]{2,1,0:T(8,128)(2,1)S(1)}, u32[]{:S(2)}, u32[]{:S(2)}) collective-permute-start(bf16[3,32,128]{2,1,0:T(8,128)(2,1)S(1)} %get-tuple-element.21), channel_id=1, source_target_pairs={{1,0},{2,1},{3,2},{4,3},{5,4},{6,5},{7,6},{8,7},{9,8},{10,9},{11,1... | collective-permute-start | bytes 73736 | tf_op jit(solution)/shard_map/ppermute | solution.py:25

commit v6 on v4

--- a/solution.py
+++ b/solution.py
@@ -80,19 +80,17 @@
 
 
 def middle_kernel(
-    own_ref, oth_ref, gain_ref, i0_ref, i1_ref, i2_ref, i3_ref, o0_ref, o1_ref, o2_ref, o3_ref,
+    own_ref, oth_ref, gain_ref, in_ref, o0_ref, o1_ref, o2_ref, o3_ref,
     keep_ref, sib_ref,
     win, wout, scaled, gmix, normed, grads, act, gpre, sem,
 ):
     blocks, _, chans, cols = own_ref.shape
     width = blocks * chans
     hid = o0_ref.shape[0]
-    pieces = [(i0_ref, o0_ref), (i1_ref, o1_ref), (i2_ref, o2_ref), (i3_ref, o3_ref)]
-    copies = []
-    for i, (a, b) in enumerate(pieces):
-        spot = pl.ds(i * hid, hid)
-        copies.append(pltpu.make_async_copy(a, win.at[:, spot], sem.at[2 * i]))
-        copies.append(pltpu.make_async_copy(b, wout.at[spot], sem.at[2 * i + 1]))
+    pieces = (o0_ref, o1_ref, o2_ref, o3_ref)
+    copies = [pltpu.make_async_copy(in_ref, win, sem.at[0])]
+    for i, piece in enumerate(pieces):
+        copies.append(pltpu.make_async_copy(piece, wout.at[pl.ds(i * hid, hid)], sem.at[i + 1]))
     for copy in copies:
         copy.start()
 
@@ -207,28 +205,32 @@
     )(*args)
 
 
-def shifted(shard):
+def moved(shard, turn_of):
     ny, nz, nx, nh, nc = (lax.axis_size(a) for a in AXES)
-    count = ny * nh
 
     def place(y, z, x, h, c):
         return (((y * nz + z) * nx + x) * nh + h) * nc + c
 
     pairs = []
     for y, z, x, h, c in itertools.product(*[range(n) for n in (ny, nz, nx, nh, nc)]):
-        turn = x % ny
-        if 2 * turn > ny or (2 * turn == ny and c):
-            turn -= ny
-        spot = (h * ny + y + turn) % count
+        spot = (h * ny + y + turn_of(x, c)) % (ny * nh)
         other = (z, c) if z % 2 == c else (z ^ 1, 1 - c)
         pairs.append((place(spot % ny, other[0], x, spot // ny, other[1]), place(y, z, x, h, c)))
     return lax.ppermute(shard, AXES, pairs)
 
 
-def gathered(shard):
-    nx = lax.axis_size("x")
-    others = [lax.ppermute(shard, "x", [((i + k) % nx, i) for i in range(nx)]) for k in (2, 1, 3)]
-    return [shard, *others]
+def turns(k, c):
+    return (0, 1, -2 if c else 2, -1)[k]
+
+
+def from_ring(shard, k):
+    nh, ny = lax.axis_size("h"), lax.axis_size("y")
+    ring = [y * nh + h for h in range(nh) for y in range(ny)]
+    count = len(ring)
+    pairs = [
+        (ring[(i + turns(k, c)) % count] * 2 + c, ring[i] * 2 + c) for i in range(count) for c in range(2)
+    ]
+    return lax.ppermute(shard, ("y", "h", "c"), pairs)
 
 
 def on_device(
@@ -242,7 +244,8 @@
     hid = w_out.shape[0] * lax.axis_size("y")
     swap = [(0, 1), (1, 0)]
 
-    w_in = shifted(w_in)
+    w_in = moved(w_in, lambda x, c: turns(x, c))
+    w_out = moved(w_out, lambda x, c: 0)
     low, high = edges(floor_tokens[:3] + 1, floor_tokens[rows - 3 :] + 1)
     taps = depth_kernel.reshape(49, chans).T
     scale = lax.dynamic_slice_in_dim(layer_scale, lax.axis_index(CHAN) * chans, chans, 0)[:, None]
@@ -256,11 +259,9 @@
         [(tile, BF16), (packed, BF16)],
         (floor_tokens, low, high, token_table.T, taps, scale, grad_local),
     )
-    send, w_in = lax.optimization_barrier((send, w_in))
-    w_out = shifted(w_out)
-    weights = gathered(w_in)
-    w_out, weights[1] = lax.optimization_barrier((w_out, weights[1]))
-    weights = weights + gathered(w_out)
+    send, w_in, w_out = lax.optimization_barrier((send, w_in, w_out))
+    w_in = lax.all_gather(w_in, "x", axis=1, tiled=True)
+    weights = [w_in, w_out, *[from_ring(w_out, k) for k in (1, 2, 3)]]
     own = lax.all_to_all(send, CHAN, 0, 0, tiled=True)
     own, *weights = lax.optimization_barrier((own, *weights))
     oth = lax.ppermute(own, "c", swap)
@@ -268,7 +269,7 @@
         middle_kernel,
         [(packed, F32), (packed, BF16)],
         (own, oth, gain, *weights),
-        [VMEM] * 3 + [ANY] * 8,
+        [VMEM] * 3 + [ANY] * 5,
         [
             pltpu.VMEM((width, hid), BF16),
             pltpu.VMEM((hid, width), BF16),
@@ -278,7 +279,7 @@
             pltpu.VMEM((width, 2 * cols), F32),
             pltpu.VMEM((hid, 2 * cols), BF16),
             pltpu.VMEM((hid, 2 * cols), BF16),
-            pltpu.SemaphoreType.DMA((8,)),
+            pltpu.SemaphoreType.DMA((5,)),
         ],
         flops=8 * hid * width * 2 * cols,
         limit=40 << 20,

time: 174 us -> 171 us (0.983)
  starting transfers between devices: 84 us -> 58.7 us
  between operations: 0.9 us -> 14.2 us
  waiting for transfers between devices: 31 us -> 41.5 us
    ppermute x8 -> x5, starting transfers between devices: 37.9 us -> 13.7 us  [the longest x3 7.2 us: from_ring(): return lax.ppermute(shard, ('y', 'h', 'c'), pairs)]
    ppermute x8 -> x5, waiting for transfers between devices: 18.6 us -> 29.1 us  [the longest x3 29.1 us: from_ring(): return lax.ppermute(shard, ('y', 'h', 'c'), pairs)]
    unnamed x22 -> x16, local copies, waits for them, and re-layouts: 5.77 us -> 4.43 us
  transfers between devices with their start and end apart: 15 -> 13, of which waited for: 6 -> 5; matrix products, arithmetic and copies ran while one was open for 1% -> 1% of each run, Pallas kernels for 1% -> 1%
where the time goes in v6:
time: 171 us; the launch traced here: 169 us
  starting transfers between devices  58.7 us (34%)
  waiting for transfers between devices  41.5 us (24%)
  blocking collectives  40.1 us (23%)
  between operations  14.2 us (8%)
  Pallas kernels  7.77 us (5%)
  local copies, waits for them, and re-layouts  5.67 us (3%)
    all_to_all x1, blocking collectives, on_device(): got = lax.all_to_all(part, CHAN, 0, 0, tiled=True)  40.1 us
    ppermute x3, waiting for transfers between devices, from_ring(): return lax.ppermute(shard, ('y', 'h', 'c'), pairs)  29.1 us
    ppermute x2, starting transfers between devices, edges(): lax.ppermute(high_side, SPACE, forward)  19.8 us
    all_to_all x1, starting transfers between devices, on_device(): own = lax.all_to_all(send, CHAN, 0, 0, tiled=True)  17.4 us
    ppermute x2, waiting for transfers between devices, edges(): lax.ppermute(low_side, SPACE, backward)  8.02 us
    pallas_call x4, Pallas kernels, call(): pl.pallas_call(body, out_shape=outs, in_specs=specs or [VMEM] * len(args)...  7.77 us
    ppermute x3, starting transfers between devices, from_ring(): return lax.ppermute(shard, ('y', 'h', 'c'), pairs)  7.2 us
    ppermute x2, starting transfers between devices, moved(): return lax.ppermute(shard, AXES, pairs)  6.48 us
  transfers between devices with their start and end apart: 13, of which 5 were waited for; matrix products, arithmetic and copies ran while one was open for 1% of the time, Pallas kernels for 1%

profile of v6, /device:TPU:57, one launch (start us, length us, event | category | flops | bytes accessed | tf_op | source)
XLA Modules:
  0.0 169.0 jit_solution(6599484919228158966)
XLA Ops:
  7.2 0.0 copy-start
  7.2 0.0 copy-start.7
  7.2 0.0 all-gather.2.cloned.1.call-start
  7.2 4.6 %collective-permute-start.2 = (bf16[1536,128]{1,0:T(8,128)(2,1)}, bf16[1536,128]{1,0:T(8,128)(2,1)S(1)}, u32[]{:S(2)}, u32[]{:S(2)}) collective-permute-start(bf16[1536,128]{1,0:T(8,128)(2,1)} %param.13), channel_id=1, source_target_pairs={{0,0},{16,1},{2,2},{18,3},{196,4},{212,5},{198,6},{214,7},{392,8},... | collective-permute-start | bytes 1179656 | tf_op jit(solution)/shard_map/ppermute | solution.py:219
  11.8 1.9 %collective-permute-start.3 = (bf16[128,1536]{1,0:T(8,128)(2,1)}, bf16[128,1536]{1,0:T(8,128)(2,1)S(1)}, u32[]{:S(2)}, u32[]{:S(2)}) collective-permute-start(bf16[128,1536]{1,0:T(8,128)(2,1)} %param.14), channel_id=1, source_target_pairs={{0,0},{16,1},{2,2},{18,3},{4,4},{20,5},{6,6},{22,7},{8,8},{24,9},{... | collective-permute-start | bytes 1179656 | tf_op jit(solution)/shard_map/ppermute | solution.py:219
  13.7 0.8 slice_add_fusion
  14.5 1.9 %collective-permute-start.1 = (s32[3,128]{1,0:T(4,128)S(1)}, s32[3,128]{1,0:T(4,128)S(1)}, u32[]{:S(2)}, u32[]{:S(2)}) collective-permute-start(s32[3,128]{1,0:T(4,128)S(1)} %get-tuple-element.36), channel_id=1, source_target_pairs={{1,0},{2,1},{3,2},{4,3},{5,4},{6,5},{7,6},{8,7},{9,8},{10,9},{11,1... | collective-permute-start | bytes 4616 | tf_op jit(solution)/shard_map/ppermute | solution.py:25
  16.4 8.4 %collective-permute-start = (s32[3,128]{1,0:T(4,128)S(1)}, s32[3,128]{1,0:T(4,128)S(1)}, u32[]{:S(2)}, u32[]{:S(2)}) collective-permute-start(s32[3,128]{1,0:T(4,128)S(1)} %get-tuple-element.37), channel_id=1, source_target_pairs={{0,1},{1,2},{2,3},{3,4},{4,5},{5,6},{6,7},{7,8},{8,9},{9,10},{10,1... | collective-permute-start | bytes 4616 | tf_op jit(solution)/shard_map/ppermute | solution.py:25
  24.9 0.0 copy-done
  24.9 0.1 dynamic-slice_bitcast_fusion
  25.0 0.7 reshape.8
  25.7 0.1 copy.13
  25.8 0.1 copy.14.scale_ref
  25.9 0.0 collective-permute-done.1.high_ref
  25.9 0.0 collective-permute-done.low_ref
  25.9 0.0 copy-start.1
  25.9 0.8 copy-done.1
  26.7 0.0 copy-start.3
  26.7 0.7 copy-done.3
  27.5 0.0 copy-start.4
  27.5 0.7 copy-done.4
  28.1 1.7 %shard_map.95 = (bf16[8,32,128]{2,1,0:T(8,128)(2,1)S(1)}, bf16[48,2,32,128]{3,2,1,0:T(8,128)(2,1)}) custom-call(s32[8,128]{1,0:T(8,128)S(1)} %copy-done.4, s32[3,128]{1,0:T(4,128)S(1)} %collective-permute-done.low_ref, s32[3,128]{1,0:T(4,128)S(1)} %collective-permute-done.1.high_ref, bf16[32,256]{1,0:T(8,128)(2,1)S(1)} %bitcast.11, ...), custom_call_target="tpu_custom_call" | custom-call | flops 1048576 | bytes 4194304 | tf_op jit(solution)/shard_map/pallas_call | solution.py:197
  29.9 0.0 collective-permute-done.2
  29.9 0.0 copy-start.6
  29.9 0.0 collective-permute-done.3.o0_ref
  29.9 0.8 copy-done.6
  30.6 0.0 all-gather.2.cloned.1.call-update
  30.7 17.4 %all-to-all-start = ((bf16[48,2,32,128]{3,2,1,0:T(8,128)(2,1)}), bf16[48,2,32,128]{3,2,1,0:T(8,128)(2,1)S(1)}, u32[]{:S(2)}, u32[]{:S(2)}) async-start(bf16[48,2,32,128]{3,2,1,0:T(8,128)(2,1)} %get-tuple-element.20), calls=%async_computation | async-start | bytes 1572864 | tf_op jit(solution)/shard_map/all_to_all | solution.py:265
  48.1 1.9 %collective-permute-start.6 = (bf16[128,1536]{1,0:T(8,128)(2,1)S(1)}, bf16[128,1536]{1,0:T(8,128)(2,1)S(1)}, u32[]{:S(2)}, u32[]{:S(2)}) collective-permute-start(bf16[128,1536]{1,0:T(8,128)(2,1)S(1)} %collective-permute-done.3.o0_ref), channel_id=1, source_target_pairs={{578,0},{579,1},{0,192},{1,193},{192,384},{193,385},{384,576},{385... | collective-permute-start | bytes 1179656 | tf_op jit(solution)/shard_map/ppermute | solution.py:233
  50.0 2.8 %collective-permute-start.5 = (bf16[128,1536]{1,0:T(8,128)(2,1)S(1)}, bf16[128,1536]{1,0:T(8,128)(2,1)S(1)}, u32[]{:S(2)}, u32[]{:S(2)}) collective-permute-start(bf16[128,1536]{1,0:T(8,128)(2,1)S(1)} %collective-permute-done.3.o0_ref), channel_id=1, source_target_pairs={{384,0},{387,1},{576,192},{579,193},{2,384},{1,385},{194,576},{193... | collective-permute-start | bytes 1179656 | tf_op jit(solution)/shard_map/ppermute | solution.py:233
  52.9 2.5 %collective-permute-start.4 = (bf16[128,1536]{1,0:T(8,128)(2,1)S(1)}, bf16[128,1536]{1,0:T(8,128)(2,1)S(1)}, u32[]{:S(2)}, u32[]{:S(2)}) collective-permute-start(bf16[128,1536]{1,0:T(8,128)(2,1)S(1)} %collective-permute-done.3.o0_ref), channel_id=1, source_target_pairs={{192,0},{193,1},{384,192},{385,193},{576,384},{577,385},{2,576},{3... | collective-permute-start | bytes 1179656 | tf_op jit(solution)/shard_map/ppermute | solution.py:233
  55.3 13.3 %collective-permute-done.6.o3_ref = bf16[128,1536]{1,0:T(8,128)(2,1)S(1)} collective-permute-done((bf16[128,1536]{1,0:T(8,128)(2,1)S(1)}, bf16[128,1536]{1,0:T(8,128)(2,1)S(1)}, u32[]{:S(2)}, u32[]{:S(2)}) %collective-permute-start.6) | collective-permute-done | bytes 393248 | tf_op jit(solution)/shard_map/ppermute | solution.py:233
  68.6 15.8 %collective-permute-done.5.o2_ref = bf16[128,1536]{1,0:T(8,128)(2,1)S(1)} collective-permute-done((bf16[128,1536]{1,0:T(8,128)(2,1)S(1)}, bf16[128,1536]{1,0:T(8,128)(2,1)S(1)}, u32[]{:S(2)}, u32[]{:S(2)}) %collective-permute-start.5) | collective-permute-done | bytes 393248 | tf_op jit(solution)/shard_map/ppermute | solution.py:233
  84.4 0.0 collective-permute-done.4.o1_ref
  84.4 0.0 all-to-all-done.own_ref
  84.4 0.0 all-gather.2.cloned.1.call-done.in_ref
  84.4 1.9 %collective-permute-start.7 = (bf16[48,2,32,128]{3,2,1,0:T(8,128)(2,1)S(1)}, bf16[48,2,32,128]{3,2,1,0:T(8,128)(2,1)S(1)}, u32[]{:S(2)}, u32[]{:S(2)}) collective-permute-start(bf16[48,2,32,128]{3,2,1,0:T(8,128)(2,1)S(1)} %all-to-all-done.own_ref), channel_id=1, source_target_pairs={{0,1},{1,0},{2,3},{3,2},{4,5},{5,4},{6,7},{7,6},{8,9},{9,8},{10,11... | collective-permute-start | bytes 2359304 | tf_op jit(solution)/shard_map/ppermute | solution.py:267
  86.4 2.3 %collective-permute-done.7.oth_ref = bf16[48,2,32,128]{3,2,1,0:T(8,128)(2,1)S(1)} collective-permute-done((bf16[48,2,32,128]{3,2,1,0:T(8,128)(2,1)S(1)}, bf16[48,2,32,128]{3,2,1,0:T(8,128)(2,1)S(1)}, u32[]{:S(2)}, u32[]{:S(2)}) %collective-permute-start.7) | collective-permute-done | bytes 786464 | tf_op jit(solution)/shard_map/ppermute | solution.py:267
  88.6 0.0 copy-done.7
  88.6 0.3 broadcast_in_dim.10.gain_ref
  88.9 0.0 copy-start.5
  88.9 1.4 copy-done.5
  90.3 4.0 %shard_map.96 = (f32[48,2,32,128]{3,2,1,0:T(8,128)S(1)}, bf16[48,2,32,128]{3,2,1,0:T(8,128)(2,1)S(1)}) custom-call(bf16[48,2,32,128]{3,2,1,0:T(8,128)(2,1)S(1)} %all-to-all-done.own_ref, bf16[48,2,32,128]{3,2,1,0:T(8,128)(2,1)S(1)} %collective-permute-done.7.oth_ref, f32[1536,128]{1,0:T(8,128)S(1)} %broadcast_in_dim.10.gain_ref, ...), custom_call_target="tpu_custom_call" | custom-call | flops 1610612736 | bytes 4194304 | tf_op jit(solution)/shard_map/pallas_call | solution.py:197
  94.3 2.0 %collective-permute-start.8 = (bf16[48,2,32,128]{3,2,1,0:T(8,128)(2,1)S(1)}, bf16[48,2,32,128]{3,2,1,0:T(8,128)(2,1)S(1)}, u32[]{:S(2)}, u32[]{:S(2)}) collective-permute-start(bf16[48,2,32,128]{3,2,1,0:T(8,128)(2,1)S(1)} %get-tuple-element.30), channel_id=1, source_target_pairs={{0,1},{1,0},{2,3},{3,2},{4,5},{5,4},{6,7},{7,6},{8,9},{9,8},{10,11... | collective-permute-start | bytes 2359304 | tf_op jit(solution)/shard_map/ppermute | solution.py:287
  96.4 2.1 %collective-permute-done.8 = bf16[48,2,32,128]{3,2,1,0:T(8,128)(2,1)S(1)} collective-permute-done((bf16[48,2,32,128]{3,2,1,0:T(8,128)(2,1)S(1)}, bf16[48,2,32,128]{3,2,1,0:T(8,128)(2,1)S(1)}, u32[]{:S(2)}, u32[]{:S(2)}) %collective-permute-start.8) | collective-permute-done | bytes 786464 | tf_op jit(solution)/shard_map/ppermute | solution.py:287
  98.5 0.3 add_convert_fusion
  98.7 0.0 copy-start.2
  98.8 40.1 %all_to_all.10.got_ref = bf16[48,2,32,128]{3,2,1,0:T(8,128)(2,1)S(1)} all-to-all(bf16[48,2,32,128]{3,2,1,0:T(8,128)(2,1)S(1)} %add_convert_fusion), channel_id=1, replica_groups=mesh['y'=4,'z'=12,'x'=4,'h'=2,'c'=2] {'y','z'}, dimensions={0} | all-to-all | bytes 1572864 | tf_op jit(solution)/shard_map/all_to_all | solution.py:288
  138.9 0.7 shard_map.97
  139.6 11.3 %collective-permute-start.9 = (bf16[3,32,128]{2,1,0:T(8,128)(2,1)S(1)}, bf16[3,32,128]{2,1,0:T(8,128)(2,1)S(1)}, u32[]{:S(2)}, u32[]{:S(2)}) collective-permute-start(bf16[3,32,128]{2,1,0:T(8,128)(2,1)S(1)} %get-tuple-element.34), channel_id=1, source_target_pairs={{0,1},{1,2},{2,3},{3,4},{4,5},{5,6},{6,7},{7,8},{8,9},{9,10},{10,1... | collective-permute-start | bytes 73736 | tf_op jit(solution)/shard_map/ppermute | solution.py:25
  150.9 1.9 %collective-permute-start.10 = (bf16[3,32,128]{2,1,0:T(8,128)(2,1)S(1)}, bf16[3,32,128]{2,1,0:T(8,128)(2,1)S(1)}, u32[]{:S(2)}, u32[]{:S(2)}) collective-permute-start(bf16[3,32,128]{2,1,0:T(8,128)(2,1)S(1)} %get-tuple-element.35), channel_id=1, source_target_pairs={{1,0},{2,1},{3,2},{4,3},{5,4},{6,5},{7,6},{8,7},{9,8},{10,9},{11,1... | collective-permute-start | bytes 73736 | tf_op jit(solution)/shard_map/ppermute | solution.py:25
  152.9 0.0 collective-permute-done.9.low_ref
  152.9 8.0 %collective-permute-done.10.high_ref = bf16[3,32,128]{2,1,0:T(8,128)(2,1)S(1)} collective-permute-done((bf16[3,32,128]{2,1,0:T(8,128)(2,1)S(1)}, bf16[3,32,128]{2,1,0:T(8,128)(2,1)S(1)}, u32[]{:S(2)}, u32[]{:S(2)}) %collective-permute-start.10) | collective-permute-done | bytes 24608 | tf_op jit(solution)/shard_map/ppermute | solution.py:25
  160.9 0.0 copy-done.2
  160.9 1.3 shard_map.98
Async XLA Ops:
  7.2 17.7 %copy-start = (f32[1536]{0:T(1024)S(1)}, f32[1536]{0:T(1024)}, u32[]{:S(2)}) copy-start(f32[1536]{0:T(1024)} %param.12) | copy-start | bytes 18436
  7.2 81.4 %copy-start.7 = (f32[1536]{0:T(1024)S(1)}, f32[1536]{0:T(1024)}, u32[]{:S(2)}) copy-start(f32[1536]{0:T(1024)} %param.11) | copy-start | bytes 18436
  7.2 77.2 %all-gather.2.cloned.1.call-start = ((), (), s32[]{:S(2)}) async-start(), calls=%async_computation.2 | async-start | bytes 1966080 | tf_op jit(solution)/shard_map/all_gather | solution.py:263
  7.2 22.6 %collective-permute-start.2 = (bf16[1536,128]{1,0:T(8,128)(2,1)}, bf16[1536,128]{1,0:T(8,128)(2,1)S(1)}, u32[]{:S(2)}, u32[]{:S(2)}) collective-permute-start(bf16[1536,128]{1,0:T(8,128)(2,1)} %param.13), channel_id=1, source_target_pairs={{0,0},{16,1},{2,2},{18,3},{196,4},{212,5},{198,6},{214,7},{392,8},... | collective-permute-start | bytes 1179656 | tf_op jit(solution)/shard_map/ppermute | solution.py:219
  11.8 18.1 %collective-permute-start.3 = (bf16[128,1536]{1,0:T(8,128)(2,1)}, bf16[128,1536]{1,0:T(8,128)(2,1)S(1)}, u32[]{:S(2)}, u32[]{:S(2)}) collective-permute-start(bf16[128,1536]{1,0:T(8,128)(2,1)} %param.14), channel_id=1, source_target_pairs={{0,0},{16,1},{2,2},{18,3},{4,4},{20,5},{6,6},{22,7},{8,8},{24,9},{... | collective-permute-start | bytes 1179656 | tf_op jit(solution)/shard_map/ppermute | solution.py:219
  14.5 11.4 %collective-permute-start.1 = (s32[3,128]{1,0:T(4,128)S(1)}, s32[3,128]{1,0:T(4,128)S(1)}, u32[]{:S(2)}, u32[]{:S(2)}) collective-permute-start(s32[3,128]{1,0:T(4,128)S(1)} %get-tuple-element.36), channel_id=1, source_target_pairs={{1,0},{2,1},{3,2},{4,3},{5,4},{6,5},{7,6},{8,7},{9,8},{10,9},{11,1... | collective-permute-start | bytes 4616 | tf_op jit(solution)/shard_map/ppermute | solution.py:25
  16.4 9.5 %collective-permute-start = (s32[3,128]{1,0:T(4,128)S(1)}, s32[3,128]{1,0:T(4,128)S(1)}, u32[]{:S(2)}, u32[]{:S(2)}) collective-permute-start(s32[3,128]{1,0:T(4,128)S(1)} %get-tuple-element.37), channel_id=1, source_target_pairs={{0,1},{1,2},{2,3},{3,4},{4,5},{5,6},{6,7},{7,8},{8,9},{9,10},{10,1... | collective-permute-start | bytes 4616 | tf_op jit(solution)/shard_map/ppermute | solution.py:25
  25.9 0.8 copy-start.1
  26.7 0.7 copy-start.3
  27.5 0.7 copy-start.4
  29.9 0.8 copy-start.6
  30.7 53.7 %all-to-all-start = ((bf16[48,2,32,128]{3,2,1,0:T(8,128)(2,1)}), bf16[48,2,32,128]{3,2,1,0:T(8,128)(2,1)S(1)}, u32[]{:S(2)}, u32[]{:S(2)}) async-start(bf16[48,2,32,128]{3,2,1,0:T(8,128)(2,1)} %get-tuple-element.20), calls=%async_computation | async-start | bytes 1572864 | tf_op jit(solution)/shard_map/all_to_all | solution.py:265
  48.1 20.5 %collective-permute-start.6 = (bf16[128,1536]{1,0:T(8,128)(2,1)S(1)}, bf16[128,1536]{1,0:T(8,128)(2,1)S(1)}, u32[]{:S(2)}, u32[]{:S(2)}) collective-permute-start(bf16[128,1536]{1,0:T(8,128)(2,1)S(1)} %collective-permute-done.3.o0_ref), channel_id=1, source_target_pairs={{578,0},{579,1},{0,192},{1,193},{192,384},{193,385},{384,576},{385... | collective-permute-start | bytes 1179656 | tf_op jit(solution)/shard_map/ppermute | solution.py:233
  50.0 34.4 %collective-permute-start.5 = (bf16[128,1536]{1,0:T(8,128)(2,1)S(1)}, bf16[128,1536]{1,0:T(8,128)(2,1)S(1)}, u32[]{:S(2)}, u32[]{:S(2)}) collective-permute-start(bf16[128,1536]{1,0:T(8,128)(2,1)S(1)} %collective-permute-done.3.o0_ref), channel_id=1, source_target_pairs={{384,0},{387,1},{576,192},{579,193},{2,384},{1,385},{194,576},{193... | collective-permute-start | bytes 1179656 | tf_op jit(solution)/shard_map/ppermute | solution.py:233
  52.9 31.6 %collective-permute-start.4 = (bf16[128,1536]{1,0:T(8,128)(2,1)S(1)}, bf16[128,1536]{1,0:T(8,128)(2,1)S(1)}, u32[]{:S(2)}, u32[]{:S(2)}) collective-permute-start(bf16[128,1536]{1,0:T(8,128)(2,1)S(1)} %collective-permute-done.3.o0_ref), channel_id=1, source_target_pairs={{192,0},{193,1},{384,192},{385,193},{576,384},{577,385},{2,576},{3... | collective-permute-start | bytes 1179656 | tf_op jit(solution)/shard_map/ppermute | solution.py:233
  84.4 4.2 %collective-permute-start.7 = (bf16[48,2,32,128]{3,2,1,0:T(8,128)(2,1)S(1)}, bf16[48,2,32,128]{3,2,1,0:T(8,128)(2,1)S(1)}, u32[]{:S(2)}, u32[]{:S(2)}) collective-permute-start(bf16[48,2,32,128]{3,2,1,0:T(8,128)(2,1)S(1)} %all-to-all-done.own_ref), channel_id=1, source_target_pairs={{0,1},{1,0},{2,3},{3,2},{4,5},{5,4},{6,7},{7,6},{8,9},{9,8},{10,11... | collective-permute-start | bytes 2359304 | tf_op jit(solution)/shard_map/ppermute | solution.py:267
  88.9 1.4 copy-start.5
  94.3 4.2 %collective-permute-start.8 = (bf16[48,2,32,128]{3,2,1,0:T(8,128)(2,1)S(1)}, bf16[48,2,32,128]{3,2,1,0:T(8,128)(2,1)S(1)}, u32[]{:S(2)}, u32[]{:S(2)}) collective-permute-start(bf16[48,2,32,128]{3,2,1,0:T(8,128)(2,1)S(1)} %get-tuple-element.30), channel_id=1, source_target_pairs={{0,1},{1,0},{2,3},{3,2},{4,5},{5,4},{6,7},{7,6},{8,9},{9,8},{10,11... | collective-permute-start | bytes 2359304 | tf_op jit(solution)/shard_map/ppermute | solution.py:287
  98.7 62.1 %copy-start.2 = (bf16[8,128,32]{1,2,0:T(8,128)(2,1)S(1)}, bf16[8,128,32]{1,2,0:T(8,128)(2,1)}, u32[]{:S(2)}) copy-start(bf16[8,128,32]{1,2,0:T(8,128)(2,1)} %param.15) | copy-start | bytes 196612
  139.6 13.2 %collective-permute-start.9 = (bf16[3,32,128]{2,1,0:T(8,128)(2,1)S(1)}, bf16[3,32,128]{2,1,0:T(8,128)(2,1)S(1)}, u32[]{:S(2)}, u32[]{:S(2)}) collective-permute-start(bf16[3,32,128]{2,1,0:T(8,128)(2,1)S(1)} %get-tuple-element.34), channel_id=1, source_target_pairs={{0,1},{1,2},{2,3},{3,4},{4,5},{5,6},{6,7},{7,8},{8,9},{9,10},{10,1... | collective-permute-start | bytes 73736 | tf_op jit(solution)/shard_map/ppermute | solution.py:25
  150.9 10.0 %collective-permute-start.10 = (bf16[3,32,128]{2,1,0:T(8,128)(2,1)S(1)}, bf16[3,32,128]{2,1,0:T(8,128)(2,1)S(1)}, u32[]{:S(2)}, u32[]{:S(2)}) collective-permute-start(bf16[3,32,128]{2,1,0:T(8,128)(2,1)S(1)} %get-tuple-element.35), channel_id=1, source_target_pairs={{1,0},{2,1},{3,2},{4,3},{5,4},{6,5},{7,6},{8,7},{9,8},{10,9},{11,1... | collective-permute-start | bytes 73736 | tf_op jit(solution)/shard_map/ppermute | solution.py:25
Sparse Core Ops, SparseCore 0:
  30.8 45.0 all-gather.1

commit v7 on v5

--- a/solution.py
+++ b/solution.py
@@ -207,28 +207,32 @@
     )(*args)
 
 
-def shifted(shard):
+def moved(shard, k):
     ny, nz, nx, nh, nc = (lax.axis_size(a) for a in AXES)
-    count = ny * nh
 
     def place(y, z, x, h, c):
         return (((y * nz + z) * nx + x) * nh + h) * nc + c
 
     pairs = []
     for y, z, x, h, c in itertools.product(*[range(n) for n in (ny, nz, nx, nh, nc)]):
-        turn = x % ny
-        if 2 * turn > ny or (2 * turn == ny and c):
-            turn -= ny
-        spot = (h * ny + y + turn) % count
+        spot = (h * ny + y + turns(k, c)) % (ny * nh)
         other = (z, c) if z % 2 == c else (z ^ 1, 1 - c)
         pairs.append((place(spot % ny, other[0], x, spot // ny, other[1]), place(y, z, x, h, c)))
     return lax.ppermute(shard, AXES, pairs)
 
 
-def gathered(shard):
-    nx = lax.axis_size("x")
-    others = [lax.ppermute(shard, "x", [((i + k) % nx, i) for i in range(nx)]) for k in (2, 1, 3)]
-    return [shard, *others]
+def turns(k, c):
+    return (0, 1, -2 if c else 2, -1)[k]
+
+
+def from_ring(shard, k):
+    nh, ny = lax.axis_size("h"), lax.axis_size("y")
+    ring = [y * nh + h for h in range(nh) for y in range(ny)]
+    count = len(ring)
+    pairs = [
+        (ring[(i + turns(k, c)) % count] * 2 + c, ring[i] * 2 + c) for i in range(count) for c in range(2)
+    ]
+    return lax.ppermute(shard, ("y", "h", "c"), pairs)
 
 
 def on_device(
@@ -242,7 +246,8 @@
     hid = w_out.shape[0] * lax.axis_size("y")
     swap = [(0, 1), (1, 0)]
 
-    both = shifted(jnp.stack([w_in.T, w_out]))
+    both = jnp.stack([w_in.T, w_out])
+    near, far = moved(both, 0), moved(both, 2)
     low, high = edges(floor_tokens[:3] + 1, floor_tokens[rows - 3 :] + 1)
     taps = depth_kernel.reshape(49, chans).T
     scale = lax.dynamic_slice_in_dim(layer_scale, lax.axis_index(CHAN) * chans, chans, 0)[:, None]
@@ -256,8 +261,8 @@
         [(tile, BF16), (packed, BF16)],
         (floor_tokens, low, high, token_table.T, taps, scale, grad_local),
     )
-    send, both = lax.optimization_barrier((send, both))
-    weights = gathered(both)
+    send, near, far = lax.optimization_barrier((send, near, far))
+    weights = [near, far, from_ring(near, 1), from_ring(near, 3)]
     own = lax.all_to_all(send, CHAN, 0, 0, tiled=True)
     oth = lax.ppermute(own, "c", swap)
     keep, sib = call(

time: 162 us -> 160 us (0.988)
  blocking collectives: 40.3 us -> 37.1 us
  starting transfers between devices: 64.6 us -> 66.4 us
    ppermute x2, waiting for transfers between devices: 17.3 us -> 8.02 us  [edges(): lax.ppermute(low_side, SPACE, backward)]
    all_to_all x1, waiting for transfers between devices: 15.5 us -> 22.9 us  [on_device(): own = lax.all_to_all(send, CHAN, 0, 0, tiled=True)]
    ppermute x1, starting transfers between devices: 1.91 us -> 8.19 us  [on_device(): oth = lax.ppermute(own, 'c', swap)]
    ppermute x1, starting transfers between devices: 5.95 us -> 2.28 us  [on_device(): part = (keep + lax.ppermute(sib, 'c', swap).astype(F32)).astype(BF16)]
    all_to_all x1, blocking collectives: 40.3 us -> 37.1 us  [on_device(): got = lax.all_to_all(part, CHAN, 0, 0, tiled=True)]
    ppermute x1, waiting for transfers between devices: 0.01 us -> 1.87 us  [on_device(): oth = lax.ppermute(own, 'c', swap)]
    all_to_all x1, starting transfers between devices: 17.7 us -> 19.4 us  [on_device(): own = lax.all_to_all(send, CHAN, 0, 0, tiled=True)]
  transfers between devices with their start and end apart: 11 -> 11, of which waited for: 5 -> 7; matrix products, arithmetic and copies ran while one was open for 0% -> 0% of each run, Pallas kernels for 1% -> 1%
where the time goes in v7:
time: 160 us; the launch traced here: 159 us
  starting transfers between devices  66.4 us (42%)
  waiting for transfers between devices  43.7 us (27%)
  blocking collectives  37.1 us (23%)
  Pallas kernels  8.02 us (5%)
  local copies, waits for them, and re-layouts  1.77 us (1%)
    all_to_all x1, blocking collectives, on_device(): got = lax.all_to_all(part, CHAN, 0, 0, tiled=True)  37.1 us
    all_to_all x1, waiting for transfers between devices, on_device(): own = lax.all_to_all(send, CHAN, 0, 0, tiled=True)  22.9 us
    all_to_all x1, starting transfers between devices, on_device(): own = lax.all_to_all(send, CHAN, 0, 0, tiled=True)  19.4 us
    ppermute x2, starting transfers between devices, edges(): lax.ppermute(high_side, SPACE, forward)  19.4 us
    ppermute x2, waiting for transfers between devices, moved(): return lax.ppermute(shard, AXES, pairs)  8.68 us
    ppermute x1, starting transfers between devices, on_device(): oth = lax.ppermute(own, 'c', swap)  8.19 us
    ppermute x2, starting transfers between devices, moved(): return lax.ppermute(shard, AXES, pairs)  8.05 us
    pallas_call x4, Pallas kernels, call(): pl.pallas_call(body, out_shape=outs, in_specs=specs or [VMEM] * len(args)...  8.02 us
  transfers between devices with their start and end apart: 11, of which 7 were waited for; matrix products, arithmetic and copies ran while one was open for 0% of the time, Pallas kernels for 1%

profile of v7, /device:TPU:57, one launch (start us, length us, event | category | flops | bytes accessed | tf_op | source)
XLA Modules:
  0.0 159.2 jit_solution(14462159368416159022)
XLA Ops:
  0.6 0.0 copy-start
  0.6 0.0 copy-start.3
  0.7 0.0 copy-start.4
  0.7 0.0 copy-start.1
  0.7 0.0 copy-start.2
  0.7 1.2 copy.16
  1.9 0.0 copy-start.5
  1.9 1.1 pad_maximum_fusion
  3.0 6.1 %collective-permute-start.3 = (bf16[2,128,1536]{2,1,0:T(8,128)(2,1)S(1)}, bf16[2,128,1536]{2,1,0:T(8,128)(2,1)S(1)}, u32[]{:S(2)}, u32[]{:S(2)}) collective-permute-start(bf16[2,128,1536]{2,1,0:T(8,128)(2,1)S(1)} %pad_maximum_fusion), channel_id=1, source_target_pairs={{384,0},{402,1},{386,2},{400,3},{388,4},{406,5},{390,6},{404,7},{3... | collective-permute-start | bytes 2359304 | tf_op jit(solution)/shard_map/ppermute | solution.py:221
  9.1 1.9 %collective-permute-start.2 = (bf16[2,128,1536]{2,1,0:T(8,128)(2,1)S(1)}, bf16[2,128,1536]{2,1,0:T(8,128)(2,1)S(1)}, u32[]{:S(2)}, u32[]{:S(2)}) collective-permute-start(bf16[2,128,1536]{2,1,0:T(8,128)(2,1)S(1)} %pad_maximum_fusion), channel_id=1, source_target_pairs={{0,0},{16,1},{2,2},{18,3},{4,4},{20,5},{6,6},{22,7},{8,8},{24,9},{... | collective-permute-start | bytes 2359304 | tf_op jit(solution)/shard_map/ppermute | solution.py:221
  11.1 0.0 copy-done.3
  11.1 1.9 %collective-permute-start.1 = (s32[3,128]{1,0:T(4,128)S(1)}, s32[3,128]{1,0:T(4,128)S(1)}, u32[]{:S(2)}, u32[]{:S(2)}) collective-permute-start(s32[3,128]{1,0:T(4,128)S(1)} %get-tuple-element.24), channel_id=1, source_target_pairs={{1,0},{2,1},{3,2},{4,3},{5,4},{6,5},{7,6},{8,7},{9,8},{10,9},{11,1... | collective-permute-start | bytes 4616 | tf_op jit(solution)/shard_map/ppermute | solution.py:25
  13.0 8.4 %collective-permute-start = (s32[3,128]{1,0:T(4,128)S(1)}, s32[3,128]{1,0:T(4,128)S(1)}, u32[]{:S(2)}, u32[]{:S(2)}) collective-permute-start(s32[3,128]{1,0:T(4,128)S(1)} %get-tuple-element.25), channel_id=1, source_target_pairs={{0,1},{1,2},{2,3},{3,4},{4,5},{5,6},{6,7},{7,8},{8,9},{9,10},{10,1... | collective-permute-start | bytes 4616 | tf_op jit(solution)/shard_map/ppermute | solution.py:25
  21.5 0.0 copy-done
  21.5 0.1 dynamic-slice_bitcast_fusion
  21.6 0.0 copy-done.4
  21.6 0.1 copy.14
  21.7 0.1 copy.15.scale_ref
  21.8 0.0 collective-permute-done.1.high_ref
  21.8 0.4 collective-permute-done.low_ref
  22.2 0.0 copy-done.1
  22.2 0.0 copy-done.2
  22.2 1.7 %shard_map.95 = (bf16[8,32,128]{2,1,0:T(8,128)(2,1)S(1)}, bf16[48,2,32,128]{3,2,1,0:T(8,128)(2,1)}) custom-call(s32[8,128]{1,0:T(8,128)S(1)} %copy-done.3, s32[3,128]{1,0:T(4,128)S(1)} %collective-permute-done.low_ref, s32[3,128]{1,0:T(4,128)S(1)} %collective-permute-done.1.high_ref, bf16[32,256]{1,0:T(8,128)(2,1)S(1)} %bitcast.15, ...), custom_call_target="tpu_custom_call" | custom-call | flops 1048576 | bytes 4194304 | tf_op jit(solution)/shard_map/pallas_call | solution.py:199
  23.9 2.8 %collective-permute-done.3.w1_ref = bf16[2,128,1536]{2,1,0:T(8,128)(2,1)S(1)} collective-permute-done((bf16[2,128,1536]{2,1,0:T(8,128)(2,1)S(1)}, bf16[2,128,1536]{2,1,0:T(8,128)(2,1)S(1)}, u32[]{:S(2)}, u32[]{:S(2)}) %collective-permute-start.3) | collective-permute-done | bytes 786464 | tf_op jit(solution)/shard_map/ppermute | solution.py:221
  26.7 5.8 %collective-permute-done.2.w0_ref = bf16[2,128,1536]{2,1,0:T(8,128)(2,1)S(1)} collective-permute-done((bf16[2,128,1536]{2,1,0:T(8,128)(2,1)S(1)}, bf16[2,128,1536]{2,1,0:T(8,128)(2,1)S(1)}, u32[]{:S(2)}, u32[]{:S(2)}) %collective-permute-start.2) | collective-permute-done | bytes 786464 | tf_op jit(solution)/shard_map/ppermute | solution.py:221
  32.6 19.4 %all-to-all-start = ((bf16[48,2,32,128]{3,2,1,0:T(8,128)(2,1)}), bf16[48,2,32,128]{3,2,1,0:T(8,128)(2,1)S(1)}, u32[]{:S(2)}, u32[]{:S(2)}) async-start(bf16[48,2,32,128]{3,2,1,0:T(8,128)(2,1)} %get-tuple-element.14), calls=%async_computation | async-start | bytes 1572864 | tf_op jit(solution)/shard_map/all_to_all | solution.py:266
  52.0 1.9 %collective-permute-start.6 = (bf16[2,128,1536]{2,1,0:T(8,128)(2,1)S(1)}, bf16[2,128,1536]{2,1,0:T(8,128)(2,1)S(1)}, u32[]{:S(2)}, u32[]{:S(2)}) collective-permute-start(bf16[2,128,1536]{2,1,0:T(8,128)(2,1)S(1)} %collective-permute-done.2.w0_ref), channel_id=1, source_target_pairs={{578,0},{579,1},{0,192},{1,193},{192,384},{193,385},{384,576},{385... | collective-permute-start | bytes 2359304 | tf_op jit(solution)/shard_map/ppermute | solution.py:235
  53.9 3.4 %collective-permute-start.5 = (bf16[2,128,1536]{2,1,0:T(8,128)(2,1)S(1)}, bf16[2,128,1536]{2,1,0:T(8,128)(2,1)}, u32[]{:S(2)}, u32[]{:S(2)}) collective-permute-start(bf16[2,128,1536]{2,1,0:T(8,128)(2,1)S(1)} %collective-permute-done.2.w0_ref), channel_id=1, source_target_pairs={{192,0},{193,1},{384,192},{385,193},{576,384},{577,385},{2,576},{3... | collective-permute-start | bytes 2359304 | tf_op jit(solution)/shard_map/ppermute | solution.py:235
  57.2 22.9 %all-to-all-done.own_ref = bf16[48,2,32,128]{3,2,1,0:T(8,128)(2,1)S(1)} async-done(((bf16[48,2,32,128]{3,2,1,0:T(8,128)(2,1)}), bf16[48,2,32,128]{3,2,1,0:T(8,128)(2,1)S(1)}, u32[]{:S(2)}, u32[]{:S(2)}) %all-to-all-start) | async-done | bytes 786464 | tf_op jit(solution)/shard_map/all_to_all | solution.py:266
  80.1 8.2 %collective-permute-start.4 = (bf16[48,2,32,128]{3,2,1,0:T(8,128)(2,1)S(1)}, bf16[48,2,32,128]{3,2,1,0:T(8,128)(2,1)S(1)}, u32[]{:S(2)}, u32[]{:S(2)}) collective-permute-start(bf16[48,2,32,128]{3,2,1,0:T(8,128)(2,1)S(1)} %all-to-all-done.own_ref), channel_id=1, source_target_pairs={{0,1},{1,0},{2,3},{3,2},{4,5},{5,4},{6,7},{7,6},{8,9},{9,8},{10,11... | collective-permute-start | bytes 2359304 | tf_op jit(solution)/shard_map/ppermute | solution.py:267
  88.3 0.0 collective-permute-done.6.w3_ref
  88.3 0.0 collective-permute-done.5.w2_ref
  88.3 1.9 %collective-permute-done.4.oth_ref = bf16[48,2,32,128]{3,2,1,0:T(8,128)(2,1)S(1)} collective-permute-done((bf16[48,2,32,128]{3,2,1,0:T(8,128)(2,1)S(1)}, bf16[48,2,32,128]{3,2,1,0:T(8,128)(2,1)S(1)}, u32[]{:S(2)}, u32[]{:S(2)}) %collective-permute-start.4) | collective-permute-done | bytes 786464 | tf_op jit(solution)/shard_map/ppermute | solution.py:267
  90.2 0.0 copy-done.5
  90.2 0.3 broadcast_in_dim.10.gain_ref
  90.5 4.3 %shard_map.96 = (f32[48,2,32,128]{3,2,1,0:T(8,128)S(1)}, bf16[48,2,32,128]{3,2,1,0:T(8,128)(2,1)S(1)}) custom-call(bf16[48,2,32,128]{3,2,1,0:T(8,128)(2,1)S(1)} %all-to-all-done.own_ref, bf16[48,2,32,128]{3,2,1,0:T(8,128)(2,1)S(1)} %collective-permute-done.4.oth_ref, f32[1536,128]{1,0:T(8,128)S(1)} %broadcast_in_dim.10.gain_ref, ...), custom_call_target="tpu_custom_call" | custom-call | flops 1610612736 | bytes 4194304 | tf_op jit(solution)/shard_map/pallas_call | solution.py:199
  94.7 2.3 %collective-permute-start.7 = (bf16[48,2,32,128]{3,2,1,0:T(8,128)(2,1)S(1)}, bf16[48,2,32,128]{3,2,1,0:T(8,128)(2,1)S(1)}, u32[]{:S(2)}, u32[]{:S(2)}) collective-permute-start(bf16[48,2,32,128]{3,2,1,0:T(8,128)(2,1)S(1)} %get-tuple-element.18), channel_id=1, source_target_pairs={{0,1},{1,0},{2,3},{3,2},{4,5},{5,4},{6,7},{7,6},{8,9},{9,8},{10,11... | collective-permute-start | bytes 2359304 | tf_op jit(solution)/shard_map/ppermute | solution.py:287
  97.0 1.9 %collective-permute-done.7 = bf16[48,2,32,128]{3,2,1,0:T(8,128)(2,1)S(1)} collective-permute-done((bf16[48,2,32,128]{3,2,1,0:T(8,128)(2,1)S(1)}, bf16[48,2,32,128]{3,2,1,0:T(8,128)(2,1)S(1)}, u32[]{:S(2)}, u32[]{:S(2)}) %collective-permute-start.7) | collective-permute-done | bytes 786464 | tf_op jit(solution)/shard_map/ppermute | solution.py:287
  98.9 0.3 add_convert_fusion
  99.2 37.1 %all_to_all.10.got_ref = bf16[48,2,32,128]{3,2,1,0:T(8,128)(2,1)S(1)} all-to-all(bf16[48,2,32,128]{3,2,1,0:T(8,128)(2,1)S(1)} %add_convert_fusion), channel_id=1, replica_groups=mesh['y'=4,'z'=12,'x'=4,'h'=2,'c'=2] {'y','z'}, dimensions={0} | all-to-all | bytes 1572864 | tf_op jit(solution)/shard_map/all_to_all | solution.py:288
  136.2 0.7 shard_map.97
  137.0 10.9 %collective-permute-start.8 = (bf16[3,32,128]{2,1,0:T(8,128)(2,1)S(1)}, bf16[3,32,128]{2,1,0:T(8,128)(2,1)S(1)}, u32[]{:S(2)}, u32[]{:S(2)}) collective-permute-start(bf16[3,32,128]{2,1,0:T(8,128)(2,1)S(1)} %get-tuple-element.22), channel_id=1, source_target_pairs={{0,1},{1,2},{2,3},{3,4},{4,5},{5,6},{6,7},{7,8},{8,9},{9,10},{10,1... | collective-permute-start | bytes 73736 | tf_op jit(solution)/shard_map/ppermute | solution.py:25
  147.9 1.9 %collective-permute-start.9 = (bf16[3,32,128]{2,1,0:T(8,128)(2,1)S(1)}, bf16[3,32,128]{2,1,0:T(8,128)(2,1)S(1)}, u32[]{:S(2)}, u32[]{:S(2)}) collective-permute-start(bf16[3,32,128]{2,1,0:T(8,128)(2,1)S(1)} %get-tuple-element.23), channel_id=1, source_target_pairs={{1,0},{2,1},{3,2},{4,3},{5,4},{6,5},{7,6},{8,7},{9,8},{10,9},{11,1... | collective-permute-start | bytes 73736 | tf_op jit(solution)/shard_map/ppermute | solution.py:25
  149.8 0.0 collective-permute-done.8.low_ref
  149.8 8.0 %collective-permute-done.9.high_ref = bf16[3,32,128]{2,1,0:T(8,128)(2,1)S(1)} collective-permute-done((bf16[3,32,128]{2,1,0:T(8,128)(2,1)S(1)}, bf16[3,32,128]{2,1,0:T(8,128)(2,1)S(1)}, u32[]{:S(2)}, u32[]{:S(2)}) %collective-permute-start.9) | collective-permute-done | bytes 24608 | tf_op jit(solution)/shard_map/ppermute | solution.py:25
  157.9 1.3 shard_map.98
  (2 shorter events, 0.0 us)
Async XLA Ops:
  0.6 20.9 %copy-start = (f32[1536]{0:T(1024)S(1)}, f32[1536]{0:T(1024)}, u32[]{:S(2)}) copy-start(f32[1536]{0:T(1024)} %param.12) | copy-start | bytes 18436
  0.6 10.4 %copy-start.3 = (s32[8,128]{1,0:T(8,128)S(1)}, s32[8,128]{1,0:T(8,128)}, u32[]{:S(2)}) copy-start(s32[8,128]{1,0:T(8,128)} %tok_ref.1) | copy-start | bytes 12292
  0.7 20.9 %copy-start.4 = (bf16[7,7,32]{2,1,0:T(8,128)(2,1)S(1)}, bf16[7,7,32]{2,1,0:T(8,128)(2,1)}, u32[]{:S(2)}) copy-start(bf16[7,7,32]{2,1,0:T(8,128)(2,1)} %param.10) | copy-start | bytes 9412
  0.7 21.5 %copy-start.1 = (bf16[8,128,32]{1,2,0:T(8,128)(2,1)S(1)}, bf16[8,128,32]{1,2,0:T(8,128)(2,1)}, u32[]{:S(2)}) copy-start(bf16[8,128,32]{1,2,0:T(8,128)(2,1)} %param.15) | copy-start | bytes 196612
  0.7 21.5 %copy-start.2 = (bf16[256,32]{0,1:T(8,128)(2,1)S(1)}, bf16[256,32]{0,1:T(8,128)(2,1)}, u32[]{:S(2)}) copy-start(bf16[256,32]{0,1:T(8,128)(2,1)} %param.9) | copy-start | bytes 49156
  1.9 88.3 %copy-start.5 = (f32[1536]{0:T(1024)S(1)}, f32[1536]{0:T(1024)}, u32[]{:S(2)}) copy-start(f32[1536]{0:T(1024)} %param.11) | copy-start | bytes 18436
  3.0 23.7 %collective-permute-start.3 = (bf16[2,128,1536]{2,1,0:T(8,128)(2,1)S(1)}, bf16[2,128,1536]{2,1,0:T(8,128)(2,1)S(1)}, u32[]{:S(2)}, u32[]{:S(2)}) collective-permute-start(bf16[2,128,1536]{2,1,0:T(8,128)(2,1)S(1)} %pad_maximum_fusion), channel_id=1, source_target_pairs={{384,0},{402,1},{386,2},{400,3},{388,4},{406,5},{390,6},{404,7},{3... | collective-permute-start | bytes 2359304 | tf_op jit(solution)/shard_map/ppermute | solution.py:221
  9.1 23.4 %collective-permute-start.2 = (bf16[2,128,1536]{2,1,0:T(8,128)(2,1)S(1)}, bf16[2,128,1536]{2,1,0:T(8,128)(2,1)S(1)}, u32[]{:S(2)}, u32[]{:S(2)}) collective-permute-start(bf16[2,128,1536]{2,1,0:T(8,128)(2,1)S(1)} %pad_maximum_fusion), channel_id=1, source_target_pairs={{0,0},{16,1},{2,2},{18,3},{4,4},{20,5},{6,6},{22,7},{8,8},{24,9},{... | collective-permute-start | bytes 2359304 | tf_op jit(solution)/shard_map/ppermute | solution.py:221
  11.1 10.7 %collective-permute-start.1 = (s32[3,128]{1,0:T(4,128)S(1)}, s32[3,128]{1,0:T(4,128)S(1)}, u32[]{:S(2)}, u32[]{:S(2)}) collective-permute-start(s32[3,128]{1,0:T(4,128)S(1)} %get-tuple-element.24), channel_id=1, source_target_pairs={{1,0},{2,1},{3,2},{4,3},{5,4},{6,5},{7,6},{8,7},{9,8},{10,9},{11,1... | collective-permute-start | bytes 4616 | tf_op jit(solution)/shard_map/ppermute | solution.py:25
  13.0 9.2 %collective-permute-start = (s32[3,128]{1,0:T(4,128)S(1)}, s32[3,128]{1,0:T(4,128)S(1)}, u32[]{:S(2)}, u32[]{:S(2)}) collective-permute-start(s32[3,128]{1,0:T(4,128)S(1)} %get-tuple-element.25), channel_id=1, source_target_pairs={{0,1},{1,2},{2,3},{3,4},{4,5},{5,6},{6,7},{7,8},{8,9},{9,10},{10,1... | collective-permute-start | bytes 4616 | tf_op jit(solution)/shard_map/ppermute | solution.py:25
  32.6 47.5 %all-to-all-start = ((bf16[48,2,32,128]{3,2,1,0:T(8,128)(2,1)}), bf16[48,2,32,128]{3,2,1,0:T(8,128)(2,1)S(1)}, u32[]{:S(2)}, u32[]{:S(2)}) async-start(bf16[48,2,32,128]{3,2,1,0:T(8,128)(2,1)} %get-tuple-element.14), calls=%async_computation | async-start | bytes 1572864 | tf_op jit(solution)/shard_map/all_to_all | solution.py:266
  52.0 36.4 %collective-permute-start.6 = (bf16[2,128,1536]{2,1,0:T(8,128)(2,1)S(1)}, bf16[2,128,1536]{2,1,0:T(8,128)(2,1)S(1)}, u32[]{:S(2)}, u32[]{:S(2)}) collective-permute-start(bf16[2,128,1536]{2,1,0:T(8,128)(2,1)S(1)} %collective-permute-done.2.w0_ref), channel_id=1, source_target_pairs={{578,0},{579,1},{0,192},{1,193},{192,384},{193,385},{384,576},{385... | collective-permute-start | bytes 2359304 | tf_op jit(solution)/shard_map/ppermute | solution.py:235
  53.9 34.4 %collective-permute-start.5 = (bf16[2,128,1536]{2,1,0:T(8,128)(2,1)S(1)}, bf16[2,128,1536]{2,1,0:T(8,128)(2,1)}, u32[]{:S(2)}, u32[]{:S(2)}) collective-permute-start(bf16[2,128,1536]{2,1,0:T(8,128)(2,1)S(1)} %collective-permute-done.2.w0_ref), channel_id=1, source_target_pairs={{192,0},{193,1},{384,192},{385,193},{576,384},{577,385},{2,576},{3... | collective-permute-start | bytes 2359304 | tf_op jit(solution)/shard_map/ppermute | solution.py:235
  80.1 10.1 %collective-permute-start.4 = (bf16[48,2,32,128]{3,2,1,0:T(8,128)(2,1)S(1)}, bf16[48,2,32,128]{3,2,1,0:T(8,128)(2,1)S(1)}, u32[]{:S(2)}, u32[]{:S(2)}) collective-permute-start(bf16[48,2,32,128]{3,2,1,0:T(8,128)(2,1)S(1)} %all-to-all-done.own_ref), channel_id=1, source_target_pairs={{0,1},{1,0},{2,3},{3,2},{4,5},{5,4},{6,7},{7,6},{8,9},{9,8},{10,11... | collective-permute-start | bytes 2359304 | tf_op jit(solution)/shard_map/ppermute | solution.py:267
  94.7 4.2 %collective-permute-start.7 = (bf16[48,2,32,128]{3,2,1,0:T(8,128)(2,1)S(1)}, bf16[48,2,32,128]{3,2,1,0:T(8,128)(2,1)S(1)}, u32[]{:S(2)}, u32[]{:S(2)}) collective-permute-start(bf16[48,2,32,128]{3,2,1,0:T(8,128)(2,1)S(1)} %get-tuple-element.18), channel_id=1, source_target_pairs={{0,1},{1,0},{2,3},{3,2},{4,5},{5,4},{6,7},{7,6},{8,9},{9,8},{10,11... | collective-permute-start | bytes 2359304 | tf_op jit(solution)/shard_map/ppermute | solution.py:287
  137.0 12.8 %collective-permute-start.8 = (bf16[3,32,128]{2,1,0:T(8,128)(2,1)S(1)}, bf16[3,32,128]{2,1,0:T(8,128)(2,1)S(1)}, u32[]{:S(2)}, u32[]{:S(2)}) collective-permute-start(bf16[3,32,128]{2,1,0:T(8,128)(2,1)S(1)} %get-tuple-element.22), channel_id=1, source_target_pairs={{0,1},{1,2},{2,3},{3,4},{4,5},{5,6},{6,7},{7,8},{8,9},{9,10},{10,1... | collective-permute-start | bytes 73736 | tf_op jit(solution)/shard_map/ppermute | solution.py:25
  147.9 10.0 %collective-permute-start.9 = (bf16[3,32,128]{2,1,0:T(8,128)(2,1)S(1)}, bf16[3,32,128]{2,1,0:T(8,128)(2,1)S(1)}, u32[]{:S(2)}, u32[]{:S(2)}) collective-permute-start(bf16[3,32,128]{2,1,0:T(8,128)(2,1)S(1)} %get-tuple-element.23), channel_id=1, source_target_pairs={{1,0},{2,1},{3,2},{4,3},{5,4},{6,5},{7,6},{8,7},{9,8},{10,9},{11,1... | collective-permute-start | bytes 73736 | tf_op jit(solution)/shard_map/ppermute | solution.py:25

commit v8 on v7

--- a/solution.py
+++ b/solution.py
@@ -79,15 +79,21 @@
     conv_rows(framed, taps_ref, False, emit)
 
 
+def join_kernel(near_ref, far_ref, out_ref):
+    out_ref[0] = near_ref[...]
+    out_ref[1] = far_ref[...]
+
+
 def middle_kernel(
-    own_ref, oth_ref, gain_ref, w0_ref, w1_ref, w2_ref, w3_ref,
+    own_ref, oth_ref, gain_ref, w0_ref, w1_ref, w2_ref,
     keep_ref, sib_ref,
     win, wout, scaled, gmix, normed, grads, act, gpre, sem,
 ):
     blocks, _, chans, cols = own_ref.shape
     width = blocks * chans
     hid = w0_ref.shape[1]
-    pieces = [(ref.at[0], ref.at[1]) for ref in (w0_ref, w1_ref, w2_ref, w3_ref)]
+    shards = (w0_ref, w1_ref, w2_ref.at[0], w2_ref.at[1])
+    pieces = [(ref.at[0], ref.at[1]) for ref in shards]
     copies = []
     for i, (a, b) in enumerate(pieces):
         spot = pl.ds(i * hid, hid)
@@ -261,15 +267,17 @@
         [(tile, BF16), (packed, BF16)],
         (floor_tokens, low, high, token_table.T, taps, scale, grad_local),
     )
-    send, near, far = lax.optimization_barrier((send, near, far))
-    weights = [near, far, from_ring(near, 1), from_ring(near, 3)]
+    weights = [from_ring(near, 1), from_ring(near, 3)]
     own = lax.all_to_all(send, CHAN, 0, 0, tiled=True)
+    (joined,) = call(join_kernel, [((2, 2, *w_out.shape), BF16)], (near, far), flops=20 << 30)
+    own, joined = lax.optimization_barrier((own, joined))
+    weights.append(joined)
     oth = lax.ppermute(own, "c", swap)
     keep, sib = call(
         middle_kernel,
         [(packed, F32), (packed, BF16)],
         (own, oth, gain, *weights),
-        [VMEM] * 3 + [ANY] * 4,
+        [VMEM] * 3 + [ANY] * 3,
         [
             pltpu.VMEM((hid, width), BF16),
             pltpu.VMEM((hid, width), BF16),

time: 160 us -> 158 us (0.988)
  waiting for transfers between devices: 43.7 us -> 35.3 us
  local copies, waits for them, and re-layouts: 1.77 us -> 4.33 us
  starting transfers between devices: 66.4 us -> 68.5 us
    ppermute x2, waiting for transfers between devices: 8.68 us -> 0.01 us  [moved(): return lax.ppermute(shard, AXES, pairs)]
    all_to_all x1, starting transfers between devices: 19.4 us -> 23.4 us  [on_device(): own = lax.all_to_all(send, CHAN, 0, 0, tiled=True)]
    unnamed x13 -> x17, local copies, waits for them, and re-layouts: 1.24 us -> 3.8 us
    ppermute x2, waiting for transfers between devices: 8.02 us -> 10 us  [edges(): lax.ppermute(low_side, SPACE, backward)]
    ppermute x2, starting transfers between devices: 19.4 us -> 17.4 us  [edges(): lax.ppermute(high_side, SPACE, forward)]
    pallas_call x4 -> x5, Pallas kernels: 8.02 us -> 8.1 us  [call(): pl.pallas_call(body, out_shape=outs, in_specs=specs or [VMEM] * len(args)...]
  transfers between devices with their start and end apart: 11 -> 11, of which waited for: 7 -> 5; matrix products, arithmetic and copies ran while one was open for 0% -> 0% of each run, Pallas kernels for 1% -> 1%
where the time goes in v8:
time: 158 us; the launch traced here: 156 us
  starting transfers between devices  68.5 us (43%)
  blocking collectives  37.1 us (23%)
  waiting for transfers between devices  35.3 us (22%)
  Pallas kernels  8.1 us (5%)
  local copies, waits for them, and re-layouts  4.33 us (3%)
  other arithmetic  2.21 us (1%)
    all_to_all x1, blocking collectives, on_device(): got = lax.all_to_all(part, CHAN, 0, 0, tiled=True)  37.1 us
    all_to_all x1, starting transfers between devices, on_device(): own = lax.all_to_all(send, CHAN, 0, 0, tiled=True)  23.4 us
    all_to_all x1, waiting for transfers between devices, on_device(): own = lax.all_to_all(send, CHAN, 0, 0, tiled=True)  21.5 us
    ppermute x2, starting transfers between devices, edges(): lax.ppermute(high_side, SPACE, forward)  17.4 us
    ppermute x2, waiting for transfers between devices, edges(): lax.ppermute(low_side, SPACE, backward)  10 us
    ppermute x1, starting transfers between devices, on_device(): oth = lax.ppermute(own, 'c', swap)  8.24 us
    pallas_call x5, Pallas kernels, call(): pl.pallas_call(body, out_shape=outs, in_specs=specs or [VMEM] * len(args)...  8.1 us
    ppermute x2, starting transfers between devices, moved(): return lax.ppermute(shard, AXES, pairs)  8.04 us
  transfers between devices with their start and end apart: 11, of which 5 were waited for; matrix products, arithmetic and copies ran while one was open for 0% of the time, Pallas kernels for 1%

profile of v8, /device:TPU:57, one launch (start us, length us, event | category | flops | bytes accessed | tf_op | source)
XLA Modules:
  0.0 156.5 jit_solution(3316234954509971744)
XLA Ops:
  0.6 0.0 copy-start
  0.6 0.0 copy-start.3
  0.7 0.0 copy-start.6
  0.7 0.0 copy-start.1
  0.7 0.0 copy-start.2
  0.7 1.2 copy.16
  1.9 2.0 %pad_maximum_fusion = bf16[2,128,1536]{2,1,0:T(8,128)(2,1)} fusion(bf16[1,128,1536]{2,1,0:T(8,128)(2,1)} %bitcast.17, bf16[1,128,1536]{2,1,0:T(8,128)(2,1)S(1)} %bitcast.16), kind=kLoop, calls=%fused_computation.1 | loop fusion | flops 393216 | bytes 1572864 | tf_op jit(solution)/shard_map/stack | solution.py:255
  3.9 4.5 %collective-permute-start.2 = (bf16[2,128,1536]{2,1,0:T(8,128)(2,1)}, bf16[2,128,1536]{2,1,0:T(8,128)(2,1)S(1)}, u32[]{:S(2)}, u32[]{:S(2)}) collective-permute-start(bf16[2,128,1536]{2,1,0:T(8,128)(2,1)} %pad_maximum_fusion), channel_id=1, source_target_pairs={{0,0},{16,1},{2,2},{18,3},{4,4},{20,5},{6,6},{22,7},{8,8},{24,9},{... | collective-permute-start | bytes 2359304 | tf_op jit(solution)/shard_map/ppermute | solution.py:227
  8.4 3.5 %collective-permute-start.3 = (bf16[2,128,1536]{2,1,0:T(8,128)(2,1)}, bf16[2,128,1536]{2,1,0:T(8,128)(2,1)S(1)}, u32[]{:S(2)}, u32[]{:S(2)}) collective-permute-start(bf16[2,128,1536]{2,1,0:T(8,128)(2,1)} %pad_maximum_fusion), channel_id=1, source_target_pairs={{384,0},{402,1},{386,2},{400,3},{388,4},{406,5},{390,6},{404,7},{3... | collective-permute-start | bytes 2359304 | tf_op jit(solution)/shard_map/ppermute | solution.py:227
  11.9 0.0 copy-done.3
  11.9 1.9 %collective-permute-start.1 = (s32[3,128]{1,0:T(4,128)S(1)}, s32[3,128]{1,0:T(4,128)S(1)}, u32[]{:S(2)}, u32[]{:S(2)}) collective-permute-start(s32[3,128]{1,0:T(4,128)S(1)} %get-tuple-element.22), channel_id=1, source_target_pairs={{1,0},{2,1},{3,2},{4,3},{5,4},{6,5},{7,6},{8,7},{9,8},{10,9},{11,1... | collective-permute-start | bytes 4616 | tf_op jit(solution)/shard_map/ppermute | solution.py:25
  13.9 8.4 %collective-permute-start = (s32[3,128]{1,0:T(4,128)S(1)}, s32[3,128]{1,0:T(4,128)S(1)}, u32[]{:S(2)}, u32[]{:S(2)}) collective-permute-start(s32[3,128]{1,0:T(4,128)S(1)} %get-tuple-element.23), channel_id=1, source_target_pairs={{0,1},{1,2},{2,3},{3,4},{4,5},{5,6},{6,7},{7,8},{8,9},{9,10},{10,1... | collective-permute-start | bytes 4616 | tf_op jit(solution)/shard_map/ppermute | solution.py:25
  22.3 0.0 copy-done
  22.4 0.1 dynamic-slice_bitcast_fusion
  22.4 0.0 copy-done.6
  22.4 0.1 copy.14
  22.5 0.1 copy.15.scale_ref
  22.6 2.0 %collective-permute-done.1.high_ref = s32[3,128]{1,0:T(4,128)S(1)} collective-permute-done((s32[3,128]{1,0:T(4,128)S(1)}, s32[3,128]{1,0:T(4,128)S(1)}, u32[]{:S(2)}, u32[]{:S(2)}) %collective-permute-start.1) | collective-permute-done | bytes 1568 | tf_op jit(solution)/shard_map/ppermute | solution.py:25
  24.6 0.0 collective-permute-done.low_ref
  24.6 0.0 copy-done.1
  24.6 0.0 copy-done.2
  24.7 1.7 %shard_map.95 = (bf16[8,32,128]{2,1,0:T(8,128)(2,1)S(1)}, bf16[48,2,32,128]{3,2,1,0:T(8,128)(2,1)}) custom-call(s32[8,128]{1,0:T(8,128)S(1)} %copy-done.3, s32[3,128]{1,0:T(4,128)S(1)} %collective-permute-done.low_ref, s32[3,128]{1,0:T(4,128)S(1)} %collective-permute-done.1.high_ref, bf16[32,256]{1,0:T(8,128)(2,1)S(1)} %bitcast.15, ...), custom_call_target="tpu_custom_call" | custom-call | flops 1048576 | bytes 4194304 | tf_op jit(solution)/shard_map/pallas_call | solution.py:205
  26.4 23.4 %all-to-all-start = ((bf16[48,2,32,128]{3,2,1,0:T(8,128)(2,1)}), bf16[48,2,32,128]{3,2,1,0:T(8,128)(2,1)S(1)}, u32[]{:S(2)}, u32[]{:S(2)}) async-start(bf16[48,2,32,128]{3,2,1,0:T(8,128)(2,1)} %get-tuple-element.12), calls=%async_computation | async-start | bytes 1572864 | tf_op jit(solution)/shard_map/all_to_all | solution.py:271
  49.8 0.0 copy-start.7
  49.8 0.0 collective-permute-done.2.near_ref
  49.8 1.9 %collective-permute-start.6 = (bf16[2,128,1536]{2,1,0:T(8,128)(2,1)S(1)}, bf16[2,128,1536]{2,1,0:T(8,128)(2,1)S(1)}, u32[]{:S(2)}, u32[]{:S(2)}) collective-permute-start(bf16[2,128,1536]{2,1,0:T(8,128)(2,1)S(1)} %collective-permute-done.2.near_ref), channel_id=1, source_target_pairs={{578,0},{579,1},{0,192},{1,193},{192,384},{193,385},{384,576},{385... | collective-permute-start | bytes 2359304 | tf_op jit(solution)/shard_map/ppermute | solution.py:241
  51.7 3.4 %collective-permute-start.5 = (bf16[2,128,1536]{2,1,0:T(8,128)(2,1)S(1)}, bf16[2,128,1536]{2,1,0:T(8,128)(2,1)}, u32[]{:S(2)}, u32[]{:S(2)}) collective-permute-start(bf16[2,128,1536]{2,1,0:T(8,128)(2,1)S(1)} %collective-permute-done.2.near_ref), channel_id=1, source_target_pairs={{192,0},{193,1},{384,192},{385,193},{576,384},{577,385},{2,576},{3... | collective-permute-start | bytes 2359304 | tf_op jit(solution)/shard_map/ppermute | solution.py:241
  55.1 0.0 collective-permute-done.3.far_ref
  55.1 0.1 shard_map.96.w2_ref
  55.2 0.0 copy-start.4
  55.2 1.2 copy-done.4
  56.4 21.5 %all-to-all-done.own_ref = bf16[48,2,32,128]{3,2,1,0:T(8,128)(2,1)S(1)} async-done(((bf16[48,2,32,128]{3,2,1,0:T(8,128)(2,1)}), bf16[48,2,32,128]{3,2,1,0:T(8,128)(2,1)S(1)}, u32[]{:S(2)}, u32[]{:S(2)}) %all-to-all-start) | async-done | bytes 786464 | tf_op jit(solution)/shard_map/all_to_all | solution.py:271
  77.9 8.2 %collective-permute-start.4 = (bf16[48,2,32,128]{3,2,1,0:T(8,128)(2,1)S(1)}, bf16[48,2,32,128]{3,2,1,0:T(8,128)(2,1)S(1)}, u32[]{:S(2)}, u32[]{:S(2)}) collective-permute-start(bf16[48,2,32,128]{3,2,1,0:T(8,128)(2,1)S(1)} %all-to-all-done.own_ref), channel_id=1, source_target_pairs={{0,1},{1,0},{2,3},{3,2},{4,5},{5,4},{6,7},{7,6},{8,9},{9,8},{10,11... | collective-permute-start | bytes 2359304 | tf_op jit(solution)/shard_map/ppermute | solution.py:275
  86.1 0.0 collective-permute-done.6.w1_ref
  86.1 0.0 collective-permute-done.5.w0_ref
  86.1 1.9 %collective-permute-done.4.oth_ref = bf16[48,2,32,128]{3,2,1,0:T(8,128)(2,1)S(1)} collective-permute-done((bf16[48,2,32,128]{3,2,1,0:T(8,128)(2,1)S(1)}, bf16[48,2,32,128]{3,2,1,0:T(8,128)(2,1)S(1)}, u32[]{:S(2)}, u32[]{:S(2)}) %collective-permute-start.4) | collective-permute-done | bytes 786464 | tf_op jit(solution)/shard_map/ppermute | solution.py:275
  88.0 0.0 copy-done.7
  88.0 0.3 broadcast_in_dim.10.gain_ref
  88.3 0.0 copy-start.5
  88.3 1.4 copy-done.5
  89.7 4.2 %shard_map.97 = (f32[48,2,32,128]{3,2,1,0:T(8,128)S(1)}, bf16[48,2,32,128]{3,2,1,0:T(8,128)(2,1)S(1)}) custom-call(bf16[48,2,32,128]{3,2,1,0:T(8,128)(2,1)S(1)} %all-to-all-done.own_ref, bf16[48,2,32,128]{3,2,1,0:T(8,128)(2,1)S(1)} %collective-permute-done.4.oth_ref, f32[1536,128]{1,0:T(8,128)S(1)} %broadcast_in_dim.10.gain_ref, ...), custom_call_target="tpu_custom_call" | custom-call | flops 1610612736 | bytes 4194304 | tf_op jit(solution)/shard_map/pallas_call | solution.py:205
  93.9 2.3 %collective-permute-start.7 = (bf16[48,2,32,128]{3,2,1,0:T(8,128)(2,1)S(1)}, bf16[48,2,32,128]{3,2,1,0:T(8,128)(2,1)S(1)}, u32[]{:S(2)}, u32[]{:S(2)}) collective-permute-start(bf16[48,2,32,128]{3,2,1,0:T(8,128)(2,1)S(1)} %get-tuple-element.16), channel_id=1, source_target_pairs={{0,1},{1,0},{2,3},{3,2},{4,5},{5,4},{6,7},{7,6},{8,9},{9,8},{10,11... | collective-permute-start | bytes 2359304 | tf_op jit(solution)/shard_map/ppermute | solution.py:295
  96.2 1.9 %collective-permute-done.7 = bf16[48,2,32,128]{3,2,1,0:T(8,128)(2,1)S(1)} collective-permute-done((bf16[48,2,32,128]{3,2,1,0:T(8,128)(2,1)S(1)}, bf16[48,2,32,128]{3,2,1,0:T(8,128)(2,1)S(1)}, u32[]{:S(2)}, u32[]{:S(2)}) %collective-permute-start.7) | collective-permute-done | bytes 786464 | tf_op jit(solution)/shard_map/ppermute | solution.py:295
  98.1 0.3 add_convert_fusion
  98.4 37.1 %all_to_all.10.got_ref = bf16[48,2,32,128]{3,2,1,0:T(8,128)(2,1)S(1)} all-to-all(bf16[48,2,32,128]{3,2,1,0:T(8,128)(2,1)S(1)} %add_convert_fusion), channel_id=1, replica_groups=mesh['y'=4,'z'=12,'x'=4,'h'=2,'c'=2] {'y','z'}, dimensions={0} | all-to-all | bytes 1572864 | tf_op jit(solution)/shard_map/all_to_all | solution.py:296
  135.5 0.7 shard_map.98
  136.2 9.0 %collective-permute-start.8 = (bf16[3,32,128]{2,1,0:T(8,128)(2,1)S(1)}, bf16[3,32,128]{2,1,0:T(8,128)(2,1)S(1)}, u32[]{:S(2)}, u32[]{:S(2)}) collective-permute-start(bf16[3,32,128]{2,1,0:T(8,128)(2,1)S(1)} %get-tuple-element.20), channel_id=1, source_target_pairs={{0,1},{1,2},{2,3},{3,4},{4,5},{5,6},{6,7},{7,8},{8,9},{9,10},{10,1... | collective-permute-start | bytes 73736 | tf_op jit(solution)/shard_map/ppermute | solution.py:25
  145.2 1.9 %collective-permute-start.9 = (bf16[3,32,128]{2,1,0:T(8,128)(2,1)S(1)}, bf16[3,32,128]{2,1,0:T(8,128)(2,1)S(1)}, u32[]{:S(2)}, u32[]{:S(2)}) collective-permute-start(bf16[3,32,128]{2,1,0:T(8,128)(2,1)S(1)} %get-tuple-element.21), channel_id=1, source_target_pairs={{1,0},{2,1},{3,2},{4,3},{5,4},{6,5},{7,6},{8,7},{9,8},{10,9},{11,1... | collective-permute-start | bytes 73736 | tf_op jit(solution)/shard_map/ppermute | solution.py:25
  147.2 0.0 collective-permute-done.8.low_ref
  147.2 8.0 %collective-permute-done.9.high_ref = bf16[3,32,128]{2,1,0:T(8,128)(2,1)S(1)} collective-permute-done((bf16[3,32,128]{2,1,0:T(8,128)(2,1)S(1)}, bf16[3,32,128]{2,1,0:T(8,128)(2,1)S(1)}, u32[]{:S(2)}, u32[]{:S(2)}) %collective-permute-start.9) | collective-permute-done | bytes 24608 | tf_op jit(solution)/shard_map/ppermute | solution.py:25
  155.2 1.3 shard_map.99
  (2 shorter events, 0.0 us)
Async XLA Ops:
  0.6 21.7 %copy-start = (f32[1536]{0:T(1024)S(1)}, f32[1536]{0:T(1024)}, u32[]{:S(2)}) copy-start(f32[1536]{0:T(1024)} %param.12) | copy-start | bytes 18436
  0.6 11.3 %copy-start.3 = (s32[8,128]{1,0:T(8,128)S(1)}, s32[8,128]{1,0:T(8,128)}, u32[]{:S(2)}) copy-start(s32[8,128]{1,0:T(8,128)} %tok_ref.1) | copy-start | bytes 12292
  0.7 21.8 %copy-start.6 = (bf16[7,7,32]{2,1,0:T(8,128)(2,1)S(1)}, bf16[7,7,32]{2,1,0:T(8,128)(2,1)}, u32[]{:S(2)}) copy-start(bf16[7,7,32]{2,1,0:T(8,128)(2,1)} %param.10) | copy-start | bytes 9412
  0.7 24.0 %copy-start.1 = (bf16[8,128,32]{1,2,0:T(8,128)(2,1)S(1)}, bf16[8,128,32]{1,2,0:T(8,128)(2,1)}, u32[]{:S(2)}) copy-start(bf16[8,128,32]{1,2,0:T(8,128)(2,1)} %param.15) | copy-start | bytes 196612
  0.7 24.0 %copy-start.2 = (bf16[256,32]{0,1:T(8,128)(2,1)S(1)}, bf16[256,32]{0,1:T(8,128)(2,1)}, u32[]{:S(2)}) copy-start(bf16[256,32]{0,1:T(8,128)(2,1)} %param.9) | copy-start | bytes 49156
  3.9 45.9 %collective-permute-start.2 = (bf16[2,128,1536]{2,1,0:T(8,128)(2,1)}, bf16[2,128,1536]{2,1,0:T(8,128)(2,1)S(1)}, u32[]{:S(2)}, u32[]{:S(2)}) collective-permute-start(bf16[2,128,1536]{2,1,0:T(8,128)(2,1)} %pad_maximum_fusion), channel_id=1, source_target_pairs={{0,0},{16,1},{2,2},{18,3},{4,4},{20,5},{6,6},{22,7},{8,8},{24,9},{... | collective-permute-start | bytes 2359304 | tf_op jit(solution)/shard_map/ppermute | solution.py:227
  8.4 46.7 %collective-permute-start.3 = (bf16[2,128,1536]{2,1,0:T(8,128)(2,1)}, bf16[2,128,1536]{2,1,0:T(8,128)(2,1)S(1)}, u32[]{:S(2)}, u32[]{:S(2)}) collective-permute-start(bf16[2,128,1536]{2,1,0:T(8,128)(2,1)} %pad_maximum_fusion), channel_id=1, source_target_pairs={{384,0},{402,1},{386,2},{400,3},{388,4},{406,5},{390,6},{404,7},{3... | collective-permute-start | bytes 2359304 | tf_op jit(solution)/shard_map/ppermute | solution.py:227
  11.9 12.7 %collective-permute-start.1 = (s32[3,128]{1,0:T(4,128)S(1)}, s32[3,128]{1,0:T(4,128)S(1)}, u32[]{:S(2)}, u32[]{:S(2)}) collective-permute-start(s32[3,128]{1,0:T(4,128)S(1)} %get-tuple-element.22), channel_id=1, source_target_pairs={{1,0},{2,1},{3,2},{4,3},{5,4},{6,5},{7,6},{8,7},{9,8},{10,9},{11,1... | collective-permute-start | bytes 4616 | tf_op jit(solution)/shard_map/ppermute | solution.py:25
  13.9 10.8 %collective-permute-start = (s32[3,128]{1,0:T(4,128)S(1)}, s32[3,128]{1,0:T(4,128)S(1)}, u32[]{:S(2)}, u32[]{:S(2)}) collective-permute-start(s32[3,128]{1,0:T(4,128)S(1)} %get-tuple-element.23), channel_id=1, source_target_pairs={{0,1},{1,2},{2,3},{3,4},{4,5},{5,6},{6,7},{7,8},{8,9},{9,10},{10,1... | collective-permute-start | bytes 4616 | tf_op jit(solution)/shard_map/ppermute | solution.py:25
  26.4 51.5 %all-to-all-start = ((bf16[48,2,32,128]{3,2,1,0:T(8,128)(2,1)}), bf16[48,2,32,128]{3,2,1,0:T(8,128)(2,1)S(1)}, u32[]{:S(2)}, u32[]{:S(2)}) async-start(bf16[48,2,32,128]{3,2,1,0:T(8,128)(2,1)} %get-tuple-element.12), calls=%async_computation | async-start | bytes 1572864 | tf_op jit(solution)/shard_map/all_to_all | solution.py:271
  49.8 38.2 %copy-start.7 = (f32[1536]{0:T(1024)S(1)}, f32[1536]{0:T(1024)}, u32[]{:S(2)}) copy-start(f32[1536]{0:T(1024)} %param.11) | copy-start | bytes 18436
  49.8 36.3 %collective-permute-start.6 = (bf16[2,128,1536]{2,1,0:T(8,128)(2,1)S(1)}, bf16[2,128,1536]{2,1,0:T(8,128)(2,1)S(1)}, u32[]{:S(2)}, u32[]{:S(2)}) collective-permute-start(bf16[2,128,1536]{2,1,0:T(8,128)(2,1)S(1)} %collective-permute-done.2.near_ref), channel_id=1, source_target_pairs={{578,0},{579,1},{0,192},{1,193},{192,384},{193,385},{384,576},{385... | collective-permute-start | bytes 2359304 | tf_op jit(solution)/shard_map/ppermute | solution.py:241
  51.7 34.4 %collective-permute-start.5 = (bf16[2,128,1536]{2,1,0:T(8,128)(2,1)S(1)}, bf16[2,128,1536]{2,1,0:T(8,128)(2,1)}, u32[]{:S(2)}, u32[]{:S(2)}) collective-permute-start(bf16[2,128,1536]{2,1,0:T(8,128)(2,1)S(1)} %collective-permute-done.2.near_ref), channel_id=1, source_target_pairs={{192,0},{193,1},{384,192},{385,193},{576,384},{577,385},{2,576},{3... | collective-permute-start | bytes 2359304 | tf_op jit(solution)/shard_map/ppermute | solution.py:241
  55.2 1.2 copy-start.4
  77.9 10.1 %collective-permute-start.4 = (bf16[48,2,32,128]{3,2,1,0:T(8,128)(2,1)S(1)}, bf16[48,2,32,128]{3,2,1,0:T(8,128)(2,1)S(1)}, u32[]{:S(2)}, u32[]{:S(2)}) collective-permute-start(bf16[48,2,32,128]{3,2,1,0:T(8,128)(2,1)S(1)} %all-to-all-done.own_ref), channel_id=1, source_target_pairs={{0,1},{1,0},{2,3},{3,2},{4,5},{5,4},{6,7},{7,6},{8,9},{9,8},{10,11... | collective-permute-start | bytes 2359304 | tf_op jit(solution)/shard_map/ppermute | solution.py:275
  88.3 1.4 copy-start.5
  93.9 4.2 %collective-permute-start.7 = (bf16[48,2,32,128]{3,2,1,0:T(8,128)(2,1)S(1)}, bf16[48,2,32,128]{3,2,1,0:T(8,128)(2,1)S(1)}, u32[]{:S(2)}, u32[]{:S(2)}) collective-permute-start(bf16[48,2,32,128]{3,2,1,0:T(8,128)(2,1)S(1)} %get-tuple-element.16), channel_id=1, source_target_pairs={{0,1},{1,0},{2,3},{3,2},{4,5},{5,4},{6,7},{7,6},{8,9},{9,8},{10,11... | collective-permute-start | bytes 2359304 | tf_op jit(solution)/shard_map/ppermute | solution.py:295
  136.2 10.9 %collective-permute-start.8 = (bf16[3,32,128]{2,1,0:T(8,128)(2,1)S(1)}, bf16[3,32,128]{2,1,0:T(8,128)(2,1)S(1)}, u32[]{:S(2)}, u32[]{:S(2)}) collective-permute-start(bf16[3,32,128]{2,1,0:T(8,128)(2,1)S(1)} %get-tuple-element.20), channel_id=1, source_target_pairs={{0,1},{1,2},{2,3},{3,4},{4,5},{5,6},{6,7},{7,8},{8,9},{9,10},{10,1... | collective-permute-start | bytes 73736 | tf_op jit(solution)/shard_map/ppermute | solution.py:25
  145.2 10.0 %collective-permute-start.9 = (bf16[3,32,128]{2,1,0:T(8,128)(2,1)S(1)}, bf16[3,32,128]{2,1,0:T(8,128)(2,1)S(1)}, u32[]{:S(2)}, u32[]{:S(2)}) collective-permute-start(bf16[3,32,128]{2,1,0:T(8,128)(2,1)S(1)} %get-tuple-element.21), channel_id=1, source_target_pairs={{1,0},{2,1},{3,2},{4,3},{5,4},{6,5},{7,6},{8,7},{9,8},{10,9},{11,1... | collective-permute-start | bytes 73736 | tf_op jit(solution)/shard_map/ppermute | solution.py:25

commit v9 on v8

--- a/solution.py
+++ b/solution.py
@@ -79,6 +79,11 @@
     conv_rows(framed, taps_ref, False, emit)
 
 
+def stack_kernel(in_ref, out_ref, both_ref):
+    both_ref[0] = in_ref[...].T
+    both_ref[1] = out_ref[...]
+
+
 def join_kernel(near_ref, far_ref, out_ref):
     out_ref[0] = near_ref[...]
     out_ref[1] = far_ref[...]
@@ -252,7 +257,7 @@
     hid = w_out.shape[0] * lax.axis_size("y")
     swap = [(0, 1), (1, 0)]
 
-    both = jnp.stack([w_in.T, w_out])
+    (both,) = call(stack_kernel, [((2, *w_out.shape), BF16)], (w_in, w_out))
     near, far = moved(both, 0), moved(both, 2)
     low, high = edges(floor_tokens[:3] + 1, floor_tokens[rows - 3 :] + 1)
     taps = depth_kernel.reshape(49, chans).T

time: 158 us -> 155 us (0.981)
  other arithmetic: 2.21 us -> 0.26 us
    another operation x1 -> x0, other arithmetic: 1.96 us -> none  [on_device(): both = jnp.stack([w_in.T, w_out])]
    unnamed x17 -> x20, local copies, waits for them, and re-layouts: 3.8 us -> 4.59 us
    pallas_call x5 -> x6, Pallas kernels: 8.1 us -> 7.87 us  [call(): pl.pallas_call(body, out_shape=outs, in_specs=specs or [VMEM] * len(args)...]
where the time goes in v9:
time: 155 us; the launch traced here: 154 us
  starting transfers between devices  69 us (45%)
  blocking collectives  37.2 us (24%)
  waiting for transfers between devices  34.1 us (22%)
  Pallas kernels  7.87 us (5%)
  local copies, waits for them, and re-layouts  5.12 us (3%)
    all_to_all x1, blocking collectives, on_device(): got = lax.all_to_all(part, CHAN, 0, 0, tiled=True)  37.2 us
    all_to_all x1, starting transfers between devices, on_device(): own = lax.all_to_all(send, CHAN, 0, 0, tiled=True)  23.3 us
    all_to_all x1, waiting for transfers between devices, on_device(): own = lax.all_to_all(send, CHAN, 0, 0, tiled=True)  21.4 us
    ppermute x2, starting transfers between devices, edges(): lax.ppermute(high_side, SPACE, forward)  17.9 us
    ppermute x2, waiting for transfers between devices, edges(): lax.ppermute(low_side, SPACE, backward)  8.88 us
    ppermute x1, starting transfers between devices, on_device(): oth = lax.ppermute(own, 'c', swap)  8.32 us
    ppermute x2, starting transfers between devices, moved(): return lax.ppermute(shard, AXES, pairs)  8.05 us
    pallas_call x6, Pallas kernels, call(): pl.pallas_call(body, out_shape=outs, in_specs=specs or [VMEM] * len(args)...  7.87 us
  transfers between devices with their start and end apart: 11, of which 5 were waited for; matrix products, arithmetic and copies ran while one was open for 0% of the time, Pallas kernels for 1%

profile of v9, /device:TPU:57, one launch (start us, length us, event | category | flops | bytes accessed | tf_op | source)
XLA Modules:
  0.0 154.4 jit_solution(17975819900895456265)
XLA Ops:
  0.6 0.0 copy-start
  0.6 0.0 copy-start.1
  0.7 1.0 copy-done.1
  1.6 0.0 copy-start.2
  1.7 1.0 copy-done.2
  2.6 0.0 copy-start.5
  2.6 0.0 copy-start.8
  2.7 0.0 copy-start.3
  2.7 0.0 copy-start.4
  2.7 0.2 shard_map.96
  2.8 4.6 %collective-permute-start.2 = (bf16[2,128,1536]{2,1,0:T(8,128)(2,1)S(1)}, bf16[2,128,1536]{2,1,0:T(8,128)(2,1)S(1)}, u32[]{:S(2)}, u32[]{:S(2)}) collective-permute-start(bf16[2,128,1536]{2,1,0:T(8,128)(2,1)S(1)} %shard_map.96), channel_id=1, source_target_pairs={{0,0},{16,1},{2,2},{18,3},{4,4},{20,5},{6,6},{22,7},{8,8},{24,9},{... | collective-permute-start | bytes 2359304 | tf_op jit(solution)/shard_map/ppermute | solution.py:232
  7.4 3.5 %collective-permute-start.3 = (bf16[2,128,1536]{2,1,0:T(8,128)(2,1)S(1)}, bf16[2,128,1536]{2,1,0:T(8,128)(2,1)S(1)}, u32[]{:S(2)}, u32[]{:S(2)}) collective-permute-start(bf16[2,128,1536]{2,1,0:T(8,128)(2,1)S(1)} %shard_map.96), channel_id=1, source_target_pairs={{384,0},{402,1},{386,2},{400,3},{388,4},{406,5},{390,6},{404,7},{3... | collective-permute-start | bytes 2359304 | tf_op jit(solution)/shard_map/ppermute | solution.py:232
  10.9 0.0 copy-done.5
  10.9 1.9 %collective-permute-start.1 = (s32[3,128]{1,0:T(4,128)S(1)}, s32[3,128]{1,0:T(4,128)S(1)}, u32[]{:S(2)}, u32[]{:S(2)}) collective-permute-start(s32[3,128]{1,0:T(4,128)S(1)} %get-tuple-element.22), channel_id=1, source_target_pairs={{1,0},{2,1},{3,2},{4,3},{5,4},{6,5},{7,6},{8,7},{9,8},{10,9},{11,1... | collective-permute-start | bytes 4616 | tf_op jit(solution)/shard_map/ppermute | solution.py:25
  12.8 8.4 %collective-permute-start = (s32[3,128]{1,0:T(4,128)S(1)}, s32[3,128]{1,0:T(4,128)S(1)}, u32[]{:S(2)}, u32[]{:S(2)}) collective-permute-start(s32[3,128]{1,0:T(4,128)S(1)} %get-tuple-element.23), channel_id=1, source_target_pairs={{0,1},{1,2},{2,3},{3,4},{4,5},{5,6},{6,7},{7,8},{8,9},{9,10},{10,1... | collective-permute-start | bytes 4616 | tf_op jit(solution)/shard_map/ppermute | solution.py:25
  21.3 0.0 copy-done
  21.3 0.1 dynamic-slice_bitcast_fusion
  21.4 0.0 copy-done.8
  21.4 0.1 copy.13
  21.5 0.1 copy.14.scale_ref
  21.6 0.7 collective-permute-done.1.high_ref
  22.3 0.0 collective-permute-done.low_ref
  22.3 0.0 copy-done.3
  22.3 0.0 copy-done.4
  22.3 1.7 %shard_map.95 = (bf16[8,32,128]{2,1,0:T(8,128)(2,1)S(1)}, bf16[48,2,32,128]{3,2,1,0:T(8,128)(2,1)}) custom-call(s32[8,128]{1,0:T(8,128)S(1)} %copy-done.5, s32[3,128]{1,0:T(4,128)S(1)} %collective-permute-done.low_ref, s32[3,128]{1,0:T(4,128)S(1)} %collective-permute-done.1.high_ref, bf16[32,256]{1,0:T(8,128)(2,1)S(1)} %bitcast.11, ...), custom_call_target="tpu_custom_call" | custom-call | flops 1048576 | bytes 4194304 | tf_op jit(solution)/shard_map/pallas_call | solution.py:210
  24.1 23.3 %all-to-all-start = ((bf16[48,2,32,128]{3,2,1,0:T(8,128)(2,1)}), bf16[48,2,32,128]{3,2,1,0:T(8,128)(2,1)S(1)}, u32[]{:S(2)}, u32[]{:S(2)}) async-start(bf16[48,2,32,128]{3,2,1,0:T(8,128)(2,1)} %get-tuple-element.12), calls=%async_computation | async-start | bytes 1572864 | tf_op jit(solution)/shard_map/all_to_all | solution.py:276
  47.4 0.0 copy-start.9
  47.4 0.0 collective-permute-done.2.near_ref
  47.4 1.9 %collective-permute-start.6 = (bf16[2,128,1536]{2,1,0:T(8,128)(2,1)S(1)}, bf16[2,128,1536]{2,1,0:T(8,128)(2,1)}, u32[]{:S(2)}, u32[]{:S(2)}) collective-permute-start(bf16[2,128,1536]{2,1,0:T(8,128)(2,1)S(1)} %collective-permute-done.2.near_ref), channel_id=1, source_target_pairs={{578,0},{579,1},{0,192},{1,193},{192,384},{193,385},{384,576},{385... | collective-permute-start | bytes 2359304 | tf_op jit(solution)/shard_map/ppermute | solution.py:246
  49.3 3.4 %collective-permute-start.5 = (bf16[2,128,1536]{2,1,0:T(8,128)(2,1)S(1)}, bf16[2,128,1536]{2,1,0:T(8,128)(2,1)}, u32[]{:S(2)}, u32[]{:S(2)}) collective-permute-start(bf16[2,128,1536]{2,1,0:T(8,128)(2,1)S(1)} %collective-permute-done.2.near_ref), channel_id=1, source_target_pairs={{192,0},{193,1},{384,192},{385,193},{576,384},{577,385},{2,576},{3... | collective-permute-start | bytes 2359304 | tf_op jit(solution)/shard_map/ppermute | solution.py:246
  52.7 0.0 collective-permute-done.3.far_ref
  52.7 0.1 shard_map.97.w2_ref
  52.8 0.0 copy-start.6
  52.8 1.2 copy-done.6
  54.0 21.4 %all-to-all-done.own_ref = bf16[48,2,32,128]{3,2,1,0:T(8,128)(2,1)S(1)} async-done(((bf16[48,2,32,128]{3,2,1,0:T(8,128)(2,1)}), bf16[48,2,32,128]{3,2,1,0:T(8,128)(2,1)S(1)}, u32[]{:S(2)}, u32[]{:S(2)}) %all-to-all-start) | async-done | bytes 786464 | tf_op jit(solution)/shard_map/all_to_all | solution.py:276
  75.4 8.3 %collective-permute-start.4 = (bf16[48,2,32,128]{3,2,1,0:T(8,128)(2,1)S(1)}, bf16[48,2,32,128]{3,2,1,0:T(8,128)(2,1)S(1)}, u32[]{:S(2)}, u32[]{:S(2)}) collective-permute-start(bf16[48,2,32,128]{3,2,1,0:T(8,128)(2,1)S(1)} %all-to-all-done.own_ref), channel_id=1, source_target_pairs={{0,1},{1,0},{2,3},{3,2},{4,5},{5,4},{6,7},{7,6},{8,9},{9,8},{10,11... | collective-permute-start | bytes 2359304 | tf_op jit(solution)/shard_map/ppermute | solution.py:280
  83.7 0.0 collective-permute-done.6.w1_ref
  83.7 0.0 collective-permute-done.5.w0_ref
  83.7 1.9 %collective-permute-done.4.oth_ref = bf16[48,2,32,128]{3,2,1,0:T(8,128)(2,1)S(1)} collective-permute-done((bf16[48,2,32,128]{3,2,1,0:T(8,128)(2,1)S(1)}, bf16[48,2,32,128]{3,2,1,0:T(8,128)(2,1)S(1)}, u32[]{:S(2)}, u32[]{:S(2)}) %collective-permute-start.4) | collective-permute-done | bytes 786464 | tf_op jit(solution)/shard_map/ppermute | solution.py:280
  85.6 0.0 copy-done.9
  85.6 0.3 broadcast_in_dim.10.gain_ref
  85.9 0.0 copy-start.7
  85.9 1.4 copy-done.7
  87.3 3.8 %shard_map.98 = (f32[48,2,32,128]{3,2,1,0:T(8,128)S(1)}, bf16[48,2,32,128]{3,2,1,0:T(8,128)(2,1)S(1)}) custom-call(bf16[48,2,32,128]{3,2,1,0:T(8,128)(2,1)S(1)} %all-to-all-done.own_ref, bf16[48,2,32,128]{3,2,1,0:T(8,128)(2,1)S(1)} %collective-permute-done.4.oth_ref, f32[1536,128]{1,0:T(8,128)S(1)} %broadcast_in_dim.10.gain_ref, ...), custom_call_target="tpu_custom_call" | custom-call | flops 1610612736 | bytes 4194304 | tf_op jit(solution)/shard_map/pallas_call | solution.py:210
  91.2 2.3 %collective-permute-start.7 = (bf16[48,2,32,128]{3,2,1,0:T(8,128)(2,1)S(1)}, bf16[48,2,32,128]{3,2,1,0:T(8,128)(2,1)S(1)}, u32[]{:S(2)}, u32[]{:S(2)}) collective-permute-start(bf16[48,2,32,128]{3,2,1,0:T(8,128)(2,1)S(1)} %get-tuple-element.16), channel_id=1, source_target_pairs={{0,1},{1,0},{2,3},{3,2},{4,5},{5,4},{6,7},{7,6},{8,9},{9,8},{10,11... | collective-permute-start | bytes 2359304 | tf_op jit(solution)/shard_map/ppermute | solution.py:300
  93.4 1.9 %collective-permute-done.7 = bf16[48,2,32,128]{3,2,1,0:T(8,128)(2,1)S(1)} collective-permute-done((bf16[48,2,32,128]{3,2,1,0:T(8,128)(2,1)S(1)}, bf16[48,2,32,128]{3,2,1,0:T(8,128)(2,1)S(1)}, u32[]{:S(2)}, u32[]{:S(2)}) %collective-permute-start.7) | collective-permute-done | bytes 786464 | tf_op jit(solution)/shard_map/ppermute | solution.py:300
  95.3 0.3 add_convert_fusion
  95.6 37.2 %all_to_all.10.got_ref = bf16[48,2,32,128]{3,2,1,0:T(8,128)(2,1)S(1)} all-to-all(bf16[48,2,32,128]{3,2,1,0:T(8,128)(2,1)S(1)} %add_convert_fusion), channel_id=1, replica_groups=mesh['y'=4,'z'=12,'x'=4,'h'=2,'c'=2] {'y','z'}, dimensions={0} | all-to-all | bytes 1572864 | tf_op jit(solution)/shard_map/all_to_all | solution.py:301
  132.8 0.7 shard_map.99
  133.6 9.5 %collective-permute-start.8 = (bf16[3,32,128]{2,1,0:T(8,128)(2,1)S(1)}, bf16[3,32,128]{2,1,0:T(8,128)(2,1)S(1)}, u32[]{:S(2)}, u32[]{:S(2)}) collective-permute-start(bf16[3,32,128]{2,1,0:T(8,128)(2,1)S(1)} %get-tuple-element.20), channel_id=1, source_target_pairs={{0,1},{1,2},{2,3},{3,4},{4,5},{5,6},{6,7},{7,8},{8,9},{9,10},{10,1... | collective-permute-start | bytes 73736 | tf_op jit(solution)/shard_map/ppermute | solution.py:25
  143.0 1.9 %collective-permute-start.9 = (bf16[3,32,128]{2,1,0:T(8,128)(2,1)S(1)}, bf16[3,32,128]{2,1,0:T(8,128)(2,1)S(1)}, u32[]{:S(2)}, u32[]{:S(2)}) collective-permute-start(bf16[3,32,128]{2,1,0:T(8,128)(2,1)S(1)} %get-tuple-element.21), channel_id=1, source_target_pairs={{1,0},{2,1},{3,2},{4,3},{5,4},{6,5},{7,6},{8,7},{9,8},{10,9},{11,1... | collective-permute-start | bytes 73736 | tf_op jit(solution)/shard_map/ppermute | solution.py:25
  145.0 0.0 collective-permute-done.8.low_ref
  145.0 8.2 %collective-permute-done.9.high_ref = bf16[3,32,128]{2,1,0:T(8,128)(2,1)S(1)} collective-permute-done((bf16[3,32,128]{2,1,0:T(8,128)(2,1)S(1)}, bf16[3,32,128]{2,1,0:T(8,128)(2,1)S(1)}, u32[]{:S(2)}, u32[]{:S(2)}) %collective-permute-start.9) | collective-permute-done | bytes 24608 | tf_op jit(solution)/shard_map/ppermute | solution.py:25
  153.1 1.3 shard_map.100
  (2 shorter events, 0.0 us)
Async XLA Ops:
  0.6 20.7 %copy-start = (f32[1536]{0:T(1024)S(1)}, f32[1536]{0:T(1024)}, u32[]{:S(2)}) copy-start(f32[1536]{0:T(1024)} %param.12) | copy-start | bytes 18436
  0.6 1.0 copy-start.1
  1.6 1.0 copy-start.2
  2.6 8.2 %copy-start.5 = (s32[8,128]{1,0:T(8,128)S(1)}, s32[8,128]{1,0:T(8,128)}, u32[]{:S(2)}) copy-start(s32[8,128]{1,0:T(8,128)} %tok_ref.1) | copy-start | bytes 12292
  2.6 18.8 %copy-start.8 = (bf16[7,7,32]{2,1,0:T(8,128)(2,1)S(1)}, bf16[7,7,32]{2,1,0:T(8,128)(2,1)}, u32[]{:S(2)}) copy-start(bf16[7,7,32]{2,1,0:T(8,128)(2,1)} %param.10) | copy-start | bytes 9412
  2.7 19.7 %copy-start.3 = (bf16[8,128,32]{1,2,0:T(8,128)(2,1)S(1)}, bf16[8,128,32]{1,2,0:T(8,128)(2,1)}, u32[]{:S(2)}) copy-start(bf16[8,128,32]{1,2,0:T(8,128)(2,1)} %param.15) | copy-start | bytes 196612
  2.7 19.7 %copy-start.4 = (bf16[256,32]{0,1:T(8,128)(2,1)S(1)}, bf16[256,32]{0,1:T(8,128)(2,1)}, u32[]{:S(2)}) copy-start(bf16[256,32]{0,1:T(8,128)(2,1)} %param.9) | copy-start | bytes 49156
  2.8 44.6 %collective-permute-start.2 = (bf16[2,128,1536]{2,1,0:T(8,128)(2,1)S(1)}, bf16[2,128,1536]{2,1,0:T(8,128)(2,1)S(1)}, u32[]{:S(2)}, u32[]{:S(2)}) collective-permute-start(bf16[2,128,1536]{2,1,0:T(8,128)(2,1)S(1)} %shard_map.96), channel_id=1, source_target_pairs={{0,0},{16,1},{2,2},{18,3},{4,4},{20,5},{6,6},{22,7},{8,8},{24,9},{... | collective-permute-start | bytes 2359304 | tf_op jit(solution)/shard_map/ppermute | solution.py:232
  7.4 45.3 %collective-permute-start.3 = (bf16[2,128,1536]{2,1,0:T(8,128)(2,1)S(1)}, bf16[2,128,1536]{2,1,0:T(8,128)(2,1)S(1)}, u32[]{:S(2)}, u32[]{:S(2)}) collective-permute-start(bf16[2,128,1536]{2,1,0:T(8,128)(2,1)S(1)} %shard_map.96), channel_id=1, source_target_pairs={{384,0},{402,1},{386,2},{400,3},{388,4},{406,5},{390,6},{404,7},{3... | collective-permute-start | bytes 2359304 | tf_op jit(solution)/shard_map/ppermute | solution.py:232
  10.9 11.4 %collective-permute-start.1 = (s32[3,128]{1,0:T(4,128)S(1)}, s32[3,128]{1,0:T(4,128)S(1)}, u32[]{:S(2)}, u32[]{:S(2)}) collective-permute-start(s32[3,128]{1,0:T(4,128)S(1)} %get-tuple-element.22), channel_id=1, source_target_pairs={{1,0},{2,1},{3,2},{4,3},{5,4},{6,5},{7,6},{8,7},{9,8},{10,9},{11,1... | collective-permute-start | bytes 4616 | tf_op jit(solution)/shard_map/ppermute | solution.py:25
  12.8 9.5 %collective-permute-start = (s32[3,128]{1,0:T(4,128)S(1)}, s32[3,128]{1,0:T(4,128)S(1)}, u32[]{:S(2)}, u32[]{:S(2)}) collective-permute-start(s32[3,128]{1,0:T(4,128)S(1)} %get-tuple-element.23), channel_id=1, source_target_pairs={{0,1},{1,2},{2,3},{3,4},{4,5},{5,6},{6,7},{7,8},{8,9},{9,10},{10,1... | collective-permute-start | bytes 4616 | tf_op jit(solution)/shard_map/ppermute | solution.py:25
  24.1 51.3 %all-to-all-start = ((bf16[48,2,32,128]{3,2,1,0:T(8,128)(2,1)}), bf16[48,2,32,128]{3,2,1,0:T(8,128)(2,1)S(1)}, u32[]{:S(2)}, u32[]{:S(2)}) async-start(bf16[48,2,32,128]{3,2,1,0:T(8,128)(2,1)} %get-tuple-element.12), calls=%async_computation | async-start | bytes 1572864 | tf_op jit(solution)/shard_map/all_to_all | solution.py:276
  47.4 38.2 %copy-start.9 = (f32[1536]{0:T(1024)S(1)}, f32[1536]{0:T(1024)}, u32[]{:S(2)}) copy-start(f32[1536]{0:T(1024)} %param.11) | copy-start | bytes 18436
  47.4 36.3 %collective-permute-start.6 = (bf16[2,128,1536]{2,1,0:T(8,128)(2,1)S(1)}, bf16[2,128,1536]{2,1,0:T(8,128)(2,1)}, u32[]{:S(2)}, u32[]{:S(2)}) collective-permute-start(bf16[2,128,1536]{2,1,0:T(8,128)(2,1)S(1)} %collective-permute-done.2.near_ref), channel_id=1, source_target_pairs={{578,0},{579,1},{0,192},{1,193},{192,384},{193,385},{384,576},{385... | collective-permute-start | bytes 2359304 | tf_op jit(solution)/shard_map/ppermute | solution.py:246
  49.3 34.4 %collective-permute-start.5 = (bf16[2,128,1536]{2,1,0:T(8,128)(2,1)S(1)}, bf16[2,128,1536]{2,1,0:T(8,128)(2,1)}, u32[]{:S(2)}, u32[]{:S(2)}) collective-permute-start(bf16[2,128,1536]{2,1,0:T(8,128)(2,1)S(1)} %collective-permute-done.2.near_ref), channel_id=1, source_target_pairs={{192,0},{193,1},{384,192},{385,193},{576,384},{577,385},{2,576},{3... | collective-permute-start | bytes 2359304 | tf_op jit(solution)/shard_map/ppermute | solution.py:246
  52.8 1.2 copy-start.6
  75.4 10.2 %collective-permute-start.4 = (bf16[48,2,32,128]{3,2,1,0:T(8,128)(2,1)S(1)}, bf16[48,2,32,128]{3,2,1,0:T(8,128)(2,1)S(1)}, u32[]{:S(2)}, u32[]{:S(2)}) collective-permute-start(bf16[48,2,32,128]{3,2,1,0:T(8,128)(2,1)S(1)} %all-to-all-done.own_ref), channel_id=1, source_target_pairs={{0,1},{1,0},{2,3},{3,2},{4,5},{5,4},{6,7},{7,6},{8,9},{9,8},{10,11... | collective-permute-start | bytes 2359304 | tf_op jit(solution)/shard_map/ppermute | solution.py:280
  85.9 1.4 copy-start.7
  91.2 4.2 %collective-permute-start.7 = (bf16[48,2,32,128]{3,2,1,0:T(8,128)(2,1)S(1)}, bf16[48,2,32,128]{3,2,1,0:T(8,128)(2,1)S(1)}, u32[]{:S(2)}, u32[]{:S(2)}) collective-permute-start(bf16[48,2,32,128]{3,2,1,0:T(8,128)(2,1)S(1)} %get-tuple-element.16), channel_id=1, source_target_pairs={{0,1},{1,0},{2,3},{3,2},{4,5},{5,4},{6,7},{7,6},{8,9},{9,8},{10,11... | collective-permute-start | bytes 2359304 | tf_op jit(solution)/shard_map/ppermute | solution.py:300
  133.6 11.4 %collective-permute-start.8 = (bf16[3,32,128]{2,1,0:T(8,128)(2,1)S(1)}, bf16[3,32,128]{2,1,0:T(8,128)(2,1)S(1)}, u32[]{:S(2)}, u32[]{:S(2)}) collective-permute-start(bf16[3,32,128]{2,1,0:T(8,128)(2,1)S(1)} %get-tuple-element.20), channel_id=1, source_target_pairs={{0,1},{1,2},{2,3},{3,4},{4,5},{5,6},{6,7},{7,8},{8,9},{9,10},{10,1... | collective-permute-start | bytes 73736 | tf_op jit(solution)/shard_map/ppermute | solution.py:25
  143.0 10.1 %collective-permute-start.9 = (bf16[3,32,128]{2,1,0:T(8,128)(2,1)S(1)}, bf16[3,32,128]{2,1,0:T(8,128)(2,1)S(1)}, u32[]{:S(2)}, u32[]{:S(2)}) collective-permute-start(bf16[3,32,128]{2,1,0:T(8,128)(2,1)S(1)} %get-tuple-element.21), channel_id=1, source_target_pairs={{1,0},{2,1},{3,2},{4,3},{5,4},{6,5},{7,6},{8,7},{9,8},{10,9},{11,1... | collective-permute-start | bytes 73736 | tf_op jit(solution)/shard_map/ppermute | solution.py:25

commit v10 on v7

--- a/solution.py
+++ b/solution.py
@@ -79,8 +79,17 @@
     conv_rows(framed, taps_ref, False, emit)
 
 
+def stack_kernel(in_ref, out_ref, both_ref):
+    both_ref[0] = in_ref[...].T
+    both_ref[1] = out_ref[...]
+
+
+def anchor_kernel(near_ref, far_ref, out_ref):
+    out_ref[...] = near_ref[0, :16, :128] + far_ref[0, :16, :128]
+
+
 def middle_kernel(
-    own_ref, oth_ref, gain_ref, w0_ref, w1_ref, w2_ref, w3_ref,
+    own_ref, oth_ref, gain_ref, w0_ref, w1_ref, w2_ref, w3_ref, _,
     keep_ref, sib_ref,
     win, wout, scaled, gmix, normed, grads, act, gpre, sem,
 ):
@@ -246,7 +255,7 @@
     hid = w_out.shape[0] * lax.axis_size("y")
     swap = [(0, 1), (1, 0)]
 
-    both = jnp.stack([w_in.T, w_out])
+    (both,) = call(stack_kernel, [((2, *w_out.shape), BF16)], (w_in, w_out))
     near, far = moved(both, 0), moved(both, 2)
     low, high = edges(floor_tokens[:3] + 1, floor_tokens[rows - 3 :] + 1)
     taps = depth_kernel.reshape(49, chans).T
@@ -261,15 +270,17 @@
         [(tile, BF16), (packed, BF16)],
         (floor_tokens, low, high, token_table.T, taps, scale, grad_local),
     )
-    send, near, far = lax.optimization_barrier((send, near, far))
-    weights = [near, far, from_ring(near, 1), from_ring(near, 3)]
+    weights = [from_ring(near, 1), from_ring(near, 3)]
     own = lax.all_to_all(send, CHAN, 0, 0, tiled=True)
+    (anchor,) = call(anchor_kernel, [((16, 128), BF16)], (near, far), flops=20 << 30)
+    own, anchor = lax.optimization_barrier((own, anchor))
+    weights += [near, far, anchor]
     oth = lax.ppermute(own, "c", swap)
     keep, sib = call(
         middle_kernel,
         [(packed, F32), (packed, BF16)],
         (own, oth, gain, *weights),
-        [VMEM] * 3 + [ANY] * 4,
+        [VMEM] * 3 + [ANY] * 5,
         [
             pltpu.VMEM((hid, width), BF16),
             pltpu.VMEM((hid, width), BF16),

time: 160 us -> 154 us (0.963)
  waiting for transfers between devices: 43.7 us -> 35.3 us
  starting transfers between devices: 66.4 us -> 69 us
    ppermute x2, waiting for transfers between devices: 8.68 us -> 0.01 us  [moved(): return lax.ppermute(shard, AXES, pairs)]
    all_to_all x1, starting transfers between devices: 19.4 us -> 23.3 us  [on_device(): own = lax.all_to_all(send, CHAN, 0, 0, tiled=True)]
    pallas_call x4 -> x6, Pallas kernels: 8.02 us -> 7.79 us  [call(): pl.pallas_call(body, out_shape=outs, in_specs=specs or [VMEM] * len(args)...]
  transfers between devices with their start and end apart: 11 -> 11, of which waited for: 7 -> 5; matrix products, arithmetic and copies ran while one was open for 0% -> 0% of each run, Pallas kernels for 1% -> 1%
where the time goes in v10:
time: 154 us; the launch traced here: 153 us
  starting transfers between devices  69 us (45%)
  blocking collectives  37.2 us (24%)
  waiting for transfers between devices  35.3 us (23%)
  Pallas kernels  7.79 us (5%)
  local copies, waits for them, and re-layouts  2.55 us (2%)
    all_to_all x1, blocking collectives, on_device(): got = lax.all_to_all(part, CHAN, 0, 0, tiled=True)  37.2 us
    all_to_all x1, starting transfers between devices, on_device(): own = lax.all_to_all(send, CHAN, 0, 0, tiled=True)  23.3 us
    all_to_all x1, waiting for transfers between devices, on_device(): own = lax.all_to_all(send, CHAN, 0, 0, tiled=True)  22.7 us
    ppermute x2, starting transfers between devices, edges(): lax.ppermute(high_side, SPACE, forward)  17.9 us
    ppermute x2, waiting for transfers between devices, edges(): lax.ppermute(low_side, SPACE, backward)  8.88 us
    ppermute x1, starting transfers between devices, on_device(): oth = lax.ppermute(own, 'c', swap)  8.32 us
    ppermute x2, starting transfers between devices, moved(): return lax.ppermute(shard, AXES, pairs)  8.05 us
    pallas_call x6, Pallas kernels, call(): pl.pallas_call(body, out_shape=outs, in_specs=specs or [VMEM] * len(args)...  7.79 us
  transfers between devices with their start and end apart: 11, of which 5 were waited for; matrix products, arithmetic and copies ran while one was open for 0% of the time, Pallas kernels for 1%

profile of v10, /device:TPU:57, one launch (start us, length us, event | category | flops | bytes accessed | tf_op | source)
XLA Modules:
  0.0 153.1 jit_solution(8408269922892713442)
XLA Ops:
  0.6 0.0 copy-start
  0.6 0.0 copy-start.1
  0.7 1.0 copy-done.1
  1.6 0.0 copy-start.2
  1.7 1.0 copy-done.2
  2.6 0.0 copy-start.5
  2.6 0.0 copy-start.6
  2.7 0.0 copy-start.3
  2.7 0.0 copy-start.4
  2.7 0.2 shard_map.96
  2.8 4.6 %collective-permute-start.2 = (bf16[2,128,1536]{2,1,0:T(8,128)(2,1)S(1)}, bf16[2,128,1536]{2,1,0:T(8,128)(2,1)S(1)}, u32[]{:S(2)}, u32[]{:S(2)}) collective-permute-start(bf16[2,128,1536]{2,1,0:T(8,128)(2,1)S(1)} %shard_map.96), channel_id=1, source_target_pairs={{0,0},{16,1},{2,2},{18,3},{4,4},{20,5},{6,6},{22,7},{8,8},{24,9},{... | collective-permute-start | bytes 2359304 | tf_op jit(solution)/shard_map/ppermute | solution.py:230
  7.4 3.5 %collective-permute-start.3 = (bf16[2,128,1536]{2,1,0:T(8,128)(2,1)S(1)}, bf16[2,128,1536]{2,1,0:T(8,128)(2,1)S(1)}, u32[]{:S(2)}, u32[]{:S(2)}) collective-permute-start(bf16[2,128,1536]{2,1,0:T(8,128)(2,1)S(1)} %shard_map.96), channel_id=1, source_target_pairs={{384,0},{402,1},{386,2},{400,3},{388,4},{406,5},{390,6},{404,7},{3... | collective-permute-start | bytes 2359304 | tf_op jit(solution)/shard_map/ppermute | solution.py:230
  10.9 0.0 copy-done.5
  10.9 1.9 %collective-permute-start.1 = (s32[3,128]{1,0:T(4,128)S(1)}, s32[3,128]{1,0:T(4,128)S(1)}, u32[]{:S(2)}, u32[]{:S(2)}) collective-permute-start(s32[3,128]{1,0:T(4,128)S(1)} %get-tuple-element.22), channel_id=1, source_target_pairs={{1,0},{2,1},{3,2},{4,3},{5,4},{6,5},{7,6},{8,7},{9,8},{10,9},{11,1... | collective-permute-start | bytes 4616 | tf_op jit(solution)/shard_map/ppermute | solution.py:25
  12.8 8.4 %collective-permute-start = (s32[3,128]{1,0:T(4,128)S(1)}, s32[3,128]{1,0:T(4,128)S(1)}, u32[]{:S(2)}, u32[]{:S(2)}) collective-permute-start(s32[3,128]{1,0:T(4,128)S(1)} %get-tuple-element.23), channel_id=1, source_target_pairs={{0,1},{1,2},{2,3},{3,4},{4,5},{5,6},{6,7},{7,8},{8,9},{9,10},{10,1... | collective-permute-start | bytes 4616 | tf_op jit(solution)/shard_map/ppermute | solution.py:25
  21.3 0.0 copy-done
  21.3 0.1 dynamic-slice_bitcast_fusion
  21.4 0.0 copy-done.6
  21.4 0.1 copy.13
  21.5 0.1 copy.14.scale_ref
  21.6 0.7 collective-permute-done.1.high_ref
  22.3 0.0 collective-permute-done.low_ref
  22.3 0.0 copy-done.3
  22.3 0.0 copy-done.4
  22.3 1.7 %shard_map.95 = (bf16[8,32,128]{2,1,0:T(8,128)(2,1)S(1)}, bf16[48,2,32,128]{3,2,1,0:T(8,128)(2,1)}) custom-call(s32[8,128]{1,0:T(8,128)S(1)} %copy-done.5, s32[3,128]{1,0:T(4,128)S(1)} %collective-permute-done.low_ref, s32[3,128]{1,0:T(4,128)S(1)} %collective-permute-done.1.high_ref, bf16[32,256]{1,0:T(8,128)(2,1)S(1)} %bitcast.11, ...), custom_call_target="tpu_custom_call" | custom-call | flops 1048576 | bytes 4194304 | tf_op jit(solution)/shard_map/pallas_call | solution.py:208
  24.1 23.3 %all-to-all-start = ((bf16[48,2,32,128]{3,2,1,0:T(8,128)(2,1)}), bf16[48,2,32,128]{3,2,1,0:T(8,128)(2,1)S(1)}, u32[]{:S(2)}, u32[]{:S(2)}) async-start(bf16[48,2,32,128]{3,2,1,0:T(8,128)(2,1)} %get-tuple-element.12), calls=%async_computation | async-start | bytes 1572864 | tf_op jit(solution)/shard_map/all_to_all | solution.py:274
  47.4 0.0 copy-start.7
  47.4 0.0 collective-permute-done.2.near_ref.w2_ref
  47.4 1.9 %collective-permute-start.6 = (bf16[2,128,1536]{2,1,0:T(8,128)(2,1)S(1)}, bf16[2,128,1536]{2,1,0:T(8,128)(2,1)}, u32[]{:S(2)}, u32[]{:S(2)}) collective-permute-start(bf16[2,128,1536]{2,1,0:T(8,128)(2,1)S(1)} %collective-permute-done.2.near_ref.w2_ref), channel_id=1, source_target_pairs={{578,0},{579,1},{0,192},{1,193},{192,384},{193,385},{384,576},{385... | collective-permute-start | bytes 2359304 | tf_op jit(solution)/shard_map/ppermute | solution.py:244
  49.3 3.4 %collective-permute-start.5 = (bf16[2,128,1536]{2,1,0:T(8,128)(2,1)S(1)}, bf16[2,128,1536]{2,1,0:T(8,128)(2,1)}, u32[]{:S(2)}, u32[]{:S(2)}) collective-permute-start(bf16[2,128,1536]{2,1,0:T(8,128)(2,1)S(1)} %collective-permute-done.2.near_ref.w2_ref), channel_id=1, source_target_pairs={{192,0},{193,1},{384,192},{385,193},{576,384},{577,385},{2,576},{3... | collective-permute-start | bytes 2359304 | tf_op jit(solution)/shard_map/ppermute | solution.py:244
  52.7 0.0 collective-permute-done.3.far_ref.w3_ref
  52.7 22.7 %all-to-all-done.own_ref = bf16[48,2,32,128]{3,2,1,0:T(8,128)(2,1)S(1)} async-done(((bf16[48,2,32,128]{3,2,1,0:T(8,128)(2,1)}), bf16[48,2,32,128]{3,2,1,0:T(8,128)(2,1)S(1)}, u32[]{:S(2)}, u32[]{:S(2)}) %all-to-all-start) | async-done | bytes 786464 | tf_op jit(solution)/shard_map/all_to_all | solution.py:274
  75.4 8.3 %collective-permute-start.4 = (bf16[48,2,32,128]{3,2,1,0:T(8,128)(2,1)S(1)}, bf16[48,2,32,128]{3,2,1,0:T(8,128)(2,1)S(1)}, u32[]{:S(2)}, u32[]{:S(2)}) collective-permute-start(bf16[48,2,32,128]{3,2,1,0:T(8,128)(2,1)S(1)} %all-to-all-done.own_ref), channel_id=1, source_target_pairs={{0,1},{1,0},{2,3},{3,2},{4,5},{5,4},{6,7},{7,6},{8,9},{9,8},{10,11... | collective-permute-start | bytes 2359304 | tf_op jit(solution)/shard_map/ppermute | solution.py:278
  83.7 0.0 collective-permute-done.6.w1_ref
  83.7 0.0 collective-permute-done.5.w0_ref
  83.7 1.9 %collective-permute-done.4.oth_ref = bf16[48,2,32,128]{3,2,1,0:T(8,128)(2,1)S(1)} collective-permute-done((bf16[48,2,32,128]{3,2,1,0:T(8,128)(2,1)S(1)}, bf16[48,2,32,128]{3,2,1,0:T(8,128)(2,1)S(1)}, u32[]{:S(2)}, u32[]{:S(2)}) %collective-permute-start.4) | collective-permute-done | bytes 786464 | tf_op jit(solution)/shard_map/ppermute | solution.py:278
  85.6 0.0 copy-done.7
  85.6 0.3 broadcast_in_dim.10.gain_ref
  85.9 3.9 %shard_map.98 = (f32[48,2,32,128]{3,2,1,0:T(8,128)S(1)}, bf16[48,2,32,128]{3,2,1,0:T(8,128)(2,1)S(1)}) custom-call(bf16[48,2,32,128]{3,2,1,0:T(8,128)(2,1)S(1)} %all-to-all-done.own_ref, bf16[48,2,32,128]{3,2,1,0:T(8,128)(2,1)S(1)} %collective-permute-done.4.oth_ref, f32[1536,128]{1,0:T(8,128)S(1)} %broadcast_in_dim.10.gain_ref, ...), custom_call_target="tpu_custom_call" | custom-call | flops 1610612736 | bytes 4194304 | tf_op jit(solution)/shard_map/pallas_call | solution.py:208
  89.8 2.3 %collective-permute-start.7 = (bf16[48,2,32,128]{3,2,1,0:T(8,128)(2,1)S(1)}, bf16[48,2,32,128]{3,2,1,0:T(8,128)(2,1)S(1)}, u32[]{:S(2)}, u32[]{:S(2)}) collective-permute-start(bf16[48,2,32,128]{3,2,1,0:T(8,128)(2,1)S(1)} %get-tuple-element.16), channel_id=1, source_target_pairs={{0,1},{1,0},{2,3},{3,2},{4,5},{5,4},{6,7},{7,6},{8,9},{9,8},{10,11... | collective-permute-start | bytes 2359304 | tf_op jit(solution)/shard_map/ppermute | solution.py:298
  92.0 1.9 %collective-permute-done.7 = bf16[48,2,32,128]{3,2,1,0:T(8,128)(2,1)S(1)} collective-permute-done((bf16[48,2,32,128]{3,2,1,0:T(8,128)(2,1)S(1)}, bf16[48,2,32,128]{3,2,1,0:T(8,128)(2,1)S(1)}, u32[]{:S(2)}, u32[]{:S(2)}) %collective-permute-start.7) | collective-permute-done | bytes 786464 | tf_op jit(solution)/shard_map/ppermute | solution.py:298
  93.9 0.3 add_convert_fusion
  94.2 37.2 %all_to_all.10.got_ref = bf16[48,2,32,128]{3,2,1,0:T(8,128)(2,1)S(1)} all-to-all(bf16[48,2,32,128]{3,2,1,0:T(8,128)(2,1)S(1)} %add_convert_fusion), channel_id=1, replica_groups=mesh['y'=4,'z'=12,'x'=4,'h'=2,'c'=2] {'y','z'}, dimensions={0} | all-to-all | bytes 1572864 | tf_op jit(solution)/shard_map/all_to_all | solution.py:299
  131.4 0.7 shard_map.99
  132.2 9.5 %collective-permute-start.8 = (bf16[3,32,128]{2,1,0:T(8,128)(2,1)S(1)}, bf16[3,32,128]{2,1,0:T(8,128)(2,1)S(1)}, u32[]{:S(2)}, u32[]{:S(2)}) collective-permute-start(bf16[3,32,128]{2,1,0:T(8,128)(2,1)S(1)} %get-tuple-element.20), channel_id=1, source_target_pairs={{0,1},{1,2},{2,3},{3,4},{4,5},{5,6},{6,7},{7,8},{8,9},{9,10},{10,1... | collective-permute-start | bytes 73736 | tf_op jit(solution)/shard_map/ppermute | solution.py:25
  141.7 1.9 %collective-permute-start.9 = (bf16[3,32,128]{2,1,0:T(8,128)(2,1)S(1)}, bf16[3,32,128]{2,1,0:T(8,128)(2,1)S(1)}, u32[]{:S(2)}, u32[]{:S(2)}) collective-permute-start(bf16[3,32,128]{2,1,0:T(8,128)(2,1)S(1)} %get-tuple-element.21), channel_id=1, source_target_pairs={{1,0},{2,1},{3,2},{4,3},{5,4},{6,5},{7,6},{8,7},{9,8},{10,9},{11,1... | collective-permute-start | bytes 73736 | tf_op jit(solution)/shard_map/ppermute | solution.py:25
  143.6 0.0 collective-permute-done.8.low_ref
  143.6 8.2 %collective-permute-done.9.high_ref = bf16[3,32,128]{2,1,0:T(8,128)(2,1)S(1)} collective-permute-done((bf16[3,32,128]{2,1,0:T(8,128)(2,1)S(1)}, bf16[3,32,128]{2,1,0:T(8,128)(2,1)S(1)}, u32[]{:S(2)}, u32[]{:S(2)}) %collective-permute-start.9) | collective-permute-done | bytes 24608 | tf_op jit(solution)/shard_map/ppermute | solution.py:25
  151.8 1.3 shard_map.100
  (3 shorter events, 0.0 us)
Async XLA Ops:
  0.6 20.7 %copy-start = (f32[1536]{0:T(1024)S(1)}, f32[1536]{0:T(1024)}, u32[]{:S(2)}) copy-start(f32[1536]{0:T(1024)} %param.12) | copy-start | bytes 18436
  0.6 1.0 copy-start.1
  1.6 1.0 copy-start.2
  2.6 8.2 %copy-start.5 = (s32[8,128]{1,0:T(8,128)S(1)}, s32[8,128]{1,0:T(8,128)}, u32[]{:S(2)}) copy-start(s32[8,128]{1,0:T(8,128)} %tok_ref.1) | copy-start | bytes 12292
  2.6 18.8 %copy-start.6 = (bf16[7,7,32]{2,1,0:T(8,128)(2,1)S(1)}, bf16[7,7,32]{2,1,0:T(8,128)(2,1)}, u32[]{:S(2)}) copy-start(bf16[7,7,32]{2,1,0:T(8,128)(2,1)} %param.10) | copy-start | bytes 9412
  2.7 19.7 %copy-start.3 = (bf16[8,128,32]{1,2,0:T(8,128)(2,1)S(1)}, bf16[8,128,32]{1,2,0:T(8,128)(2,1)}, u32[]{:S(2)}) copy-start(bf16[8,128,32]{1,2,0:T(8,128)(2,1)} %param.15) | copy-start | bytes 196612
  2.7 19.7 %copy-start.4 = (bf16[256,32]{0,1:T(8,128)(2,1)S(1)}, bf16[256,32]{0,1:T(8,128)(2,1)}, u32[]{:S(2)}) copy-start(bf16[256,32]{0,1:T(8,128)(2,1)} %param.9) | copy-start | bytes 49156
  2.8 44.6 %collective-permute-start.2 = (bf16[2,128,1536]{2,1,0:T(8,128)(2,1)S(1)}, bf16[2,128,1536]{2,1,0:T(8,128)(2,1)S(1)}, u32[]{:S(2)}, u32[]{:S(2)}) collective-permute-start(bf16[2,128,1536]{2,1,0:T(8,128)(2,1)S(1)} %shard_map.96), channel_id=1, source_target_pairs={{0,0},{16,1},{2,2},{18,3},{4,4},{20,5},{6,6},{22,7},{8,8},{24,9},{... | collective-permute-start | bytes 2359304 | tf_op jit(solution)/shard_map/ppermute | solution.py:230
  7.4 45.3 %collective-permute-start.3 = (bf16[2,128,1536]{2,1,0:T(8,128)(2,1)S(1)}, bf16[2,128,1536]{2,1,0:T(8,128)(2,1)S(1)}, u32[]{:S(2)}, u32[]{:S(2)}) collective-permute-start(bf16[2,128,1536]{2,1,0:T(8,128)(2,1)S(1)} %shard_map.96), channel_id=1, source_target_pairs={{384,0},{402,1},{386,2},{400,3},{388,4},{406,5},{390,6},{404,7},{3... | collective-permute-start | bytes 2359304 | tf_op jit(solution)/shard_map/ppermute | solution.py:230
  10.9 11.4 %collective-permute-start.1 = (s32[3,128]{1,0:T(4,128)S(1)}, s32[3,128]{1,0:T(4,128)S(1)}, u32[]{:S(2)}, u32[]{:S(2)}) collective-permute-start(s32[3,128]{1,0:T(4,128)S(1)} %get-tuple-element.22), channel_id=1, source_target_pairs={{1,0},{2,1},{3,2},{4,3},{5,4},{6,5},{7,6},{8,7},{9,8},{10,9},{11,1... | collective-permute-start | bytes 4616 | tf_op jit(solution)/shard_map/ppermute | solution.py:25
  12.8 9.5 %collective-permute-start = (s32[3,128]{1,0:T(4,128)S(1)}, s32[3,128]{1,0:T(4,128)S(1)}, u32[]{:S(2)}, u32[]{:S(2)}) collective-permute-start(s32[3,128]{1,0:T(4,128)S(1)} %get-tuple-element.23), channel_id=1, source_target_pairs={{0,1},{1,2},{2,3},{3,4},{4,5},{5,6},{6,7},{7,8},{8,9},{9,10},{10,1... | collective-permute-start | bytes 4616 | tf_op jit(solution)/shard_map/ppermute | solution.py:25
  24.1 51.3 %all-to-all-start = ((bf16[48,2,32,128]{3,2,1,0:T(8,128)(2,1)}), bf16[48,2,32,128]{3,2,1,0:T(8,128)(2,1)S(1)}, u32[]{:S(2)}, u32[]{:S(2)}) async-start(bf16[48,2,32,128]{3,2,1,0:T(8,128)(2,1)} %get-tuple-element.12), calls=%async_computation | async-start | bytes 1572864 | tf_op jit(solution)/shard_map/all_to_all | solution.py:274
  47.4 38.2 %copy-start.7 = (f32[1536]{0:T(1024)S(1)}, f32[1536]{0:T(1024)}, u32[]{:S(2)}) copy-start(f32[1536]{0:T(1024)} %param.11) | copy-start | bytes 18436
  47.4 36.3 %collective-permute-start.6 = (bf16[2,128,1536]{2,1,0:T(8,128)(2,1)S(1)}, bf16[2,128,1536]{2,1,0:T(8,128)(2,1)}, u32[]{:S(2)}, u32[]{:S(2)}) collective-permute-start(bf16[2,128,1536]{2,1,0:T(8,128)(2,1)S(1)} %collective-permute-done.2.near_ref.w2_ref), channel_id=1, source_target_pairs={{578,0},{579,1},{0,192},{1,193},{192,384},{193,385},{384,576},{385... | collective-permute-start | bytes 2359304 | tf_op jit(solution)/shard_map/ppermute | solution.py:244
  49.3 34.4 %collective-permute-start.5 = (bf16[2,128,1536]{2,1,0:T(8,128)(2,1)S(1)}, bf16[2,128,1536]{2,1,0:T(8,128)(2,1)}, u32[]{:S(2)}, u32[]{:S(2)}) collective-permute-start(bf16[2,128,1536]{2,1,0:T(8,128)(2,1)S(1)} %collective-permute-done.2.near_ref.w2_ref), channel_id=1, source_target_pairs={{192,0},{193,1},{384,192},{385,193},{576,384},{577,385},{2,576},{3... | collective-permute-start | bytes 2359304 | tf_op jit(solution)/shard_map/ppermute | solution.py:244
  75.4 10.2 %collective-permute-start.4 = (bf16[48,2,32,128]{3,2,1,0:T(8,128)(2,1)S(1)}, bf16[48,2,32,128]{3,2,1,0:T(8,128)(2,1)S(1)}, u32[]{:S(2)}, u32[]{:S(2)}) collective-permute-start(bf16[48,2,32,128]{3,2,1,0:T(8,128)(2,1)S(1)} %all-to-all-done.own_ref), channel_id=1, source_target_pairs={{0,1},{1,0},{2,3},{3,2},{4,5},{5,4},{6,7},{7,6},{8,9},{9,8},{10,11... | collective-permute-start | bytes 2359304 | tf_op jit(solution)/shard_map/ppermute | solution.py:278
  89.8 4.2 %collective-permute-start.7 = (bf16[48,2,32,128]{3,2,1,0:T(8,128)(2,1)S(1)}, bf16[48,2,32,128]{3,2,1,0:T(8,128)(2,1)S(1)}, u32[]{:S(2)}, u32[]{:S(2)}) collective-permute-start(bf16[48,2,32,128]{3,2,1,0:T(8,128)(2,1)S(1)} %get-tuple-element.16), channel_id=1, source_target_pairs={{0,1},{1,0},{2,3},{3,2},{4,5},{5,4},{6,7},{7,6},{8,9},{9,8},{10,11... | collective-permute-start | bytes 2359304 | tf_op jit(solution)/shard_map/ppermute | solution.py:298
  132.2 11.4 %collective-permute-start.8 = (bf16[3,32,128]{2,1,0:T(8,128)(2,1)S(1)}, bf16[3,32,128]{2,1,0:T(8,128)(2,1)S(1)}, u32[]{:S(2)}, u32[]{:S(2)}) collective-permute-start(bf16[3,32,128]{2,1,0:T(8,128)(2,1)S(1)} %get-tuple-element.20), channel_id=1, source_target_pairs={{0,1},{1,2},{2,3},{3,4},{4,5},{5,6},{6,7},{7,8},{8,9},{9,10},{10,1... | collective-permute-start | bytes 73736 | tf_op jit(solution)/shard_map/ppermute | solution.py:25
  141.7 10.1 %collective-permute-start.9 = (bf16[3,32,128]{2,1,0:T(8,128)(2,1)S(1)}, bf16[3,32,128]{2,1,0:T(8,128)(2,1)S(1)}, u32[]{:S(2)}, u32[]{:S(2)}) collective-permute-start(bf16[3,32,128]{2,1,0:T(8,128)(2,1)S(1)} %get-tuple-element.21), channel_id=1, source_target_pairs={{1,0},{2,1},{3,2},{4,3},{5,4},{6,5},{7,6},{8,7},{9,8},{10,9},{11,1... | collective-permute-start | bytes 73736 | tf_op jit(solution)/shard_map/ppermute | solution.py:25

commit v11 on v10

--- a/solution.py
+++ b/solution.py
@@ -79,9 +79,14 @@
     conv_rows(framed, taps_ref, False, emit)
 
 
-def stack_kernel(in_ref, out_ref, both_ref):
-    both_ref[0] = in_ref[...].T
-    both_ref[1] = out_ref[...]
+def stack_kernel(in_ref, out_ref, both_ref, shard, sem):
+    first = pltpu.make_async_copy(in_ref, shard, sem.at[0])
+    second = pltpu.make_async_copy(out_ref, both_ref.at[1], sem.at[1])
+    first.start()
+    second.start()
+    first.wait()
+    both_ref[0] = shard[...].T
+    second.wait()
 
 
 def anchor_kernel(near_ref, far_ref, out_ref):
@@ -255,7 +260,14 @@
     hid = w_out.shape[0] * lax.axis_size("y")
     swap = [(0, 1), (1, 0)]
 
-    (both,) = call(stack_kernel, [((2, *w_out.shape), BF16)], (w_in, w_out))
+    (both,) = call(
+        stack_kernel,
+        [((2, *w_out.shape), BF16)],
+        (w_in, w_out),
+        [ANY] * 2,
+        [pltpu.VMEM(w_in.shape, BF16), pltpu.SemaphoreType.DMA((2,))],
+        limit=60 << 20,
+    )
     near, far = moved(both, 0), moved(both, 2)
     low, high = edges(floor_tokens[:3] + 1, floor_tokens[rows - 3 :] + 1)
     taps = depth_kernel.reshape(49, chans).T

time: 154 us -> 156 us (1.013)
  Pallas kernels: 7.79 us -> 10.1 us
  local copies, waits for them, and re-layouts: 2.55 us -> 0.56 us
    pallas_call x6, Pallas kernels: 7.79 us -> 10.1 us  [call(): pl.pallas_call(body, out_shape=outs, in_specs=specs or [VMEM] * len(args)...]
    unnamed x16 -> x12, local copies, waits for them, and re-layouts: 2.02 us -> 0.03 us
where the time goes in v11:
time: 156 us; the launch traced here: 154 us
  starting transfers between devices  68.5 us (44%)
  blocking collectives  37.1 us (24%)
  waiting for transfers between devices  36.6 us (23%)
  Pallas kernels  10.1 us (6%)
    all_to_all x1, blocking collectives, on_device(): got = lax.all_to_all(part, CHAN, 0, 0, tiled=True)  37.1 us
    all_to_all x1, starting transfers between devices, on_device(): own = lax.all_to_all(send, CHAN, 0, 0, tiled=True)  23.4 us
    all_to_all x1, waiting for transfers between devices, on_device(): own = lax.all_to_all(send, CHAN, 0, 0, tiled=True)  22.8 us
    ppermute x2, starting transfers between devices, edges(): lax.ppermute(high_side, SPACE, forward)  17.4 us
    pallas_call x6, Pallas kernels, call(): pl.pallas_call(body, out_shape=outs, in_specs=specs or [VMEM] * len(args)...  10.1 us
    ppermute x2, waiting for transfers between devices, edges(): lax.ppermute(low_side, SPACE, backward)  10 us
    ppermute x1, starting transfers between devices, on_device(): oth = lax.ppermute(own, 'c', swap)  8.24 us
    ppermute x2, starting transfers between devices, moved(): return lax.ppermute(shard, AXES, pairs)  8.05 us
  transfers between devices with their start and end apart: 11, of which 5 were waited for; matrix products, arithmetic and copies ran while one was open for 0% of the time, Pallas kernels for 1%

profile of v11, /device:TPU:57, one launch (start us, length us, event | category | flops | bytes accessed | tf_op | source)
XLA Modules:
  0.0 154.0 jit_solution(2667234382086553854)
XLA Ops:
  0.6 0.0 copy-start
  0.6 0.0 copy-start.3
  0.7 0.0 copy-start.4
  0.7 0.0 copy-start.1
  0.7 0.0 copy-start.2
  0.7 2.1 %shard_map.96 = bf16[2,128,1536]{2,1,0:T(8,128)(2,1)} custom-call(bf16[1536,128]{1,0:T(8,128)(2,1)} %in_ref.1, bf16[128,1536]{1,0:T(8,128)(2,1)} %out_ref.1), custom_call_target="tpu_custom_call" | custom-call | flops 1048576 | bytes 4194304 | tf_op jit(solution)/shard_map/pallas_call | solution.py:213
  2.8 4.6 %collective-permute-start.2 = (bf16[2,128,1536]{2,1,0:T(8,128)(2,1)}, bf16[2,128,1536]{2,1,0:T(8,128)(2,1)S(1)}, u32[]{:S(2)}, u32[]{:S(2)}) collective-permute-start(bf16[2,128,1536]{2,1,0:T(8,128)(2,1)} %shard_map.96), channel_id=1, source_target_pairs={{0,0},{16,1},{2,2},{18,3},{4,4},{20,5},{6,6},{22,7},{8,8},{24,9},{... | collective-permute-start | bytes 2359304 | tf_op jit(solution)/shard_map/ppermute | solution.py:235
  7.4 3.5 %collective-permute-start.3 = (bf16[2,128,1536]{2,1,0:T(8,128)(2,1)}, bf16[2,128,1536]{2,1,0:T(8,128)(2,1)S(1)}, u32[]{:S(2)}, u32[]{:S(2)}) collective-permute-start(bf16[2,128,1536]{2,1,0:T(8,128)(2,1)} %shard_map.96), channel_id=1, source_target_pairs={{384,0},{402,1},{386,2},{400,3},{388,4},{406,5},{390,6},{404,7},{3... | collective-permute-start | bytes 2359304 | tf_op jit(solution)/shard_map/ppermute | solution.py:235
  10.9 0.0 copy-done.3
  10.9 1.9 %collective-permute-start.1 = (s32[3,128]{1,0:T(4,128)S(1)}, s32[3,128]{1,0:T(4,128)S(1)}, u32[]{:S(2)}, u32[]{:S(2)}) collective-permute-start(s32[3,128]{1,0:T(4,128)S(1)} %get-tuple-element.22), channel_id=1, source_target_pairs={{1,0},{2,1},{3,2},{4,3},{5,4},{6,5},{7,6},{8,7},{9,8},{10,9},{11,1... | collective-permute-start | bytes 4616 | tf_op jit(solution)/shard_map/ppermute | solution.py:25
  12.8 8.4 %collective-permute-start = (s32[3,128]{1,0:T(4,128)S(1)}, s32[3,128]{1,0:T(4,128)S(1)}, u32[]{:S(2)}, u32[]{:S(2)}) collective-permute-start(s32[3,128]{1,0:T(4,128)S(1)} %get-tuple-element.23), channel_id=1, source_target_pairs={{0,1},{1,2},{2,3},{3,4},{4,5},{5,6},{6,7},{7,8},{8,9},{9,10},{10,1... | collective-permute-start | bytes 4616 | tf_op jit(solution)/shard_map/ppermute | solution.py:25
  21.3 0.0 copy-done
  21.3 0.1 dynamic-slice_bitcast_fusion
  21.4 0.0 copy-done.4
  21.4 0.1 copy.13
  21.5 0.1 copy.14.scale_ref
  21.6 2.0 %collective-permute-done.1.high_ref = s32[3,128]{1,0:T(4,128)S(1)} collective-permute-done((s32[3,128]{1,0:T(4,128)S(1)}, s32[3,128]{1,0:T(4,128)S(1)}, u32[]{:S(2)}, u32[]{:S(2)}) %collective-permute-start.1) | collective-permute-done | bytes 1568 | tf_op jit(solution)/shard_map/ppermute | solution.py:25
  23.6 0.0 collective-permute-done.low_ref
  23.6 0.0 copy-done.1
  23.6 0.0 copy-done.2
  23.6 1.7 %shard_map.95 = (bf16[8,32,128]{2,1,0:T(8,128)(2,1)S(1)}, bf16[48,2,32,128]{3,2,1,0:T(8,128)(2,1)}) custom-call(s32[8,128]{1,0:T(8,128)S(1)} %copy-done.3, s32[3,128]{1,0:T(4,128)S(1)} %collective-permute-done.low_ref, s32[3,128]{1,0:T(4,128)S(1)} %collective-permute-done.1.high_ref, bf16[32,256]{1,0:T(8,128)(2,1)S(1)} %bitcast.11, ...), custom_call_target="tpu_custom_call" | custom-call | flops 1048576 | bytes 4194304 | tf_op jit(solution)/shard_map/pallas_call | solution.py:213
  25.3 23.4 %all-to-all-start = ((bf16[48,2,32,128]{3,2,1,0:T(8,128)(2,1)}), bf16[48,2,32,128]{3,2,1,0:T(8,128)(2,1)S(1)}, u32[]{:S(2)}, u32[]{:S(2)}) async-start(bf16[48,2,32,128]{3,2,1,0:T(8,128)(2,1)} %get-tuple-element.12), calls=%async_computation | async-start | bytes 1572864 | tf_op jit(solution)/shard_map/all_to_all | solution.py:286
  48.7 0.0 copy-start.5
  48.7 0.0 collective-permute-done.2.near_ref.w2_ref
  48.8 1.9 %collective-permute-start.6 = (bf16[2,128,1536]{2,1,0:T(8,128)(2,1)S(1)}, bf16[2,128,1536]{2,1,0:T(8,128)(2,1)S(1)}, u32[]{:S(2)}, u32[]{:S(2)}) collective-permute-start(bf16[2,128,1536]{2,1,0:T(8,128)(2,1)S(1)} %collective-permute-done.2.near_ref.w2_ref), channel_id=1, source_target_pairs={{578,0},{579,1},{0,192},{1,193},{192,384},{193,385},{384,576},{385... | collective-permute-start | bytes 2359304 | tf_op jit(solution)/shard_map/ppermute | solution.py:249
  50.7 3.4 %collective-permute-start.5 = (bf16[2,128,1536]{2,1,0:T(8,128)(2,1)S(1)}, bf16[2,128,1536]{2,1,0:T(8,128)(2,1)}, u32[]{:S(2)}, u32[]{:S(2)}) collective-permute-start(bf16[2,128,1536]{2,1,0:T(8,128)(2,1)S(1)} %collective-permute-done.2.near_ref.w2_ref), channel_id=1, source_target_pairs={{192,0},{193,1},{384,192},{385,193},{576,384},{577,385},{2,576},{3... | collective-permute-start | bytes 2359304 | tf_op jit(solution)/shard_map/ppermute | solution.py:249
  54.1 0.0 collective-permute-done.3.far_ref.w3_ref
  54.1 22.8 %all-to-all-done.own_ref = bf16[48,2,32,128]{3,2,1,0:T(8,128)(2,1)S(1)} async-done(((bf16[48,2,32,128]{3,2,1,0:T(8,128)(2,1)}), bf16[48,2,32,128]{3,2,1,0:T(8,128)(2,1)S(1)}, u32[]{:S(2)}, u32[]{:S(2)}) %all-to-all-start) | async-done | bytes 786464 | tf_op jit(solution)/shard_map/all_to_all | solution.py:286
  76.8 8.2 %collective-permute-start.4 = (bf16[48,2,32,128]{3,2,1,0:T(8,128)(2,1)S(1)}, bf16[48,2,32,128]{3,2,1,0:T(8,128)(2,1)S(1)}, u32[]{:S(2)}, u32[]{:S(2)}) collective-permute-start(bf16[48,2,32,128]{3,2,1,0:T(8,128)(2,1)S(1)} %all-to-all-done.own_ref), channel_id=1, source_target_pairs={{0,1},{1,0},{2,3},{3,2},{4,5},{5,4},{6,7},{7,6},{8,9},{9,8},{10,11... | collective-permute-start | bytes 2359304 | tf_op jit(solution)/shard_map/ppermute | solution.py:290
  85.1 0.0 collective-permute-done.6.w1_ref
  85.1 0.0 collective-permute-done.5.w0_ref
  85.1 1.9 %collective-permute-done.4.oth_ref = bf16[48,2,32,128]{3,2,1,0:T(8,128)(2,1)S(1)} collective-permute-done((bf16[48,2,32,128]{3,2,1,0:T(8,128)(2,1)S(1)}, bf16[48,2,32,128]{3,2,1,0:T(8,128)(2,1)S(1)}, u32[]{:S(2)}, u32[]{:S(2)}) %collective-permute-start.4) | collective-permute-done | bytes 786464 | tf_op jit(solution)/shard_map/ppermute | solution.py:290
  87.0 0.0 copy-done.5
  87.0 0.3 broadcast_in_dim.10.gain_ref
  87.2 4.2 %shard_map.98 = (f32[48,2,32,128]{3,2,1,0:T(8,128)S(1)}, bf16[48,2,32,128]{3,2,1,0:T(8,128)(2,1)S(1)}) custom-call(bf16[48,2,32,128]{3,2,1,0:T(8,128)(2,1)S(1)} %all-to-all-done.own_ref, bf16[48,2,32,128]{3,2,1,0:T(8,128)(2,1)S(1)} %collective-permute-done.4.oth_ref, f32[1536,128]{1,0:T(8,128)S(1)} %broadcast_in_dim.10.gain_ref, ...), custom_call_target="tpu_custom_call" | custom-call | flops 1610612736 | bytes 4194304 | tf_op jit(solution)/shard_map/pallas_call | solution.py:213
  91.5 2.3 %collective-permute-start.7 = (bf16[48,2,32,128]{3,2,1,0:T(8,128)(2,1)S(1)}, bf16[48,2,32,128]{3,2,1,0:T(8,128)(2,1)S(1)}, u32[]{:S(2)}, u32[]{:S(2)}) collective-permute-start(bf16[48,2,32,128]{3,2,1,0:T(8,128)(2,1)S(1)} %get-tuple-element.16), channel_id=1, source_target_pairs={{0,1},{1,0},{2,3},{3,2},{4,5},{5,4},{6,7},{7,6},{8,9},{9,8},{10,11... | collective-permute-start | bytes 2359304 | tf_op jit(solution)/shard_map/ppermute | solution.py:310
  93.8 1.9 %collective-permute-done.7 = bf16[48,2,32,128]{3,2,1,0:T(8,128)(2,1)S(1)} collective-permute-done((bf16[48,2,32,128]{3,2,1,0:T(8,128)(2,1)S(1)}, bf16[48,2,32,128]{3,2,1,0:T(8,128)(2,1)S(1)}, u32[]{:S(2)}, u32[]{:S(2)}) %collective-permute-start.7) | collective-permute-done | bytes 786464 | tf_op jit(solution)/shard_map/ppermute | solution.py:310
  95.7 0.3 add_convert_fusion
  95.9 37.1 %all_to_all.10.got_ref = bf16[48,2,32,128]{3,2,1,0:T(8,128)(2,1)S(1)} all-to-all(bf16[48,2,32,128]{3,2,1,0:T(8,128)(2,1)S(1)} %add_convert_fusion), channel_id=1, replica_groups=mesh['y'=4,'z'=12,'x'=4,'h'=2,'c'=2] {'y','z'}, dimensions={0} | all-to-all | bytes 1572864 | tf_op jit(solution)/shard_map/all_to_all | solution.py:311
  133.0 0.7 shard_map.99
  133.8 9.0 %collective-permute-start.8 = (bf16[3,32,128]{2,1,0:T(8,128)(2,1)S(1)}, bf16[3,32,128]{2,1,0:T(8,128)(2,1)S(1)}, u32[]{:S(2)}, u32[]{:S(2)}) collective-permute-start(bf16[3,32,128]{2,1,0:T(8,128)(2,1)S(1)} %get-tuple-element.20), channel_id=1, source_target_pairs={{0,1},{1,2},{2,3},{3,4},{4,5},{5,6},{6,7},{7,8},{8,9},{9,10},{10,1... | collective-permute-start | bytes 73736 | tf_op jit(solution)/shard_map/ppermute | solution.py:25
  142.8 1.9 %collective-permute-start.9 = (bf16[3,32,128]{2,1,0:T(8,128)(2,1)S(1)}, bf16[3,32,128]{2,1,0:T(8,128)(2,1)S(1)}, u32[]{:S(2)}, u32[]{:S(2)}) collective-permute-start(bf16[3,32,128]{2,1,0:T(8,128)(2,1)S(1)} %get-tuple-element.21), channel_id=1, source_target_pairs={{1,0},{2,1},{3,2},{4,3},{5,4},{6,5},{7,6},{8,7},{9,8},{10,9},{11,1... | collective-permute-start | bytes 73736 | tf_op jit(solution)/shard_map/ppermute | solution.py:25
  144.7 0.0 collective-permute-done.8.low_ref
  144.7 8.0 %collective-permute-done.9.high_ref = bf16[3,32,128]{2,1,0:T(8,128)(2,1)S(1)} collective-permute-done((bf16[3,32,128]{2,1,0:T(8,128)(2,1)S(1)}, bf16[3,32,128]{2,1,0:T(8,128)(2,1)S(1)}, u32[]{:S(2)}, u32[]{:S(2)}) %collective-permute-start.9) | collective-permute-done | bytes 24608 | tf_op jit(solution)/shard_map/ppermute | solution.py:25
  152.7 1.3 shard_map.100
  (3 shorter events, 0.0 us)
Async XLA Ops:
  0.6 20.7 %copy-start = (f32[1536]{0:T(1024)S(1)}, f32[1536]{0:T(1024)}, u32[]{:S(2)}) copy-start(f32[1536]{0:T(1024)} %param.12) | copy-start | bytes 18436
  0.6 10.2 %copy-start.3 = (s32[8,128]{1,0:T(8,128)S(1)}, s32[8,128]{1,0:T(8,128)}, u32[]{:S(2)}) copy-start(s32[8,128]{1,0:T(8,128)} %tok_ref.1) | copy-start | bytes 12292
  0.7 20.7 %copy-start.4 = (bf16[7,7,32]{2,1,0:T(8,128)(2,1)S(1)}, bf16[7,7,32]{2,1,0:T(8,128)(2,1)}, u32[]{:S(2)}) copy-start(bf16[7,7,32]{2,1,0:T(8,128)(2,1)} %param.10) | copy-start | bytes 9412
  0.7 23.0 %copy-start.1 = (bf16[8,128,32]{1,2,0:T(8,128)(2,1)S(1)}, bf16[8,128,32]{1,2,0:T(8,128)(2,1)}, u32[]{:S(2)}) copy-start(bf16[8,128,32]{1,2,0:T(8,128)(2,1)} %param.15) | copy-start | bytes 196612
  0.7 22.9 %copy-start.2 = (bf16[256,32]{0,1:T(8,128)(2,1)S(1)}, bf16[256,32]{0,1:T(8,128)(2,1)}, u32[]{:S(2)}) copy-start(bf16[256,32]{0,1:T(8,128)(2,1)} %param.9) | copy-start | bytes 49156
  2.8 45.9 %collective-permute-start.2 = (bf16[2,128,1536]{2,1,0:T(8,128)(2,1)}, bf16[2,128,1536]{2,1,0:T(8,128)(2,1)S(1)}, u32[]{:S(2)}, u32[]{:S(2)}) collective-permute-start(bf16[2,128,1536]{2,1,0:T(8,128)(2,1)} %shard_map.96), channel_id=1, source_target_pairs={{0,0},{16,1},{2,2},{18,3},{4,4},{20,5},{6,6},{22,7},{8,8},{24,9},{... | collective-permute-start | bytes 2359304 | tf_op jit(solution)/shard_map/ppermute | solution.py:235
  7.4 46.7 %collective-permute-start.3 = (bf16[2,128,1536]{2,1,0:T(8,128)(2,1)}, bf16[2,128,1536]{2,1,0:T(8,128)(2,1)S(1)}, u32[]{:S(2)}, u32[]{:S(2)}) collective-permute-start(bf16[2,128,1536]{2,1,0:T(8,128)(2,1)} %shard_map.96), channel_id=1, source_target_pairs={{384,0},{402,1},{386,2},{400,3},{388,4},{406,5},{390,6},{404,7},{3... | collective-permute-start | bytes 2359304 | tf_op jit(solution)/shard_map/ppermute | solution.py:235
  10.9 12.7 %collective-permute-start.1 = (s32[3,128]{1,0:T(4,128)S(1)}, s32[3,128]{1,0:T(4,128)S(1)}, u32[]{:S(2)}, u32[]{:S(2)}) collective-permute-start(s32[3,128]{1,0:T(4,128)S(1)} %get-tuple-element.22), channel_id=1, source_target_pairs={{1,0},{2,1},{3,2},{4,3},{5,4},{6,5},{7,6},{8,7},{9,8},{10,9},{11,1... | collective-permute-start | bytes 4616 | tf_op jit(solution)/shard_map/ppermute | solution.py:25
  12.8 10.8 %collective-permute-start = (s32[3,128]{1,0:T(4,128)S(1)}, s32[3,128]{1,0:T(4,128)S(1)}, u32[]{:S(2)}, u32[]{:S(2)}) collective-permute-start(s32[3,128]{1,0:T(4,128)S(1)} %get-tuple-element.23), channel_id=1, source_target_pairs={{0,1},{1,2},{2,3},{3,4},{4,5},{5,6},{6,7},{7,8},{8,9},{9,10},{10,1... | collective-permute-start | bytes 4616 | tf_op jit(solution)/shard_map/ppermute | solution.py:25
  25.3 51.5 %all-to-all-start = ((bf16[48,2,32,128]{3,2,1,0:T(8,128)(2,1)}), bf16[48,2,32,128]{3,2,1,0:T(8,128)(2,1)S(1)}, u32[]{:S(2)}, u32[]{:S(2)}) async-start(bf16[48,2,32,128]{3,2,1,0:T(8,128)(2,1)} %get-tuple-element.12), calls=%async_computation | async-start | bytes 1572864 | tf_op jit(solution)/shard_map/all_to_all | solution.py:286
  48.7 38.2 %copy-start.5 = (f32[1536]{0:T(1024)S(1)}, f32[1536]{0:T(1024)}, u32[]{:S(2)}) copy-start(f32[1536]{0:T(1024)} %param.11) | copy-start | bytes 18436
  48.8 36.3 %collective-permute-start.6 = (bf16[2,128,1536]{2,1,0:T(8,128)(2,1)S(1)}, bf16[2,128,1536]{2,1,0:T(8,128)(2,1)S(1)}, u32[]{:S(2)}, u32[]{:S(2)}) collective-permute-start(bf16[2,128,1536]{2,1,0:T(8,128)(2,1)S(1)} %collective-permute-done.2.near_ref.w2_ref), channel_id=1, source_target_pairs={{578,0},{579,1},{0,192},{1,193},{192,384},{193,385},{384,576},{385... | collective-permute-start | bytes 2359304 | tf_op jit(solution)/shard_map/ppermute | solution.py:249
  50.7 34.4 %collective-permute-start.5 = (bf16[2,128,1536]{2,1,0:T(8,128)(2,1)S(1)}, bf16[2,128,1536]{2,1,0:T(8,128)(2,1)}, u32[]{:S(2)}, u32[]{:S(2)}) collective-permute-start(bf16[2,128,1536]{2,1,0:T(8,128)(2,1)S(1)} %collective-permute-done.2.near_ref.w2_ref), channel_id=1, source_target_pairs={{192,0},{193,1},{384,192},{385,193},{576,384},{577,385},{2,576},{3... | collective-permute-start | bytes 2359304 | tf_op jit(solution)/shard_map/ppermute | solution.py:249
  76.8 10.1 %collective-permute-start.4 = (bf16[48,2,32,128]{3,2,1,0:T(8,128)(2,1)S(1)}, bf16[48,2,32,128]{3,2,1,0:T(8,128)(2,1)S(1)}, u32[]{:S(2)}, u32[]{:S(2)}) collective-permute-start(bf16[48,2,32,128]{3,2,1,0:T(8,128)(2,1)S(1)} %all-to-all-done.own_ref), channel_id=1, source_target_pairs={{0,1},{1,0},{2,3},{3,2},{4,5},{5,4},{6,7},{7,6},{8,9},{9,8},{10,11... | collective-permute-start | bytes 2359304 | tf_op jit(solution)/shard_map/ppermute | solution.py:290
  91.5 4.2 %collective-permute-start.7 = (bf16[48,2,32,128]{3,2,1,0:T(8,128)(2,1)S(1)}, bf16[48,2,32,128]{3,2,1,0:T(8,128)(2,1)S(1)}, u32[]{:S(2)}, u32[]{:S(2)}) collective-permute-start(bf16[48,2,32,128]{3,2,1,0:T(8,128)(2,1)S(1)} %get-tuple-element.16), channel_id=1, source_target_pairs={{0,1},{1,0},{2,3},{3,2},{4,5},{5,4},{6,7},{7,6},{8,9},{9,8},{10,11... | collective-permute-start | bytes 2359304 | tf_op jit(solution)/shard_map/ppermute | solution.py:310
  133.8 10.9 %collective-permute-start.8 = (bf16[3,32,128]{2,1,0:T(8,128)(2,1)S(1)}, bf16[3,32,128]{2,1,0:T(8,128)(2,1)S(1)}, u32[]{:S(2)}, u32[]{:S(2)}) collective-permute-start(bf16[3,32,128]{2,1,0:T(8,128)(2,1)S(1)} %get-tuple-element.20), channel_id=1, source_target_pairs={{0,1},{1,2},{2,3},{3,4},{4,5},{5,6},{6,7},{7,8},{8,9},{9,10},{10,1... | collective-permute-start | bytes 73736 | tf_op jit(solution)/shard_map/ppermute | solution.py:25
  142.8 10.0 %collective-permute-start.9 = (bf16[3,32,128]{2,1,0:T(8,128)(2,1)S(1)}, bf16[3,32,128]{2,1,0:T(8,128)(2,1)S(1)}, u32[]{:S(2)}, u32[]{:S(2)}) collective-permute-start(bf16[3,32,128]{2,1,0:T(8,128)(2,1)S(1)} %get-tuple-element.21), channel_id=1, source_target_pairs={{1,0},{2,1},{3,2},{4,3},{5,4},{6,5},{7,6},{8,7},{9,8},{10,9},{11,1... | collective-permute-start | bytes 73736 | tf_op jit(solution)/shard_map/ppermute | solution.py:25
